TPU v7x, 32 devices: a whole 2x2x4 slice. The times are simulated.
32 devices in a mesh: dp: 8 (over z, y), tensor: 4 (over x, core).
Axes of the slice: x: 2, y: 2, z: 4, core: 2. Of those that a mesh axis runs over, the one named last changes fastest.
Arguments:
- block_in: bfloat16 [16384, 768], P(('dp', 'tensor')), may hold values from -6 to 6
- enc_states: bfloat16 [65536, 768], P(('dp', 'tensor')), may hold values from -6 to 6
- dec_len: int32 [64], P('dp'), may hold values from 32 to 256
- enc_len: int32 [64], P('dp'), may hold values from 128 to 1024
- gain_self: bfloat16 [768], replicated, may hold values from 0.5 to 1.5
- self_query: bfloat16 [768, 768], P(None, 'tensor'), may hold values from -0.02734375 to 0.02734375
- self_key: bfloat16 [768, 768], P(None, 'tensor'), may hold values from -0.21875 to 0.21875
- self_value: bfloat16 [768, 768], P(None, 'tensor'), may hold values from -0.21875 to 0.21875
- self_out: bfloat16 [768, 768], P('tensor'), may hold values from -0.875 to 0.875
- rel_table: bfloat16 [32, 12], P(None, 'tensor'), may hold values from -4 to 4
- gain_cross: bfloat16 [768], replicated, may hold values from 0.5 to 1.5
- cross_query: bfloat16 [768, 768], P(None, 'tensor'), may hold values from -0.02734375 to 0.02734375
- cross_key: bfloat16 [768, 768], P(None, 'tensor'), may hold values from -0.21875 to 0.21875
- cross_value: bfloat16 [768, 768], P(None, 'tensor'), may hold values from -0.21875 to 0.21875
- cross_out: bfloat16 [768, 768], P('tensor'), may hold values from -0.875 to 0.875
- gain_ff: bfloat16 [768], replicated, may hold values from 0.5 to 1.5
- ff_in: bfloat16 [768, 3072], P(None, 'tensor'), may hold values from -0.21875 to 0.21875
- ff_out: bfloat16 [3072, 768], P('tensor'), may hold values from -0.109375 to 0.109375
- out_grad: bfloat16 [16384, 768], P(('dp', 'tensor')), may hold values from -6 to 6
Outputs:
- block_out: bfloat16 [16384, 768], P(('dp', 'tensor'))
- grad_in: float32 [16384, 768], P(('dp', 'tensor'))
- grad_enc: float32 [65536, 768], P(('dp', 'tensor'))
- grad_gain_self: float32 [768], replicated
- grad_self_query: float32 [768, 768], P(None, 'tensor')
- grad_self_key: float32 [768, 768], P(None, 'tensor')
- grad_self_value: float32 [768, 768], P(None, 'tensor')
- grad_self_out: float32 [768, 768], P('tensor')
- grad_rel_table: float32 [32, 12], P(None, 'tensor')
- grad_gain_cross: float32 [768], replicated
- grad_cross_query: float32 [768, 768], P(None, 'tensor')
- grad_cross_key: float32 [768, 768], P(None, 'tensor')
- grad_cross_value: float32 [768, 768], P(None, 'tensor')
- grad_cross_out: float32 [768, 768], P('tensor')
- grad_gain_ff: float32 [768], replicated
- grad_ff_in: float32 [768, 3072], P(None, 'tensor')
- grad_ff_out: float32 [3072, 768], P('tensor')
All inputs are finite; a program needn't handle non-finite values.
Results may differ from a plain program's by a relative error of at most 0.025.
Values may be sent and summed in bfloat16 or wider, within the bound.
No kernel may reach another device: no remote copies, remote signals or barrier semaphores. Data moves between devices by JAX's collectives and lax.ppermute only.
A program may use at most 256 MiB of HBM per device.

v0:
```python
import math

import jax
import jax.numpy as jnp
import numpy as np
from jax import lax
from jax.sharding import PartitionSpec as P

BUCKETS = 32
MAX_DIST = 128
LEN = 256
ENC = 1024


norm_eps = 1e-06
masked_score = -1000000000.0


def bucket_limits():
    half_count = BUCKETS // 2
    growth_ratio = MAX_DIST / half_count
    return np.array(
        [
            int(math.ceil(half_count * growth_ratio ** (level_index / half_count)))
            for level_index in range(1, half_count)
        ],
        dtype=np.int32,
    )


def bucket_onehot(length):
    places = jnp.arange(length, dtype=jnp.int32)
    distance = jnp.maximum(places[:, None] - places[None, :], 0)
    limits = jnp.asarray(bucket_limits())
    above_count = jnp.sum((distance[:, :, None] >= limits[None, None, :]).astype(jnp.int32), axis=2)
    half_count = BUCKETS // 2
    buckets = jnp.where(distance < half_count, distance, half_count + above_count)
    return (buckets[:, :, None] == jnp.arange(BUCKETS, dtype=jnp.int32)[None, None, :]).astype(
        jnp.float32
    )


def collect_rows(values):
    return lax.all_gather(values, "tensor", axis=0, tiled=True)


def spread_rows(values):
    return lax.psum_scatter(values, "tensor", scatter_dimension=0, tiled=True)


def rms_norm(values, scales):
    return values * lax.rsqrt(jnp.mean(values * values, axis=-1, keepdims=True) + norm_eps) * scales


def norm_back(values, scales, incoming):
    primal, pullback = jax.vjp(rms_norm, values, scales)
    return pullback(incoming)


def smooth_act(values):
    return jax.nn.gelu(values, approximate=True)


def act_back(values, incoming):
    primal, pullback = jax.vjp(smooth_act, values)
    return pullback(incoming)[0]


def matmul(former, latter):
    return jnp.dot(former, latter, preferred_element_type=jnp.float32)


def inner_rows(former, latter):
    return lax.dot_general(
        former, latter, (((0,), (0,)), ((), ())), preferred_element_type=jnp.float32
    )


def times_transposed(former, latter):
    return lax.dot_general(
        former, latter, (((1,), (1,)), ((), ())), preferred_element_type=jnp.float32
    )


def attend_forward(query_rows, key_rows, value_rows, extra_bias, allowed):
    scores = (
        jnp.einsum("sqhd,skhd->shqk", query_rows, key_rows, preferred_element_type=jnp.float32)
        + extra_bias
    )
    scores = jnp.where(allowed, scores, masked_score)
    top_score = jnp.max(scores, axis=-1, keepdims=True)
    weights = jnp.exp(scores - top_score)
    totals = jnp.sum(weights, axis=-1, keepdims=True)
    softmax_out = (weights / totals).astype(jnp.bfloat16)
    mixed_out = jnp.einsum(
        "shqk,skhd->sqhd", softmax_out, value_rows, preferred_element_type=jnp.float32
    ).astype(jnp.bfloat16)
    return (mixed_out, top_score + jnp.log(totals))


def attend_backward(query_rows, key_rows, value_rows, extra_bias, allowed, log_totals, grad_mixed):
    scores = (
        jnp.einsum("sqhd,skhd->shqk", query_rows, key_rows, preferred_element_type=jnp.float32)
        + extra_bias
    )
    scores = jnp.where(allowed, scores, masked_score)
    softmax_out = jnp.exp(scores - log_totals)
    grad_values = jnp.einsum(
        "shqk,sqhd->skhd",
        softmax_out.astype(jnp.bfloat16),
        grad_mixed,
        preferred_element_type=jnp.float32,
    ).astype(jnp.bfloat16)
    grad_probs = jnp.einsum(
        "sqhd,skhd->shqk", grad_mixed, value_rows, preferred_element_type=jnp.float32
    )
    row_dots = jnp.sum(grad_probs * softmax_out, axis=-1, keepdims=True)
    grad_scores = (softmax_out * (grad_probs - row_dots)).astype(jnp.bfloat16)
    grad_queries = jnp.einsum(
        "shqk,skhd->sqhd", grad_scores, key_rows, preferred_element_type=jnp.float32
    ).astype(jnp.bfloat16)
    grad_keys = jnp.einsum(
        "shqk,sqhd->skhd", grad_scores, query_rows, preferred_element_type=jnp.float32
    ).astype(jnp.bfloat16)
    return (grad_queries, grad_keys, grad_values, grad_scores)


def local(
    block_in,
    enc_states,
    dec_len,
    enc_len,
    gain_self,
    self_query,
    self_key,
    self_value,
    self_out,
    rel_table,
    gain_cross,
    cross_query,
    cross_key,
    cross_value,
    cross_out,
    gain_ff,
    ff_in,
    ff_out,
    out_grad,
):
    seq_count = dec_len.shape[0]
    local_heads = rel_table.shape[1]
    head_size = self_query.shape[1] // local_heads

    def heads_view(values, length):
        return values.reshape(seq_count, length, local_heads, head_size)

    def flat_view(values):
        return values.reshape(values.shape[0] * values.shape[1], local_heads * head_size)

    places = jnp.arange(LEN, dtype=jnp.int32)
    causal = places[None, :] <= places[:, None]
    self_allowed = causal[None, None] & (places[None, None, None, :] < dec_len[:, None, None, None])
    enc_places = jnp.arange(ENC, dtype=jnp.int32)
    cross_allowed = enc_places[None, None, None, :] < enc_len[:, None, None, None]
    onehot = bucket_onehot(LEN)
    rel_bias = jnp.einsum(
        "qkb,bh->hqk", onehot, rel_table.astype(jnp.float32), precision=lax.Precision.HIGHEST
    )[None]
    scale_self = gain_self.astype(jnp.float32)
    scale_cross = gain_cross.astype(jnp.float32)
    scale_ff = gain_ff.astype(jnp.float32)
    residual = block_in.astype(jnp.float32)
    full_self = collect_rows(rms_norm(residual, scale_self).astype(jnp.bfloat16))
    query_self = heads_view(matmul(full_self, self_query).astype(jnp.bfloat16), LEN)
    key_self = heads_view(matmul(full_self, self_key).astype(jnp.bfloat16), LEN)
    value_self = heads_view(matmul(full_self, self_value).astype(jnp.bfloat16), LEN)
    mixed_self, logsum_self = attend_forward(
        query_self, key_self, value_self, rel_bias, self_allowed
    )
    mixed_self = flat_view(mixed_self)
    after_self = residual + spread_rows(matmul(mixed_self, self_out))
    full_cross = collect_rows(rms_norm(after_self, scale_cross).astype(jnp.bfloat16))
    query_cross = heads_view(matmul(full_cross, cross_query).astype(jnp.bfloat16), LEN)
    enc_full = lax.all_gather(enc_states, "tensor", axis=0, tiled=True)
    key_flat = matmul(enc_full, cross_key).astype(jnp.bfloat16)
    value_flat = matmul(enc_full, cross_value).astype(jnp.bfloat16)
    key_cross = heads_view(key_flat, ENC)
    value_cross = heads_view(value_flat, ENC)
    mixed_cross, logsum_cross = attend_forward(
        query_cross, key_cross, value_cross, 0.0, cross_allowed
    )
    mixed_cross = flat_view(mixed_cross)
    after_cross = after_self + spread_rows(matmul(mixed_cross, cross_out))
    full_ff = collect_rows(rms_norm(after_cross, scale_ff).astype(jnp.bfloat16))
    pre_act = matmul(full_ff, ff_in)
    hidden = smooth_act(pre_act).astype(jnp.bfloat16)
    block_out = (after_cross + spread_rows(matmul(hidden, ff_out))).astype(jnp.bfloat16)
    grad_top = out_grad.astype(jnp.float32)
    full_grad_ff = collect_rows(out_grad)
    grad_ff_out = inner_rows(hidden, full_grad_ff)
    grad_pre = act_back(pre_act, times_transposed(full_grad_ff, ff_out)).astype(jnp.bfloat16)
    grad_ff_in = inner_rows(full_ff, grad_pre)
    back_values, grad_gain_ff = norm_back(
        after_cross, scale_ff, spread_rows(times_transposed(grad_pre, ff_in))
    )
    grad_after_cross = grad_top + back_values
    full_grad_cross = collect_rows(grad_after_cross.astype(jnp.bfloat16))
    grad_cross_out = inner_rows(mixed_cross, full_grad_cross)
    grad_mixed_cross = heads_view(
        times_transposed(full_grad_cross, cross_out).astype(jnp.bfloat16), LEN
    )
    grad_query, grad_key, grad_value, unused = attend_backward(
        query_cross, key_cross, value_cross, 0.0, cross_allowed, logsum_cross, grad_mixed_cross
    )
    grad_query = flat_view(grad_query)
    grad_key = flat_view(grad_key)
    grad_value = flat_view(grad_value)
    grad_cross_query = inner_rows(full_cross, grad_query)
    grad_cross_key = inner_rows(enc_full, grad_key)
    grad_cross_value = inner_rows(enc_full, grad_value)
    grad_enc = lax.psum_scatter(
        (times_transposed(grad_key, cross_key) + times_transposed(grad_value, cross_value)).astype(
            jnp.bfloat16
        ),
        "tensor",
        scatter_dimension=0,
        tiled=True,
    ).astype(jnp.float32)
    back_values, grad_gain_cross = norm_back(
        after_self, scale_cross, spread_rows(times_transposed(grad_query, cross_query))
    )
    grad_after_self = grad_after_cross + back_values
    full_grad_self = collect_rows(grad_after_self.astype(jnp.bfloat16))
    grad_self_out = inner_rows(mixed_self, full_grad_self)
    grad_mixed_self = heads_view(
        times_transposed(full_grad_self, self_out).astype(jnp.bfloat16), LEN
    )
    grad_query, grad_key, grad_value, grad_scores = attend_backward(
        query_self, key_self, value_self, rel_bias, self_allowed, logsum_self, grad_mixed_self
    )
    grad_rel_table = jnp.einsum(
        "hqk,qkb->bh",
        jnp.sum(grad_scores.astype(jnp.float32), axis=0),
        onehot,
        precision=lax.Precision.HIGHEST,
    )
    grad_query = flat_view(grad_query)
    grad_key = flat_view(grad_key)
    grad_value = flat_view(grad_value)
    grad_self_query = inner_rows(full_self, grad_query)
    grad_self_key = inner_rows(full_self, grad_key)
    grad_self_value = inner_rows(full_self, grad_value)
    grad_normed = (
        times_transposed(grad_query, self_query)
        + times_transposed(grad_key, self_key)
        + times_transposed(grad_value, self_value)
    )
    back_values, grad_gain_self = norm_back(residual, scale_self, spread_rows(grad_normed))
    grad_in = grad_after_self + back_values
    (
        grad_self_query,
        grad_self_key,
        grad_self_value,
        grad_self_out,
        grad_rel_table,
        grad_cross_query,
        grad_cross_key,
        grad_cross_value,
        grad_cross_out,
        grad_ff_in,
        grad_ff_out,
    ) = (
        lax.psum(grad_self_query.astype(jnp.bfloat16), "dp").astype(jnp.float32),
        lax.psum(grad_self_key.astype(jnp.bfloat16), "dp").astype(jnp.float32),
        lax.psum(grad_self_value.astype(jnp.bfloat16), "dp").astype(jnp.float32),
        lax.psum(grad_self_out.astype(jnp.bfloat16), "dp").astype(jnp.float32),
        lax.psum(grad_rel_table.astype(jnp.bfloat16), "dp").astype(jnp.float32),
        lax.psum(grad_cross_query.astype(jnp.bfloat16), "dp").astype(jnp.float32),
        lax.psum(grad_cross_key.astype(jnp.bfloat16), "dp").astype(jnp.float32),
        lax.psum(grad_cross_value.astype(jnp.bfloat16), "dp").astype(jnp.float32),
        lax.psum(grad_cross_out.astype(jnp.bfloat16), "dp").astype(jnp.float32),
        lax.psum(grad_ff_in.astype(jnp.bfloat16), "dp").astype(jnp.float32),
        lax.psum(grad_ff_out.astype(jnp.bfloat16), "dp").astype(jnp.float32),
    )
    grad_gain_self, grad_gain_cross, grad_gain_ff = lax.psum(
        (grad_gain_self, grad_gain_cross, grad_gain_ff), ("dp", "tensor")
    )
    return (
        block_out,
        grad_in,
        grad_enc,
        grad_gain_self,
        grad_self_query,
        grad_self_key,
        grad_self_value,
        grad_self_out,
        grad_rel_table,
        grad_gain_cross,
        grad_cross_query,
        grad_cross_key,
        grad_cross_value,
        grad_cross_out,
        grad_gain_ff,
        grad_ff_in,
        grad_ff_out,
    )


def solution(mesh):
    placed = (
        P(("dp", "tensor"), None),
        P(("dp", "tensor"), None),
        P("dp"),
        P("dp"),
        P(),
        P(None, "tensor"),
        P(None, "tensor"),
        P(None, "tensor"),
        P("tensor", None),
        P(None, "tensor"),
        P(),
        P(None, "tensor"),
        P(None, "tensor"),
        P(None, "tensor"),
        P("tensor", None),
        P(),
        P(None, "tensor"),
        P("tensor", None),
        P(("dp", "tensor"), None),
    )
    return jax.shard_map(
        local,
        mesh=mesh,
        in_specs=placed,
        out_specs=(
            P(("dp", "tensor"), None),
            P(("dp", "tensor"), None),
            P(("dp", "tensor"), None),
            P(),
            P(None, "tensor"),
            P(None, "tensor"),
            P(None, "tensor"),
            P("tensor", None),
            P(None, "tensor"),
            P(),
            P(None, "tensor"),
            P(None, "tensor"),
            P(None, "tensor"),
            P("tensor", None),
            P(),
            P(None, "tensor"),
            P("tensor", None),
        ),
        check_vma=False,
    )
```

profile of v0, /device:TPU:0, one launch (start us, length us, event | category | flops | bytes accessed | tf_op | source)
XLA Modules:
  0.0 1159.5 jit_solution(13267662903418676840)
XLA Ops:
  14.8 11.5 copy.126
  28.7 15.5 %all-gather.8.cloned.1.call-done = bf16[2048,768]{1,0:T(8,128)(2,1)} async-done(((bf16[512,768]{1,0:T(8,128)(2,1)}), bf16[2048,768]{1,0:T(8,128)(2,1)}) %all-gather.8.cloned.1.call-update) | async-done | bytes 3145744 | tf_op jit(solution)/shard_map/all_gather | solution.py:44
  62.4 57.7 %reduce-scatter.8.cloned.1.call-done = f32[512,768]{1,0:T(8,128)} async-done(((f32[2048,768]{1,0:T(8,128)}), f32[512,768]{1,0:T(8,128)}) %reduce-scatter.8.cloned.1.call-update) | async-done | bytes 1572880 | tf_op jit(solution)/shard_map/reduce_scatter | solution.py:48
  123.8 80.1 %all-gather.10.cloned.1.call-done = bf16[8192,768]{1,0:T(8,128)(2,1)} async-done(((bf16[2048,768]{1,0:T(8,128)(2,1)}), bf16[8192,768]{1,0:T(8,128)(2,1)}) %all-gather.10.cloned.1.call-update) | async-done | bytes 12582928 | tf_op jit(solution)/shard_map/all_gather | solution.py:183
  203.9 8.9 convolution_convert_fusion
  225.1 9.4 all-gather.12.cloned.1.call-done
  238.0 11.5 select_reduce_fusion
  249.5 11.0 fusion
  260.5 17.9 %fusion.58 = bf16[8,256,3,64]{1,3,2,0:T(8,128)(2,1)S(1)} fusion(f32[8,3,256,1024]{3,2,1,0:T(8,128)} %get-tuple-element.48, f32[8,3,256]{2,1,0:T(4,128)S(1)} %fusion, f32[8,3,256]{2,1,0:T(4,128)S(1)} %get-tuple-element.47, pred[8,1024]{1,0:T(8,128)(4,1)S(1)} %iota_compare_fusion.2, bf16[8,1024,3,64]{1,0,3,2:T(8,128)(2,1)} %bitcast.180), kind=kOutput, calls=%fused_computation.96 | convolution fusion | flops 830865408 | bytes 29155328 | tf_op jit(solution)/shard_map/shqk,skhd->sqhd/dot_general | solution.py:95
  283.8 57.8 %reduce-scatter.10.cloned.1.call-done = f32[512,768]{1,0:T(8,128)} async-done(((f32[2048,768]{1,0:T(8,128)}), f32[512,768]{1,0:T(8,128)}) %reduce-scatter.10.cloned.1.call-update) | async-done | bytes 1572880 | tf_op jit(solution)/shard_map/reduce_scatter | solution.py:48
  345.6 26.0 %all-gather.16.cloned.1.call-done = bf16[2048,768]{1,0:T(8,128)(2,1)} async-done(((bf16[512,768]{1,0:T(8,128)(2,1)}), bf16[2048,768]{1,0:T(8,128)(2,1)}) %all-gather.16.cloned.1.call-update) | async-done | bytes 3145744 | tf_op jit(solution)/shard_map/all_gather | solution.py:44
  371.6 7.6 fusion.91
  379.2 23.1 %all-gather.14.cloned.1.call-done = bf16[2048,768]{1,0:T(8,128)(2,1)} async-done(((bf16[512,768]{1,0:T(8,128)(2,1)}), bf16[2048,768]{1,0:T(8,128)(2,1)}) %all-gather.14.cloned.1.call-update) | async-done | bytes 3145744 | tf_op jit(solution)/shard_map/all_gather | solution.py:44
  402.3 12.0 %fusion.14 = (bf16[2048,768]{1,0:T(8,128)(2,1)S(1)}, f32[2048,768]{1,0:T(8,128)}) fusion(f32[2048,768]{1,0:T(8,128)} %fusion.91, bf16[2048,768]{1,0:T(8,128)(2,1)} %all-gather.14.cloned.1.call-done, bf16[768,768]{1,0:T(8,128)(2,1)S(1)} %copy-done), kind=kOutput, calls=%fused_computation.25 | convolution fusion | flops 2447376384 | bytes 20054016 | tf_op jit(solution)/shard_map/dot_general | solution.py:70
  420.6 58.4 %reduce-scatter.14.cloned.1.call-done = f32[512,768]{1,0:T(8,128)} async-done(((f32[2048,768]{1,0:T(8,128)}), f32[512,768]{1,0:T(8,128)}) %reduce-scatter.14.cloned.1.call-update) | async-done | bytes 1572880 | tf_op jit(solution)/shard_map/reduce_scatter | solution.py:48
  485.1 28.6 %all-gather.18.cloned.1.call-done = bf16[2048,768]{1,0:T(8,128)(2,1)} async-done(((bf16[512,768]{1,0:T(8,128)(2,1)}), bf16[2048,768]{1,0:T(8,128)(2,1)}) %all-gather.18.cloned.1.call-update) | async-done | bytes 3145744 | tf_op jit(solution)/shard_map/all_gather | solution.py:44
  516.9 23.5 %multiply_reduce_fusion = (f32[8,3,256]{2,1,0:T(4,128)S(1)}, f32[8,3,256,1024]{3,2,1,0:T(8,128)}) fusion(f32[8,3,256,1024]{3,2,1,0:T(8,128)} %get-tuple-element.48, f32[8,3,256]{2,1,0:T(4,128)S(1)} %log_add_fusion.1, pred[8,1024]{1,0:T(8,128)(4,1)S(1)} %iota_compare_fusion.2, bf16[8,1024,3,64]{1,0,3,2:T(8,128)(2,1)} %bitcast.181, ...), kind=kOutput, calls=%fused_computation.2 | convolution fusion | flops 830466048 | bytes 54321152 | tf_op jit(solution)/shard_map/sqhd,skhd->shqk/dot_general | solution.py:114
  540.4 21.8 %multiply_convert_fusion = bf16[8,3,256,1024]{3,2,1,0:T(8,128)(2,1)} fusion(f32[8,3,256,1024]{3,2,1,0:T(8,128)} %get-tuple-element.52, f32[8,3,256,1024]{3,2,1,0:T(8,128)} %get-tuple-element.48, f32[8,3,256]{2,1,0:T(4,128)S(1)} %get-tuple-element.51, f32[8,3,256]{2,1,0:T(4,128)S(1)} %log_add_fusion.1, pred[8,1024]{1,0:T(8,128)(4,1)S(1)} %iota_compare_fusion.2), kind=kLoop, calls=%fused_computation.1 | loop fusion | flops 31457280 | bytes 62971904 | tf_op jit(solution)/shard_map/convert_element_type | solution.py:118
  562.3 10.4 fusion.53
  579.3 10.6 fusion.85
  597.8 7.3 convolution_convert_fusion.8
  605.1 32.7 %reduce-scatter.16.cloned.1.call-done = f32[512,768]{1,0:T(8,128)} async-done(((f32[2048,768]{1,0:T(8,128)}), f32[512,768]{1,0:T(8,128)}) %reduce-scatter.16.cloned.1.call-update) | async-done | bytes 1572880 | tf_op jit(solution)/shard_map/reduce_scatter | solution.py:48
  640.2 58.5 %reduce-scatter.12.cloned.1.call-done = f32[512,768]{1,0:T(8,128)} async-done(((f32[2048,768]{1,0:T(8,128)}), f32[512,768]{1,0:T(8,128)}) %reduce-scatter.12.cloned.1.call-update) | async-done | bytes 1572880 | tf_op jit(solution)/shard_map/reduce_scatter | solution.py:48
  704.3 11.3 convert_bitcast_fusion
  719.6 8.1 convert_bitcast_fusion.1
  772.7 13.9 %fusion.96 = f32[8192,768]{1,0:T(8,128)} fusion(bf16[8192,192]{0,1:T(8,128)(2,1)} %bitcast.179, bf16[768,192]{0,1:T(8,128)(2,1)S(1)} %copy-done.35), kind=kOutput, calls=%fused_computation.154 | convolution fusion | flops 2415919104 | bytes 28606464 | tf_op jit(solution)/shard_map/dot_general | solution.py:80
  786.6 14.6 %add_convert_fusion = bf16[8192,768]{1,0:T(8,128)(2,1)} fusion(f32[8192,768]{1,0:T(8,128)} %fusion.96, bf16[8192,192]{0,1:T(8,128)(2,1)} %bitcast.177, bf16[768,192]{0,1:T(8,128)(2,1)S(1)} %copy-done.37), kind=kOutput, calls=%fused_computation | convolution fusion | flops 2428502016 | bytes 41189376 | tf_op jit(solution)/shard_map/dot_general | solution.py:80
  813.5 22.4 %psum.103 = bf16[32,3]{0,1:T(4,128)(2,1)S(1)} all-reduce(bf16[32,3]{0,1:T(4,128)(2,1)S(1)} %fusion.63), channel_id=1, replica_groups=mesh['dp'=8,'tensor'=4] {'dp'}, use_global_device_ids=true, to_apply=%region_27.28 | all-reduce | flops 96 | bytes 384 | tf_op jit(solution)/shard_map/psum | solution.py:276
  836.4 108.9 %all-reduce.4.cloned.1.call-done = (bf16[768,192]{0,1:T(8,128)(2,1)}, bf16[768,192]{0,1:T(8,128)(2,1)}, bf16[768,192]{0,1:T(8,128)(2,1)}, bf16[192,768]{1,0:T(8,...) async-done(((bf16[768,192]{0,1:T(8,128)(2,1)}, ...) | async-done | bytes 4718608 | tf_op jit(solution)/shard_map/psum | solution.py:272
  959.4 86.4 %reduce-scatter.20.cloned.1.call-done = bf16[2048,768]{1,0:T(8,128)(2,1)} async-done(((bf16[8192,768]{1,0:T(8,128)(2,1)}), bf16[2048,768]{1,0:T(8,128)(2,1)}) %reduce-scatter.20.cloned.1.call-update) | async-done | bytes 3145744 | tf_op jit(solution)/shard_map/reduce_scatter | solution.py:220
  1050.9 55.8 %reduce-scatter.18.cloned.1.call-done = f32[512,768]{1,0:T(8,128)} async-done(((f32[2048,768]{1,0:T(8,128)}), f32[512,768]{1,0:T(8,128)}) %reduce-scatter.18.cloned.1.call-update) | async-done | bytes 1572880 | tf_op jit(solution)/shard_map/reduce_scatter | solution.py:48
  1110.1 39.7 %all-reduce = (f32[768]{0:T(1024)}, f32[768]{0:T(1024)}, f32[768]{0:T(1024)}) all-reduce(f32[768]{0:T(1024)} %get-tuple-element.21, f32[768]{0:T(1024)} %get-tuple-element.19, f32[768]{0:T(1024)S(1)} %copy-done.77), channel_id=1, replica_groups=mesh['dp'=8,'tensor'=4] {'dp','tensor'}, use_global_device_ids=true, to_apply=%region_21.22 | all-reduce | flops 2304 | bytes 18432 | tf_op jit(solution)/shard_map/psum | solution.py:284
  (319 shorter events, 181.2 us)
Async XLA Ops:
  7.2 395.1 %copy-start = (bf16[768,768]{1,0:T(8,128)(2,1)S(1)}, bf16[768,768]{1,0:T(8,128)(2,1)}, u32[]{:S(2)}) copy-start(bf16[768,768]{1,0:T(8,128)(2,1)} %param.36) | copy-start | bytes 3538948
  7.2 37.0 %all-gather.8.cloned.1.call-start = ((), (), s32[]{:S(2)}) async-start(), calls=%async_computation.7 | async-start | bytes 3932160 | tf_op jit(solution)/shard_map/all_gather | solution.py:44
  12.9 107.2 %reduce-scatter.8.cloned.1.call-start = ((), (), s32[]{:S(2)}) async-start(), calls=%async_computation.8 | async-start | bytes 7864320 | tf_op jit(solution)/shard_map/reduce_scatter | solution.py:48
  61.6 58.5 %copy-start.9 = (bf16[512,768]{1,0:T(8,128)(2,1)S(1)}, bf16[512,768]{1,0:T(8,128)(2,1)}, u32[]{:S(2)}) copy-start(bf16[512,768]{1,0:T(8,128)(2,1)} %param.20) | copy-start | bytes 2359300
  61.6 142.3 %all-gather.10.cloned.1.call-start = ((), (), s32[]{:S(2)}) async-start(), calls=%async_computation.9 | async-start | bytes 15728640 | tf_op jit(solution)/shard_map/all_gather | solution.py:183
  62.3 172.2 %all-gather.12.cloned.1.call-start = ((), (), s32[]{:S(2)}) async-start(), calls=%async_computation.10 | async-start | bytes 3932160 | tf_op jit(solution)/shard_map/all_gather | solution.py:44
  62.4 61.0 %copy-start.61 = (f32[768]{0:T(1024)}, f32[768]{0:T(1024)S(1)}, u32[]{:S(2)}) copy-start(f32[768]{0:T(1024)S(1)} %convert_element_type.226) | copy-start | bytes 9220
  62.4 61.3 %copy-start.83 = (s32[8]{0:T(128)S(1)}, s32[8]{0:T(128)}, u32[]{:S(2)}) copy-start(s32[8]{0:T(128)} %param.23) | copy-start | bytes 100
  122.4 90.4 %copy-start.67 = (f32[512]{0:T(512)}, f32[512]{0:T(512)S(1)}, u32[]{:S(2)}) copy-start(f32[512]{0:T(512)S(1)} %fusion.79) | copy-start | bytes 6148
  123.5 218.1 %reduce-scatter.10.cloned.1.call-start = ((), (), s32[]{:S(2)}) async-start(), calls=%async_computation.11 | async-start | bytes 7864320 | tf_op jit(solution)/shard_map/reduce_scatter | solution.py:48
  283.1 88.5 %all-gather.16.cloned.1.call-start = ((), (), s32[]{:S(2)}) async-start(), calls=%async_computation.14 | async-start | bytes 3932160 | tf_op jit(solution)/shard_map/all_gather | solution.py:44
  283.7 118.6 %all-gather.14.cloned.1.call-start = ((), (), s32[]{:S(2)}) async-start(), calls=%async_computation.12 | async-start | bytes 3932160 | tf_op jit(solution)/shard_map/all_gather | solution.py:44
  345.5 133.5 %reduce-scatter.14.cloned.1.call-start = ((), (), s32[]{:S(2)}) async-start(), calls=%async_computation.15 | async-start | bytes 7864320 | tf_op jit(solution)/shard_map/reduce_scatter | solution.py:48
  420.5 61.6 %copy-start.76 = (f32[512]{0:T(512)S(1)}, f32[512]{0:T(512)}, u32[]{:S(2)}) copy-start(f32[512]{0:T(512)} %copy-done.75) | copy-start | bytes 6148
  420.6 61.6 %copy-start.17 = (bf16[512,768]{1,0:T(8,128)(2,1)S(1)}, bf16[512,768]{1,0:T(8,128)(2,1)}, u32[]{:S(2)}) copy-start(bf16[512,768]{1,0:T(8,128)(2,1)} %param.38) | copy-start | bytes 2359300
  420.6 93.1 %all-gather.18.cloned.1.call-start = ((), (), s32[]{:S(2)}) async-start(), calls=%async_computation.16 | async-start | bytes 3932160 | tf_op jit(solution)/shard_map/all_gather | solution.py:44
  485.0 152.8 %reduce-scatter.16.cloned.1.call-start = ((), (), s32[]{:S(2)}) async-start(), calls=%async_computation.17 | async-start | bytes 7864320 | tf_op jit(solution)/shard_map/reduce_scatter | solution.py:48
  579.3 119.5 %reduce-scatter.12.cloned.1.call-start = ((), (), s32[]{:S(2)}) async-start(), calls=%async_computation.13 | async-start | bytes 7864320 | tf_op jit(solution)/shard_map/reduce_scatter | solution.py:48
  589.9 153.8 %all-gather.20.cloned.1.call-start = ((), (), s32[]{:S(2)}) async-start(), calls=%async_computation.18 | async-start | bytes 3932160 | tf_op jit(solution)/shard_map/all_gather | solution.py:44
  597.7 40.0 %copy-start.62 = (f32[768]{0:T(1024)S(1)}, f32[768]{0:T(1024)}, u32[]{:S(2)}) copy-start(f32[768]{0:T(1024)} %copy-done.61) | copy-start | bytes 9220
  597.7 40.0 %copy-start.68 = (f32[512]{0:T(512)S(1)}, f32[512]{0:T(512)}, u32[]{:S(2)}) copy-start(f32[512]{0:T(512)} %copy-done.67) | copy-start | bytes 6148
  605.1 93.6 %copy-start.72 = (f32[512]{0:T(512)S(1)}, f32[512]{0:T(512)}, u32[]{:S(2)}) copy-start(f32[512]{0:T(512)} %copy-done.71) | copy-start | bytes 6148
  704.3 241.0 %all-reduce.4.cloned.1.call-start = ((), (), s32[]{:S(2)}) async-start(), calls=%async_computation.21 | async-start | bytes 9437184 | tf_op jit(solution)/shard_map/psum | solution.py:272
  771.8 274.0 %reduce-scatter.20.cloned.1.call-start = ((), (), s32[]{:S(2)}) async-start(), calls=%async_computation.20 | async-start | bytes 15728640 | tf_op jit(solution)/shard_map/reduce_scatter | solution.py:220
  801.3 305.5 %reduce-scatter.18.cloned.1.call-start = ((), (), s32[]{:S(2)}) async-start(), calls=%async_computation.19 | async-start | bytes 7864320 | tf_op jit(solution)/shard_map/reduce_scatter | solution.py:48
  959.4 147.3 %copy-start.10 = (bf16[512,768]{1,0:T(8,128)(2,1)S(1)}, bf16[512,768]{1,0:T(8,128)(2,1)}, u32[]{:S(2)}) copy-start(bf16[512,768]{1,0:T(8,128)(2,1)} %param.20) | copy-start | bytes 2359300
  959.4 147.3 %copy-start.64 = (f32[768]{0:T(1024)S(1)}, f32[768]{0:T(1024)}, u32[]{:S(2)}) copy-start(f32[768]{0:T(1024)} %copy-done.63) | copy-start | bytes 9220
  959.4 147.3 %copy-start.66 = (f32[512]{0:T(512)S(1)}, f32[512]{0:T(512)}, u32[]{:S(2)}) copy-start(f32[512]{0:T(512)} %copy-done.65) | copy-start | bytes 6148
  959.4 150.1 %copy-start.74 = (f32[512]{0:T(512)S(1)}, f32[512]{0:T(512)}, u32[]{:S(2)}) copy-start(f32[512]{0:T(512)} %copy-done.73) | copy-start | bytes 6148
  959.4 150.7 %copy-start.77 = (f32[768]{0:T(1024)S(1)}, f32[768]{0:T(1024)}, u32[]{:S(2)}) copy-start(f32[768]{0:T(1024)} %get-tuple-element.17) | copy-start | bytes 9220
  1106.7 43.1 %copy-start.24 = (f32[512,768]{1,0:T(8,128)S(1)}, f32[512,768]{1,0:T(8,128)}, u32[]{:S(2)}) copy-start(f32[512,768]{1,0:T(8,128)} %reduce-scatter.18.cloned.1.call-done) | copy-start | bytes 4718596
  1106.7 46.0 %copy-start.1 = (bf16[768,768]{1,0:T(8,128)(2,1)S(1)}, bf16[768,768]{1,0:T(8,128)(2,1)}, u32[]{:S(2)}) copy-start(bf16[768,768]{1,0:T(8,128)(2,1)} %param.36) | copy-start | bytes 3538948
  (75 other events, 447.0 us)
Sparse Core Ops, SparseCore 0:
  13.0 31.2 all-gather.7
  61.7 58.3 reduce-scatter.7
  121.7 82.0 all-gather.9
  205.9 28.5 all-gather.11
  283.2 58.3 reduce-scatter.9
  343.0 28.5 all-gather.15
  373.8 28.5 all-gather.13
  420.7 58.3 reduce-scatter.13
  485.1 28.5 all-gather.17
  579.4 58.3 reduce-scatter.15
  640.3 58.3 reduce-scatter.11
  704.4 28.5 all-gather.19
  771.9 173.4 all-reduce.3
  948.0 97.7 reduce-scatter.19
  1048.3 58.3 reduce-scatter.17
where the time goes:
time: 1170 us; the launch traced here: 1160 us
  waiting for transfers between devices  700 us (60%)
  matrix products  240 us (21%)
  other arithmetic  92.2 us (8%)
  blocking collectives  62.1 us (5%)
  local copies, waits for them, and re-layouts  48.2 us (4%)
  between operations  15.3 us (1%)
    reduce_scatter x6, waiting for transfers between devices, spread_rows(): return lax.psum_scatter(values, 'tensor', scatter_dimension=0, tiled=True)  321 us
    psum x1, waiting for transfers between devices, local(): lax.psum(grad_self_query.astype(jnp.bfloat16), 'dp').astype(jnp.float32)  109 us
    all_gather x6, waiting for transfers between devices, collect_rows(): return lax.all_gather(values, 'tensor', axis=0, tiled=True)  103 us
    reduce_scatter x1, waiting for transfers between devices, local(): lax.psum_scatter((times_transposed(grad_key, cross_key) + times_transpose...  86.4 us
    all_gather x1, waiting for transfers between devices, local(): enc_full = lax.all_gather(enc_states, 'tensor', axis=0, tiled=True)  80.1 us
    dot_general x10, matrix products, times_transposed(): lax.dot_general(former, latter, (((1,), (1,)), ((), ())), preferred_eleme...  56.5 us
    dot_general x10, matrix products, matmul(): return jnp.dot(former, latter, preferred_element_type=jnp.float32)  52.1 us
    psum x1, blocking collectives, local(): lax.psum((grad_gain_self, grad_gain_cross, grad_gain_ff), ('dp', 'tensor'))  39.7 us
  transfers between devices with their start and end apart: 15, of which 14 were waited for; matrix products, arithmetic and copies ran while one was open for 15% of the time, Pallas kernels for 0%

commit v1 on v0

v1 whole, which is shorter than its diff:
```python
import math

import jax
import jax.numpy as jnp
import numpy as np
from jax import lax
from jax.experimental import pallas as pl
from jax.experimental.pallas import tpu as pltpu
from jax.sharding import PartitionSpec as P

BUCKETS = 32
MAX_DIST = 128
LEN = 256
ENC = 1024
DH = 64

norm_eps = 1e-06
masked_score = -1000000000.0
bf16 = jnp.bfloat16
f32 = jnp.float32
VMEM_CAP = 60 * 1024 * 1024


def bucket_of_distance():
    half_count = BUCKETS // 2
    growth_ratio = MAX_DIST / half_count
    limits = np.array(
        [int(math.ceil(half_count * growth_ratio ** (m / half_count))) for m in range(1, half_count)],
        dtype=np.int32,
    )
    distance = np.arange(LEN, dtype=np.int32)
    above = np.sum(distance[:, None] >= limits[None, :], axis=1)
    return np.where(distance < half_count, distance, half_count + above).astype(np.int32)


def nn(a, b):
    return lax.dot_general(a, b, (((1,), (0,)), ((), ())), preferred_element_type=f32)


def nt(a, b):
    return lax.dot_general(a, b, (((1,), (1,)), ((), ())), preferred_element_type=f32)


def tn(a, b):
    return lax.dot_general(a, b, (((0,), (0,)), ((), ())), preferred_element_type=f32)


def inv_rms(v):
    return lax.rsqrt(jnp.mean(v * v, axis=-1, keepdims=True) + norm_eps)


def normed(v, gain):
    return (v * inv_rms(v) * gain).astype(bf16)


def norm_back(v, gain, e):
    s = inv_rms(v)
    ge = gain * e
    dot = jnp.mean(ge * v, axis=-1, keepdims=True)
    grad_v = s * ge - v * (s * s * s * dot)
    grad_gain = jnp.sum(e * v * s, axis=0, keepdims=True)
    return grad_v, grad_gain


def lane_half(shape, h):
    lane = lax.broadcasted_iota(jnp.int32, shape, 1)
    return (lane < DH) if h == 0 else (lane >= DH)


def call(kernel, out_shape, args, *, grid=(), in_specs=None, out_specs=None, scratch=(), flops=0, nbytes=0, trans=0, name=None):
    kw = {}
    if in_specs is not None:
        kw["in_specs"] = in_specs
    if out_specs is not None:
        kw["out_specs"] = out_specs
    return pl.pallas_call(
        kernel,
        out_shape=out_shape,
        grid=grid,
        scratch_shapes=scratch,
        compiler_params=pltpu.CompilerParams(vmem_limit_bytes=VMEM_CAP),
        cost_estimate=pl.CostEstimate(flops=int(flops), bytes_accessed=int(nbytes), transcendentals=int(trans)),
        name=name,
        **kw,
    )(*args)


def whole(shape):
    return pl.BlockSpec(shape, lambda *_: (0,) * len(shape))


SMEM = pl.BlockSpec(memory_space=pltpu.SMEM)


def pack_kernel(y_ref, q_ref, k_ref, v_ref, o_ref, own_ref, half_ref):
    w = o_ref.shape[0]
    own_ref[0:w] = q_ref[...].T
    own_ref[w : 2 * w] = k_ref[...].T
    own_ref[2 * w : 3 * w] = v_ref[...].T
    own_ref[3 * w : 4 * w] = o_ref[...]
    y = y_ref[0]

    @pl.when(y == 0)
    def _():
        half_ref[...] = own_ref[0 : 2 * w]

    @pl.when(y != 0)
    def _():
        half_ref[...] = own_ref[2 * w : 4 * w]


def pack(y, q, k, v, o):
    w, d = o.shape
    return call(
        pack_kernel,
        (jax.ShapeDtypeStruct((4 * w, d), bf16), jax.ShapeDtypeStruct((2 * w, d), bf16)),
        (y, q, k, v, o),
        in_specs=[SMEM] + [whole(t.shape) for t in (q, k, v, o)],
        out_specs=(whole((4 * w, d)), whole((2 * w, d))),
        nbytes=4 * 4 * w * d,
        name="pack",
    )


def self_fwd_kernel(last, len_ref, x_ref, g_ref, g2_ref, wa_ref, wb_ref, bias_ref, *rest):
    if last:
        xin_ref, q_ref, k_ref, vt_ref, e_ref, r_ref, at_ref, x1_ref, n1_ref, n2_ref, bs_ref = rest
    else:
        q_ref, k_ref, vt_ref, e_ref, r_ref, at_ref, x1_ref, bs_ref = rest
    w = wa_ref.shape[0] // 4
    nh = 2 * w // DH
    nb = x_ref.shape[0] // LEN
    x = x_ref[...].astype(f32)
    n1 = normed(x, g_ref[...].astype(f32))
    if last:
        n1_ref[...] = n1

    def rows(i):
        return jnp.concatenate([wa_ref[i * w : (i + 1) * w], wb_ref[i * w : (i + 1) * w]], axis=0)

    q_ref[...] = nt(n1, rows(0)).astype(bf16)
    k_ref[...] = nt(n1, rows(1)).astype(bf16)
    vt_ref[...] = nt(rows(2), n1).astype(bf16)
    key = lax.broadcasted_iota(jnp.int32, (LEN, LEN), 0)
    query = lax.broadcasted_iota(jnp.int32, (LEN, LEN), 1)
    for p in range(nh // 2):
        lanes = slice(p * 2 * DH, (p + 1) * 2 * DH)
        for h in range(2):
            row = jnp.broadcast_to(bias_ref[2 * p + h : 2 * p + h + 1, :], (LEN, LEN))
            bs_ref[h] = pltpu.roll(row, 0, 1, stride=1, stride_axis=0)
        for b in range(nb):
            tok = slice(b * LEN, (b + 1) * LEN)
            allowed = (key <= query) & (key < len_ref[b])
            kp = k_ref[tok, lanes]
            qp = q_ref[tok, lanes]
            outs = []
            for h in range(2):
                head = 2 * p + h
                qh = jnp.where(lane_half(qp.shape, h), qp, jnp.zeros_like(qp))
                s = nt(kp, qh) + bs_ref[h]
                s = jnp.where(allowed, s, masked_score)
                top = jnp.max(s, axis=0, keepdims=True)
                e = jnp.exp(s - top)
                r = 1.0 / jnp.sum(e, axis=0, keepdims=True)
                eb = e.astype(bf16)
                e_ref[b, head] = eb
                r_ref[b, head : head + 1, :] = r
                outs.append(nn(vt_ref[head * DH : (head + 1) * DH, tok], eb) * r)
            at_ref[lanes, tok] = jnp.concatenate(outs, axis=0).astype(bf16)
    mixed = tn(at_ref[...], rows(3))
    if last:
        x1 = xin_ref[...] + mixed
        n2_ref[...] = normed(x1, g2_ref[...].astype(f32))
    else:
        x1 = x + mixed
    x1_ref[...] = x1


def self_fwd(last, lens, x, g, g2, wa, wb, bias, xin=None):
    t, d = x.shape
    w = wa.shape[0] // 4
    c = 2 * w
    nh = c // DH
    nb = t // LEN
    outs = [
        jax.ShapeDtypeStruct((t, c), bf16),
        jax.ShapeDtypeStruct((t, c), bf16),
        jax.ShapeDtypeStruct((c, t), bf16),
        jax.ShapeDtypeStruct((nb, nh, LEN, LEN), bf16),
        jax.ShapeDtypeStruct((nb, nh, LEN), f32),
        jax.ShapeDtypeStruct((c, t), bf16),
        jax.ShapeDtypeStruct((t, d), f32),
    ]
    args = [lens, x, g, g2, wa, wb, bias]
    if last:
        args.append(xin)
        outs += [jax.ShapeDtypeStruct((t, d), bf16)] * 2
    flops = 2 * t * d * c * 4 + 2 * t * LEN * nh * 128 * 2
    return call(
        lambda *r: self_fwd_kernel(last, *r),
        tuple(outs),
        args,
        in_specs=[SMEM] + [whole(a.shape) for a in args[1:]],
        out_specs=tuple(whole(o.shape) for o in outs),
        scratch=[pltpu.VMEM((2, LEN, LEN), f32)],
        flops=flops * 3,
        nbytes=12 * 1024 * 1024,
        trans=t * LEN * nh,
        name="self_fwd",
    )


def enc_kv_kernel(enc_ref, wa_ref, wb_ref, k_ref, kt_ref, v_ref, vt_ref):
    w = wa_ref.shape[0] // 4
    enc = enc_ref[...]

    def rows(i):
        return jnp.concatenate([wa_ref[i * w : (i + 1) * w], wb_ref[i * w : (i + 1) * w]], axis=0)

    wk = rows(1)
    wv = rows(2)
    k = nt(enc, wk).astype(bf16)
    k_ref[...] = k
    kt_ref[...] = k.T
    vt = nt(wv, enc).astype(bf16)
    vt_ref[...] = vt
    v_ref[...] = vt.T


def enc_kv(enc, wa, wb):
    t, d = enc.shape
    c = wa.shape[0] // 2
    rows = 512
    return call(
        enc_kv_kernel,
        (
            jax.ShapeDtypeStruct((t, c), bf16),
            jax.ShapeDtypeStruct((c, t), bf16),
            jax.ShapeDtypeStruct((t, c), bf16),
            jax.ShapeDtypeStruct((c, t), bf16),
        ),
        (enc, wa, wb),
        grid=(t // rows,),
        in_specs=[pl.BlockSpec((rows, d), lambda i: (i, 0)), whole(wa.shape), whole(wb.shape)],
        out_specs=(
            pl.BlockSpec((rows, c), lambda i: (i, 0)),
            pl.BlockSpec((c, rows), lambda i: (0, i)),
            pl.BlockSpec((rows, c), lambda i: (i, 0)),
            pl.BlockSpec((c, rows), lambda i: (0, i)),
        ),
        flops=2 * t * d * c * 2 * 2,
        nbytes=t * d * 2 + 4 * t * c * 2,
        name="enc_kv",
    )


def cross_fwd_kernel(last, pairs, len_ref, n2_ref, g_ref, wa_ref, wb_ref, k_ref, vt_ref, xin_ref, *rest):
    if last:
        q_ref, e_ref, r_ref, at_ref, x2_ref, n3_ref = rest
    else:
        q_ref, e_ref, r_ref, at_ref, x2_ref = rest
    w = wa_ref.shape[0] // 4
    step = pl.program_id(0)
    b = step // pairs
    p = lax.rem(step, pairs)

    def rows(i):
        return jnp.concatenate([wa_ref[i * w : (i + 1) * w], wb_ref[i * w : (i + 1) * w]], axis=0)

    @pl.when(step == 0)
    def _():
        q_ref[...] = nt(n2_ref[...], rows(0)).astype(bf16)

    tok = pl.ds(pl.multiple_of(b * LEN, LEN), LEN)
    lanes = pl.ds(pl.multiple_of(p * 2 * DH, 2 * DH), 2 * DH)
    qp = q_ref[tok, lanes]
    key = lax.broadcasted_iota(jnp.int32, (ENC, LEN), 0)
    allowed = key < len_ref[b]
    outs = []
    for h in range(2):
        qh = jnp.where(lane_half(qp.shape, h), qp, jnp.zeros_like(qp))
        s = nt(k_ref[...], qh)
        s = jnp.where(allowed, s, masked_score)
        top = jnp.max(s, axis=0, keepdims=True)
        e = jnp.exp(s - top)
        r = 1.0 / jnp.sum(e, axis=0, keepdims=True)
        eb = e.astype(bf16)
        e_ref[0, h] = eb
        r_ref[0, h : h + 1, :] = r
        outs.append(nn(vt_ref[h * DH : (h + 1) * DH, :], eb) * r)
    at_ref[lanes, tok] = jnp.concatenate(outs, axis=0).astype(bf16)

    @pl.when(step == pl.num_programs(0) - 1)
    def _():
        x2 = xin_ref[...] + tn(at_ref[...], rows(3))
        x2_ref[...] = x2
        if last:
            n3_ref[...] = normed(x2, g_ref[...].astype(f32))


def cross_fwd(last, lens, n2, g, wa, wb, k, vt, xin):
    t, d = n2.shape
    w = wa.shape[0] // 4
    c = 2 * w
    nb = t // LEN
    pairs = c // (2 * DH)
    outs = [
        jax.ShapeDtypeStruct((t, c), bf16),
        jax.ShapeDtypeStruct((nb * pairs, 2, ENC, LEN), bf16),
        jax.ShapeDtypeStruct((nb * pairs, 2, LEN), f32),
        jax.ShapeDtypeStruct((c, t), bf16),
        jax.ShapeDtypeStruct((t, d), f32),
    ]
    specs = [
        whole((t, c)),
        pl.BlockSpec((1, 2, ENC, LEN), lambda i: (i, 0, 0, 0)),
        pl.BlockSpec((1, 2, LEN), lambda i: (i, 0, 0)),
        whole((c, t)),
        whole((t, d)),
    ]
    if last:
        outs.append(jax.ShapeDtypeStruct((t, d), bf16))
        specs.append(whole((t, d)))
    return call(
        lambda *r: cross_fwd_kernel(last, pairs, *r),
        tuple(outs),
        (lens, n2, g, wa, wb, k, vt, xin),
        grid=(nb * pairs,),
        in_specs=[
            SMEM,
            whole(n2.shape),
            whole(g.shape),
            whole(wa.shape),
            whole(wb.shape),
            pl.BlockSpec((ENC, 2 * DH), lambda i: (i // pairs, i % pairs)),
            pl.BlockSpec((2 * DH, ENC), lambda i: (i % pairs, i // pairs)),
            whole(xin.shape),
        ],
        out_specs=tuple(specs),
        flops=3 * (2 * t * d * c * 2 + 2 * t * ENC * c * 2 * 2),
        nbytes=14 * 1024 * 1024,
        trans=t * ENC * (c // DH),
        name="cross_fwd",
    )


ROOT = math.sqrt(2.0 / math.pi)
CUBE = 0.044715


def ff_kernel(last, n3_ref, gf_ref, wia_ref, woa_ref, wib_ref, wob_ref, *rest):
    if last:
        yin_ref, gin_ref, x2_ref, g_ref = rest[:4]
        gwia, gwoa, gwib, gwob, out_ref, gx2_ref, go2_ref, gg_ref, y_ref, gn_ref, n3t_ref = rest[4:]
    else:
        gwia, gwoa, gwib, gwob, y_ref, gn_ref, n3t_ref = rest
    step = pl.program_id(0)

    @pl.when(step == 0)
    def _():
        n3t_ref[...] = n3_ref[...].T
        if last:
            y_ref[...] = yin_ref[...]
            gn_ref[...] = gin_ref[...]
        else:
            y_ref[...] = jnp.zeros_like(y_ref)
            gn_ref[...] = jnp.zeros_like(gn_ref)

    n3 = n3_ref[...]
    gf = gf_ref[...]
    for wi_ref, wo_ref, gwi, gwo in ((wia_ref, woa_ref, gwia, gwoa), (wib_ref, wob_ref, gwib, gwob)):
        u = nn(n3, wi_ref[...])
        dh = nt(gf, wo_ref[...])
        u2 = u * u
        th = jnp.tanh(ROOT * u * (1.0 + CUBE * u2))
        half = 0.5 * (1.0 + th)
        r = (u * half).astype(bf16)
        slope = half + 0.5 * u * (1.0 - th * th) * (ROOT * (1.0 + (3.0 * CUBE) * u2))
        gu = (dh * slope).astype(bf16)
        y_ref[...] += nn(r, wo_ref[...])
        gn_ref[...] += nt(gu, wi_ref[...])
        gwo[...] = tn(r, gf).astype(bf16)
        gwi[...] = nn(n3t_ref[...], gu).astype(bf16)

    if last:

        @pl.when(step == pl.num_programs(0) - 1)
        def _():
            x2 = x2_ref[...]
            out_ref[...] = (x2 + y_ref[...]).astype(bf16)
            gx, gg = norm_back(x2, g_ref[...].astype(f32), gn_ref[...])
            gx2 = gf.astype(f32) + gx
            gx2_ref[...] = gx2
            go2_ref[...] = gx2.astype(bf16)
            gg_ref[...] = gg


def ff(last, n3, gf, wia, woa, wib, wob, yin=None, gin=None, x2=None, g=None):
    t, d = n3.shape
    hid = wia.shape[1]
    blk = 256
    args = [n3, gf, wia, woa, wib, wob]
    col = pl.BlockSpec((d, blk), lambda i: (0, i))
    row = pl.BlockSpec((blk, d), lambda i: (i, 0))
    in_specs = [whole((t, d)), whole((t, d)), col, row, col, row]
    outs = [jax.ShapeDtypeStruct((d, hid), bf16), jax.ShapeDtypeStruct((hid, d), bf16)] * 2
    specs = [col, row, col, row]
    acc = jax.ShapeDtypeStruct((t, d), f32)
    scratch = [pltpu.VMEM((d, t), bf16)]
    if last:
        args += [yin, gin, x2, g]
        in_specs += [whole((t, d))] * 3 + [whole(g.shape)]
        outs += [jax.ShapeDtypeStruct((t, d), bf16), acc, jax.ShapeDtypeStruct((t, d), bf16), jax.ShapeDtypeStruct((1, d), f32)]
        specs += [whole((t, d))] * 3 + [whole((1, d))]
        scratch = [pltpu.VMEM((t, d), f32)] * 2 + scratch
    else:
        outs += [acc, acc]
        specs += [whole((t, d))] * 2
    return call(
        lambda *r: ff_kernel(last, *r),
        tuple(outs),
        args,
        grid=(hid // blk,),
        in_specs=in_specs,
        out_specs=tuple(specs),
        scratch=scratch,
        flops=2 * 6 * 2 * t * d * hid * 2,
        nbytes=12 * 1024 * 1024,
        trans=2 * t * hid,
        name="ff",
    )


def head_pair_back(k_t, v, q, ga, ga_t, a_t, es, rs, extra=None):
    gv = None
    gk = None
    gq_t = []
    for h in range(2):
        part = slice(h * DH, (h + 1) * DH)
        r = rs[h]
        gah = ga_t[part].astype(f32) * r
        delta = jnp.sum(gah * a_t[part].astype(f32), axis=0, keepdims=True)
        gah = gah.astype(bf16)
        zero = jnp.zeros_like(gah)
        rhs = jnp.concatenate([gah, zero] if h == 0 else [zero, gah], axis=0)
        gp = nn(v, rhs)
        e = es[h]
        gs = (e.astype(f32) * (gp - delta)).astype(bf16)
        if extra is not None:
            extra(h, gs)
        keep = lane_half(q.shape, h)
        term_v = nt(e, rhs)
        term_k = nn(gs, jnp.where(keep, q, jnp.zeros_like(q)))
        gv = term_v if gv is None else gv + term_v
        gk = term_k if gk is None else gk + term_k
        gq_t.append(nn(k_t[part], gs))
    return jnp.concatenate(gq_t, axis=0).astype(bf16), gk.astype(bf16), gv.astype(bf16)


def cross_bwd_kernel(pairs, go_ref, n2_ref, wa_ref, wb_ref, q_ref, kt_ref, v_ref, e_ref, r_ref, at_ref, gin_ref,
                     gk_ref, gv_ref, gqoa_ref, gqob_ref, gn_ref, gat_ref, gqt_ref):
    w = wa_ref.shape[0] // 4
    step = pl.program_id(0)
    b = step // pairs
    p = lax.rem(step, pairs)

    def rows(i):
        return jnp.concatenate([wa_ref[i * w : (i + 1) * w], wb_ref[i * w : (i + 1) * w]], axis=0)

    @pl.when(step == 0)
    def _():
        gat_ref[...] = nt(rows(3), go_ref[...]).astype(bf16)

    tok = pl.ds(pl.multiple_of(b * LEN, LEN), LEN)
    lanes = pl.ds(pl.multiple_of(p * 2 * DH, 2 * DH), 2 * DH)
    gq, gk, gv = head_pair_back(
        kt_ref[...], v_ref[...], q_ref[tok, lanes], None, gat_ref[lanes, tok], at_ref[lanes, tok],
        [e_ref[0, 0], e_ref[0, 1]], [r_ref[0, 0:1, :], r_ref[0, 1:2, :]],
    )
    gqt_ref[lanes, tok] = gq
    gk_ref[...] = gk
    gv_ref[...] = gv

    @pl.when(step == pl.num_programs(0) - 1)
    def _():
        gqt = gqt_ref[...]
        gwq = nn(gqt, n2_ref[...]).astype(bf16)
        gwo = nn(at_ref[...], go_ref[...]).astype(bf16)
        gqoa_ref[0:w] = gwq[0:w]
        gqob_ref[0:w] = gwq[w:]
        gqoa_ref[w:] = gwo[0:w]
        gqob_ref[w:] = gwo[w:]
        gn_ref[...] = gin_ref[...] + tn(gqt, rows(0))


def cross_bwd(go, n2, wa, wb, q, kt, v, e, r, at, gin):
    t, d = go.shape
    w = wa.shape[0] // 4
    c = 2 * w
    nb = t // LEN
    pairs = c // (2 * DH)
    te = v.shape[0]
    tokhead = pl.BlockSpec((ENC, 2 * DH), lambda i: (i // pairs, i % pairs))
    return call(
        lambda *r_: cross_bwd_kernel(pairs, *r_),
        (
            jax.ShapeDtypeStruct((te, c), bf16),
            jax.ShapeDtypeStruct((te, c), bf16),
            jax.ShapeDtypeStruct((2 * w, d), bf16),
            jax.ShapeDtypeStruct((2 * w, d), bf16),
            jax.ShapeDtypeStruct((t, d), f32),
        ),
        (go, n2, wa, wb, q, kt, v, e, r, at, gin),
        grid=(nb * pairs,),
        in_specs=[
            whole((t, d)),
            whole((t, d)),
            whole(wa.shape),
            whole(wb.shape),
            whole((t, c)),
            pl.BlockSpec((2 * DH, ENC), lambda i: (i % pairs, i // pairs)),
            tokhead,
            pl.BlockSpec((1, 2, ENC, LEN), lambda i: (i, 0, 0, 0)),
            pl.BlockSpec((1, 2, LEN), lambda i: (i, 0, 0)),
            whole((c, t)),
            whole((t, d)),
        ],
        out_specs=(tokhead, tokhead, whole((2 * w, d)), whole((2 * w, d)), whole((t, d))),
        scratch=[pltpu.VMEM((c, t), bf16), pltpu.VMEM((c, t), bf16)],
        flops=3 * (2 * t * d * c * 4 + 2 * t * ENC * c * 4 * 2),
        nbytes=18 * 1024 * 1024,
        trans=0,
        name="cross_bwd",
    )


def enc_grad_kernel(enc_ref, gk_ref, gv_ref, wa_ref, wb_ref, gin_ref, ga_ref, gb_ref, ge_ref, accs_ref):
    w = wa_ref.shape[0] // 4
    step = pl.program_id(0)

    def rows(i):
        return jnp.concatenate([wa_ref[i * w : (i + 1) * w], wb_ref[i * w : (i + 1) * w]], axis=0)

    gk = gk_ref[...]
    gv = gv_ref[...]
    enc = enc_ref[...]
    part = nn(gk, rows(1)) + nn(gv, rows(2))
    ge_ref[...] = part if gin_ref is None else gin_ref[...] + part
    tk = tn(gk, enc)
    tv = tn(gv, enc)

    @pl.when(step == 0)
    def _():
        accs_ref[0] = tk
        accs_ref[1] = tv

    @pl.when(step != 0)
    def _():
        accs_ref[0] += tk
        accs_ref[1] += tv

    @pl.when(step == pl.num_programs(0) - 1)
    def _():
        for i in range(2):
            ga_ref[i * w : (i + 1) * w] = accs_ref[i, 0:w].astype(bf16)
            gb_ref[i * w : (i + 1) * w] = accs_ref[i, w:].astype(bf16)


def enc_grad(enc, gk, gv, wa, wb, gin=None):
    te, d = enc.shape
    w = wa.shape[0] // 4
    c = 2 * w
    rows = 512
    blk = pl.BlockSpec((rows, d), lambda i: (i, 0))
    half = pl.BlockSpec((rows, c), lambda i: (i, 0))
    args = [enc, gk, gv, wa, wb]
    in_specs = [blk, half, half, whole(wa.shape), whole(wb.shape)]
    if gin is None:
        body = lambda a, b, c_, d_, e, *r: enc_grad_kernel(a, b, c_, d_, e, None, *r)
    else:
        body = enc_grad_kernel
        args.append(gin)
        in_specs.append(blk)
    return call(
        body,
        (
            jax.ShapeDtypeStruct((2 * w, d), bf16),
            jax.ShapeDtypeStruct((2 * w, d), bf16),
            jax.ShapeDtypeStruct((te, d), f32),
        ),
        args,
        grid=(te // rows,),
        in_specs=in_specs,
        out_specs=(whole((2 * w, d)), whole((2 * w, d)), blk),
        scratch=[pltpu.VMEM((2, c, d), f32)],
        flops=2 * te * d * c * 4 * 2,
        nbytes=te * d * 10,
        name="enc_grad",
    )


def self_bwd_kernel(last, x1_ref, gx2_ref, gn2_ref, g2_ref, n1_ref, wa_ref, wb_ref, q_ref, k_ref, vt_ref, e_ref, r_ref, at_ref, *rest):
    if last:
        gin_ref, x_ref, g1_ref, ga_ref, gb_ref, gd_ref, gg2_ref, gg1_ref, gi_ref, gat_ref, gqt_ref, gk_ref, gv_ref, gx1_ref = rest
    else:
        ga_ref, gb_ref, gd_ref, gn_ref, gat_ref, gqt_ref, gk_ref, gv_ref, gx1_ref = rest
    w = wa_ref.shape[0] // 4
    c = 2 * w
    nb = n1_ref.shape[0] // LEN

    def rows(i):
        return jnp.concatenate([wa_ref[i * w : (i + 1) * w], wb_ref[i * w : (i + 1) * w]], axis=0)

    gx, gg2 = norm_back(x1_ref[...], g2_ref[...].astype(f32), gn2_ref[...])
    gx1 = gx2_ref[...] + gx
    gx1_ref[...] = gx1
    go = gx1.astype(bf16)
    gat_ref[...] = nt(rows(3), go).astype(bf16)
    gwo = nn(at_ref[...], go).astype(bf16)
    ri = lax.broadcasted_iota(jnp.int32, (LEN, LEN), 0)
    ci = lax.broadcasted_iota(jnp.int32, (LEN, LEN), 1)
    flip = jnp.where(ri + ci == LEN - 1, 1.0, 0.0).astype(bf16)
    gd_ref[...] = jnp.zeros_like(gd_ref)
    for p in range(c // (2 * DH)):
        lanes = slice(p * 2 * DH, (p + 1) * 2 * DH)
        for b in range(nb):
            tok = slice(b * LEN, (b + 1) * LEN)

            def extra(h, gs):
                turned = pltpu.roll(nn(gs, flip), 0, 1, stride=1, stride_axis=0)
                head = 2 * p + h
                gd_ref[head : head + 1, :] += jnp.sum(turned, axis=0, keepdims=True)

            gq, gk, gv = head_pair_back(
                k_ref[tok, lanes].T, vt_ref[lanes, tok].T, q_ref[tok, lanes], None, gat_ref[lanes, tok], at_ref[lanes, tok],
                [e_ref[b, 2 * p], e_ref[b, 2 * p + 1]],
                [r_ref[b, 2 * p : 2 * p + 1, :], r_ref[b, 2 * p + 1 : 2 * p + 2, :]],
                extra,
            )
            gqt_ref[lanes, tok] = gq
            gk_ref[tok, lanes] = gk
            gv_ref[tok, lanes] = gv
    n1 = n1_ref[...]
    gqt = gqt_ref[...]
    gk = gk_ref[...]
    gv = gv_ref[...]
    gwq = nn(gqt, n1).astype(bf16)
    gwk = tn(gk, n1).astype(bf16)
    gwv = tn(gv, n1).astype(bf16)
    for i, gw in enumerate((gwq, gwk, gwv, gwo)):
        ga_ref[i * w : (i + 1) * w] = gw[0:w]
        gb_ref[i * w : (i + 1) * w] = gw[w:]
    gn = tn(gqt, rows(0)) + nn(gk, rows(1)) + nn(gv, rows(2))
    if last:
        gn = gin_ref[...] + gn
        gi, gg1 = norm_back(x_ref[...].astype(f32), g1_ref[...].astype(f32), gn)
        gi_ref[...] = gx1_ref[...] + gi
        gg1_ref[...] = gg1
        gg2_ref[...] = gg2
    else:
        gn_ref[...] = gn


def self_bwd(last, x1, gx2, gn2, g2, n1, wa, wb, q, k, vt, e, r, at, gin=None, x=None, g1=None):
    t, d = x1.shape
    w = wa.shape[0] // 4
    c = 2 * w
    nh = c // DH
    args = [x1, gx2, gn2, g2, n1, wa, wb, q, k, vt, e, r, at]
    outs = [
        jax.ShapeDtypeStruct((4 * w, d), bf16),
        jax.ShapeDtypeStruct((4 * w, d), bf16),
        jax.ShapeDtypeStruct((nh, LEN), f32),
    ]
    if last:
        args += [gin, x, g1]
        outs += [jax.ShapeDtypeStruct((1, d), f32), jax.ShapeDtypeStruct((1, d), f32), jax.ShapeDtypeStruct((t, d), f32)]
    else:
        outs += [jax.ShapeDtypeStruct((t, d), f32)]
    return call(
        lambda *r_: self_bwd_kernel(last, *r_),
        tuple(outs),
        args,
        in_specs=[whole(a.shape) for a in args],
        out_specs=tuple(whole(o.shape) for o in outs),
        scratch=[
            pltpu.VMEM((c, t), bf16),
            pltpu.VMEM((c, t), bf16),
            pltpu.VMEM((t, c), bf16),
            pltpu.VMEM((t, c), bf16),
            pltpu.VMEM((t, d), f32),
        ],
        flops=3 * (2 * t * d * c * 8 + 2 * t * LEN * c * 5 * 2),
        nbytes=14 * 1024 * 1024,
        name="self_bwd",
    )


def local_program(tensor_size, dp_size, *arrays):
    (block_in, enc_states, dec_len, enc_len, gain_self, self_query, self_key, self_value, self_out, rel_table,
     gain_cross, cross_query, cross_key, cross_value, cross_out, gain_ff, ff_in, ff_out, out_grad) = arrays
    t_index = lax.axis_index("tensor")
    d_index = lax.axis_index("dp")
    nb = block_in.shape[0] // LEN
    w, d = self_out.shape
    heads = w // DH

    def swap(v, axis, bit):
        n = tensor_size if axis == "tensor" else dp_size
        return lax.ppermute(v, axis, [(i, i ^ bit) for i in range(n)])

    def d_bit(bit):
        return (d_index // bit) % 2

    y = d_bit(1).astype(jnp.int32)
    y_is0 = y == 0
    y_arr = y.reshape(1)

    def across(send):
        h = swap(send, "tensor", 2)
        g = swap(h, "dp", 1)
        return h, g

    def joined(h, g):
        return jnp.where(y_is0, jnp.concatenate([h, g], axis=0), jnp.concatenate([g, h], axis=0))

    own_s, half_s = pack(y_arr, self_query, self_key, self_value, self_out)
    own_c, half_c = pack(y_arr, cross_query, cross_key, cross_value, cross_out)

    buckets = np.eye(BUCKETS, dtype=np.float32)[bucket_of_distance()]
    rel_own = jnp.dot(rel_table.astype(f32).T, jnp.asarray(buckets.T), precision=lax.Precision.HIGHEST)
    bias0 = jnp.concatenate([rel_own, swap(rel_own, "tensor", 1)], axis=0)
    bias1 = swap(bias0, "tensor", 2)

    w_s0, w_s1 = own_s, swap(own_s, "tensor", 1)
    w_c0, w_c1 = own_c, swap(own_c, "tensor", 1)
    h_s, g_s = across(half_s)
    half_c = lax.optimization_barrier((half_c, h_s))[0]
    h_c, g_c = across(half_c)
    wi0, wi1 = ff_in, swap(ff_in, "tensor", 1)
    wo0, wo1 = ff_out, swap(ff_out, "tensor", 1)
    send_f = jnp.where(y_is0, ff_in, ff_out)
    send_f = lax.optimization_barrier((send_f, h_c))[0]
    h_f, g_f = across(send_f)
    w_s2 = joined(h_s, g_s)
    w_s3 = swap(w_s2, "tensor", 1)
    w_c2 = joined(h_c, g_c)
    w_c3 = swap(w_c2, "tensor", 1)
    wi2 = jnp.where(y_is0, h_f, g_f)
    wo2 = jnp.where(y_is0, g_f, h_f)
    wi3 = swap(wi2, "tensor", 1)
    wo3 = swap(wo2, "tensor", 1)

    my_dec = lax.dynamic_slice(dec_len, (t_index * nb,), (nb,))
    my_enc = lax.dynamic_slice(enc_len, (t_index * nb,), (nb,))
    g1 = gain_self.reshape(1, d)
    g2 = gain_cross.reshape(1, d)
    g3 = gain_ff.reshape(1, d)
    sq0, sk0, sv0, se0, sr0, sa0, xp = self_fwd(False, my_dec, block_in, g1, g2, w_s0, w_s1, bias0)
    k0, kt0, v0, vt0 = enc_kv(enc_states, w_c0, w_c1)
    sq1, sk1, sv1, se1, sr1, sa1, x1, n1, n2 = self_fwd(True, my_dec, block_in, g1, g2, w_s2, w_s3, bias1, xp)
    cq0, ce0, cr0, ca0, x2p = cross_fwd(False, my_enc, n2, g3, w_c0, w_c1, k0, vt0, x1)
    k1, kt1, v1, vt1 = enc_kv(enc_states, w_c2, w_c3)
    cq1, ce1, cr1, ca1, x2, n3 = cross_fwd(True, my_enc, n2, g3, w_c2, w_c3, k1, vt1, x2p)

    gwi2, gwo2, gwi3, gwo3, yp, gp = ff(False, n3, out_grad, wi2, wo2, wi3, wo3)
    gwi0, gwo0, gwi1, gwo1, block_out, gx2, go2, gg3 = ff(True, n3, out_grad, wi0, wo0, wi1, wo1, yp, gp, x2, g3)

    def halves(v, bit):
        v = v.reshape((2, v.shape[0] // 2) + v.shape[1:])
        m = d_bit(bit)
        keep = lax.dynamic_index_in_dim(v, m, 0, keepdims=False)
        send = lax.dynamic_index_in_dim(v, 1 - m, 0, keepdims=False)
        return keep, send

    def plus(a, b):
        return (a.astype(f32) + b.astype(f32)).astype(bf16)

    def reduce_shards(s0, s1, s2, s3):
        s2 = plus(s2, swap(s3, "tensor", 1))
        s0 = plus(s0, swap(s1, "tensor", 1))
        v = plus(s0, swap(s2, "tensor", 2))
        bit = 1
        while bit < dp_size:
            keep, send = halves(v, bit)
            v = plus(keep, swap(send, "dp", bit))
            bit *= 2
        while bit > 1:
            bit //= 2
            got = swap(v, "dp", bit)
            low = d_bit(bit) == 0
            v = jnp.where(low, jnp.concatenate([v, got], axis=0), jnp.concatenate([got, v], axis=0))
        return v

    r_wo = reduce_shards(gwo0, gwo1, gwo2, gwo3)
    r_wi = reduce_shards(gwi0, gwi1, gwi2, gwi3)

    zero = jnp.zeros((nb * LEN, d), f32)
    gk1, gv1, gqo2, gqo3, gn2 = cross_bwd(go2, n2, w_c2, w_c3, cq1, kt1, v1, ce1, cr1, ca1, zero)
    gk0, gv0, gqo0, gqo1, gn2 = cross_bwd(go2, n2, w_c0, w_c1, cq0, kt0, v0, ce0, cr0, ca0, gn2)
    r_qo = reduce_shards(gqo0, gqo1, gqo2, gqo3)
    gkv2, gkv3, gep = enc_grad(enc_states, gk1, gv1, w_c2, w_c3)
    gkv0, gkv1, grad_enc = enc_grad(enc_states, gk0, gv0, w_c0, w_c1, gep)
    r_kv = reduce_shards(gkv0, gkv1, gkv2, gkv3)

    gs2, gs3, gd1, gnp = self_bwd(False, x1, gx2, gn2, g2, n1, w_s2, w_s3, sq1, sk1, sv1, se1, sr1, sa1)
    gs0, gs1, gd0, gg2, gg1, grad_in = self_bwd(True, x1, gx2, gn2, g2, n1, w_s0, w_s1, sq0, sk0, sv0, se0, sr0, sa0, gnp, block_in, g1)
    r_s = reduce_shards(gs0, gs1, gs2, gs3)

    flipped = jnp.asarray(np.ascontiguousarray(buckets[::-1]))
    gd = jnp.concatenate([gd0, gd1], axis=0)
    grel = jnp.dot(gd, flipped, precision=lax.Precision.HIGHEST)
    grel = grel.reshape(tensor_size, heads * BUCKETS)
    slots = jnp.arange(tensor_size)[:, None] ^ t_index
    order = (slots == jnp.arange(tensor_size)[None, :]).astype(f32)
    grel = jnp.dot(order.T, grel, precision=lax.Precision.HIGHEST)
    grel = jnp.pad(grel.reshape(1, -1), ((0, 0), (0, d - grel.size)))
    small = jnp.concatenate([gg1, gg2, gg3, grel], axis=0)
    small = lax.psum(small, ("dp", "tensor"))
    grad_rel = lax.dynamic_slice(small[3], (t_index * heads * BUCKETS,), (heads * BUCKETS,)).reshape(heads, BUCKETS).T

    def part(v, i):
        return v[i * w : (i + 1) * w].astype(f32)

    return (
        block_out,
        grad_in,
        grad_enc,
        small[0],
        part(r_s, 0).T,
        part(r_s, 1).T,
        part(r_s, 2).T,
        part(r_s, 3),
        grad_rel,
        small[1],
        part(r_qo, 0).T,
        part(r_kv, 0).T,
        part(r_kv, 1).T,
        part(r_qo, 1),
        small[2],
        r_wi.astype(f32),
        r_wo.astype(f32),
    )


def solution(mesh):
    tensor_size = mesh.shape["tensor"]
    dp_size = mesh.shape["dp"]
    both = P(("dp", "tensor"), None)
    col = P(None, "tensor")
    row = P("tensor", None)
    placed = (both, both, P("dp"), P("dp"), P(), col, col, col, row, col, P(), col, col, col, row, P(), col, row, both)
    outs = (both, both, both, P(), col, col, col, row, col, P(), col, col, col, row, P(), col, row)
    return jax.shard_map(
        lambda *a: local_program(tensor_size, dp_size, *a),
        mesh=mesh,
        in_specs=placed,
        out_specs=outs,
        check_vma=False,
    )
```

time: 1170 us -> 545 us (0.47)
  waiting for transfers between devices: 700 us -> 215 us
  matrix products: 240 us -> 2.57 us
  Pallas kernels: 0 us -> 181 us
  other arithmetic: 92.2 us -> 24.8 us
  starting transfers between devices: 1.37 us -> 47.9 us
  local copies, waits for them, and re-layouts: 48.2 us -> 18.2 us
  between operations: 15.3 us -> 1.64 us
  blocking collectives: 62.1 us -> 49.5 us
    reduce_scatter x7 -> x0, waiting for transfers between devices: 407 us -> none  [the longest x6 321 us: spread_rows(): return lax.psum_scatter(values, 'tensor', scatter_dimension=0, tiled=True)]
    dot_general x44 -> x3, matrix products: 240 us -> 2.57 us  [the longest x1 1.51 us: local_program(): grel = jnp.dot(order.T, grel, precision=lax.Precision.HIGHEST)]
    ppermute x0 -> x61, waiting for transfers between devices: none -> 215 us  [swap(): return lax.ppermute(v, axis, [(i, i ^ bit) for i in range(n)])]
    all_gather x7 -> x0, waiting for transfers between devices: 183 us -> none  [the longest x6 103 us: collect_rows(): return lax.all_gather(values, 'tensor', axis=0, tiled=True)]
    pallas_call x0 -> x16, Pallas kernels: none -> 181 us  [call(): pl.pallas_call(kernel, out_shape=out_shape, grid=grid, scratch_shapes=scr...]
    psum x1 -> x0, waiting for transfers between devices: 109 us -> none  [local(): lax.psum(grad_self_query.astype(jnp.bfloat16), 'dp').astype(jnp.float32)]
    ppermute x0 -> x61, starting transfers between devices: none -> 47.9 us  [swap(): return lax.ppermute(v, axis, [(i, i ^ bit) for i in range(n)])]
    convert_element_type x21 -> x29, other arithmetic: 55 us -> 13.3 us  [the longest x25 7.53 us: plus(): return (a.astype(f32) + b.astype(f32)).astype(bf16)]
  transfers between devices with their start and end apart: 15 -> 61, of which waited for: 14 -> 31; matrix products, arithmetic and copies ran while one was open for 15% -> 7% of each run, Pallas kernels for 0% -> 33%
where the time goes in v1:
time: 545 us; the launch traced here: 541 us
  waiting for transfers between devices  215 us (39%)
  Pallas kernels  181 us (33%)
  blocking collectives  49.5 us (9%)
  starting transfers between devices  47.9 us (9%)
  other arithmetic  24.8 us (5%)
  local copies, waits for them, and re-layouts  18.2 us (3%)
    ppermute x61, waiting for transfers between devices, swap(): return lax.ppermute(v, axis, [(i, i ^ bit) for i in range(n)])  215 us
    pallas_call x16, Pallas kernels, call(): pl.pallas_call(kernel, out_shape=out_shape, grid=grid, scratch_shapes=scr...  181 us
    psum x1, blocking collectives, local_program(): small = lax.psum(small, ('dp', 'tensor'))  49.5 us
    ppermute x61, starting transfers between devices, swap(): return lax.ppermute(v, axis, [(i, i ^ bit) for i in range(n)])  47.9 us
  transfers between devices with their start and end apart: 61, of which 31 were waited for; matrix products, arithmetic and copies ran while one was open for 7% of the time, Pallas kernels for 33%

profile of v1, /device:TPU:0, one launch (start us, length us, event | category | flops | bytes accessed | tf_op | source)
XLA Modules:
  0.0 540.8 jit_solution(901168779530954198)
XLA Ops:
  17.0 7.9 %collective-permute-done = bf16[384,768]{1,0:T(8,128)(2,1)S(1)} collective-permute-done((bf16[384,768]{1,0:T(8,128)(2,1)}, bf16[384,768]{1,0:T(8,128)(2,1)S(1)}, u32[]{:S(2)}, u32[]{:S(2)}) %collective-permute-start) | collective-permute-done | bytes 589856 | tf_op jit(solution)/shard_map/ppermute | solution.py:710
  28.1 11.5 %collective-permute-done.6 = bf16[384,768]{1,0:T(8,128)(2,1)S(1)} collective-permute-done((bf16[384,768]{1,0:T(8,128)(2,1)}, bf16[384,768]{1,0:T(8,128)(2,1)S(1)}, u32[]{:S(2)}, u32[]{:S(2)}) %collective-permute-start.6) | collective-permute-done | bytes 589856 | tf_op jit(solution)/shard_map/ppermute | solution.py:710
  43.2 10.9 %collective-permute-done.1 = bf16[384,768]{1,0:T(8,128)(2,1)} collective-permute-done((bf16[384,768]{1,0:T(8,128)(2,1)S(1)}, bf16[384,768]{1,0:T(8,128)(2,1)}, u32[]{:S(2)}, u32[]{:S(2)}) %collective-permute-start.1) | collective-permute-done | bytes 589856 | tf_op jit(solution)/shard_map/ppermute | solution.py:710
  67.0 7.4 %enc_kv.3 = (bf16[2048,384]{1,0:T(8,128)(2,1)}, bf16[384,2048]{1,0:T(8,128)(2,1)}, bf16[2048,384]{1,0:T(8,128)(2,1)}, bf16[384,2048]{1,0:T(8,128)(2,1)}) custom-call(bf16[2048,768]{1,0:T(8,128)(2,1)} %enc_ref.5, bf16[768,768]{1,0:T(8,128)(2,1)} %get-tuple-element.106.wa_ref.r_3_.r__2_, bf16[768,768]{1,0:T(8,128)(2,1)} %collective-permute-done.9.wb_ref.r_4_.r__3_), custom_call_target="tpu_custom_call" | custom-call | flops 4831838208 | bytes 9437184 | tf_op jit(solution)/shard_map/enc_kv/pallas_call | solution.py:76
  74.5 8.4 %self_fwd.2 = (bf16[512,384]{1,0:T(8,128)(2,1)}, bf16[512,384]{1,0:T(8,128)(2,1)}, bf16[384,512]{1,0:T(8,128)(2,1)}, bf16[2,6,256,256]{3,2,1,0:T(8,128)(2,1)}, f...) custom-call(s32[2]{0:T(128)} %dynamic_slice.104.r_0_, bf16[512,768]{1,0:T(8,128)(2,1)} %r__14_.1, ...), custom_call_target="tpu_custom_call" | custom-call | flops 4831838208 | bytes 12582912 | tf_op jit(solution)/shard_map/self_fwd/pallas_call | solution.py:76
  88.0 9.5 %self_fwd.3 = (bf16[512,384]{1,0:T(8,128)(2,1)}, bf16[512,384]{1,0:T(8,128)(2,1)}, bf16[384,512]{1,0:T(8,128)(2,1)}, bf16[2,6,256,256]{3,2,1,0:T(8,128)(2,1)}, f...) custom-call(s32[2]{0:T(128)} %dynamic_slice.104.r_0_, ...), custom_call_target="tpu_custom_call" | custom-call | flops 4831838208 | bytes 12582912 | tf_op jit(solution)/shard_map/self_fwd/pallas_call | solution.py:76
  97.5 6.0 %collective-permute-done.13 = bf16[768,768]{1,0:T(8,128)(2,1)S(1)} collective-permute-done((bf16[768,768]{1,0:T(8,128)(2,1)S(1)}, bf16[768,768]{1,0:T(8,128)(2,1)S(1)}, u32[]{:S(2)}, u32[]{:S(2)}) %collective-permute-start.13) | collective-permute-done | bytes 1179680 | tf_op jit(solution)/shard_map/ppermute | solution.py:710
  105.2 16.2 %cross_fwd.2 = (bf16[512,384]{1,0:T(8,128)(2,1)}, bf16[6,2,1024,256]{3,2,1,0:T(8,128)(2,1)}, f32[6,2,256]{2,1,0:T(2,128)}, bf16[384,512]{1,0:T(8,128)(2,1)}, f32[512,768]{1,0:T(8,128)}) custom-call(s32[2]{0:T(128)} %dynamic_slice.103.r_0_, bf16[512,768]{1,0:T(8,128)(2,1)} %get-tuple-element.101.r_1_.r__1_, bf16[1,768]{1,0:T(2,128)(2,1)} %reshape.140.r_2_.r_9_, ...), custom_call_target="tpu_custom_call" | custom-call | flops 6643777536 | bytes 14680064 | tf_op jit(solution)/shard_map/cross_fwd/pallas_call | solution.py:76
  121.4 7.5 %enc_kv.2 = (bf16[2048,384]{1,0:T(8,128)(2,1)}, bf16[384,2048]{1,0:T(8,128)(2,1)}, bf16[2048,384]{1,0:T(8,128)(2,1)}, bf16[384,2048]{1,0:T(8,128)(2,1)}) custom-call(bf16[2048,768]{1,0:T(8,128)(2,1)} %enc_ref.5, bf16[768,768]{1,0:T(8,128)(2,1)} %maximum_select_fusion.1.wa_ref.r_3_.r__2_.d_, bf16[768,768]{1,0:T(8,128)(2,1)} %collective-permute-done.8.wb_ref.r_4_.r__3_.e), custom_call_target="tpu_custom_call" | custom-call | flops 4831838208 | bytes 9437184 | tf_op jit(solution)/shard_map/enc_kv/pallas_call | solution.py:76
  128.9 16.6 %cross_fwd.3 = (bf16[512,384]{1,0:T(8,128)(2,1)}, bf16[6,2,1024,256]{3,2,1,0:T(8,128)(2,1)}, f32[6,2,256]{2,1,0:T(2,128)}, bf16[384,512]{1,0:T(8,128)(2,1)}, f32...) custom-call(s32[2]{0:T(128)} %dynamic_slice.103.r_0_, bf16[512,768]{1,0:T(8,128)(2,1)} %get-tuple-element.101.r_1_.r__1_, ...), custom_call_target="tpu_custom_call" | custom-call | flops 6643777536 | bytes 14680064 | tf_op jit(solution)/shard_map/cross_fwd/pallas_call | solution.py:76
  146.9 13.2 %ff.2 = (bf16[768,768]{1,0:T(8,128)(2,1)}, bf16[768,768]{1,0:T(8,128)(2,1)}, bf16[768,768]{1,0:T(8,128)(2,1)}, bf16[768,768]{1,0:T(8,128)(2,1)}, f32[512,768]{1,0:T(8,128)}, /*index=5*/f32[512,768]{1,0:T(8,128)}) custom-call(bf16[512,768]{1,0:T(8,128)(2,1)} %get-tuple-element.111.r_0_, bf16[512,768]{1,0:T(8,128)(2,1)} %r_1_.7, ...), custom_call_target="tpu_custom_call" | custom-call | flops 14495514624 | bytes 12582912 | tf_op jit(solution)/shard_map/ff/pallas_call | solution.py:76
  160.3 16.3 %ff.3 = (bf16[768,768]{1,0:T(8,128)(2,1)}, bf16[768,768]{1,0:T(8,128)(2,1)}, bf16[768,768]{1,0:T(8,128)(2,1)}, bf16[768,768]{1,0:T(8,128)(2,1)}, bf16[512,768]{1...) custom-call(bf16[512,768]{1,0:T(8,128)(2,1)} %get-tuple-element.111.r_0_, ...), custom_call_target="tpu_custom_call" | custom-call | flops 14495514624 | bytes 12582912 | tf_op jit(solution)/shard_map/ff/pallas_call | solution.py:76
  177.8 16.1 %cross_bwd.2 = (bf16[2048,384]{1,0:T(8,128)(2,1)}, bf16[2048,384]{1,0:T(8,128)(2,1)}, bf16[384,768]{1,0:T(8,128)(2,1)}, bf16[384,768]{1,0:T(8,128)(2,1)}, f32[512,768]{1,0:T(8,128)}) custom-call(bf16[512,768]{1,0:T(8,128)(2,1)} %get-tuple-element.118.r__0_, bf16[512,768]{1,0:T(8,128)(2,1)} %get-tuple-element.101.r_1_.r__1_, ...), custom_call_target="tpu_custom_call" | custom-call | flops 13287555072 | bytes 18874368 | tf_op jit(solution)/shard_map/cross_bwd/pallas_call | solution.py:76
  193.9 11.3 %enc_grad.2 = (bf16[384,768]{1,0:T(8,128)(2,1)}, bf16[384,768]{1,0:T(8,128)(2,1)}, f32[2048,768]{1,0:T(8,128)}) custom-call(bf16[2048,768]{1,0:T(8,128)(2,1)} %enc_ref.5, bf16[2048,384]{1,0:T(8,128)(2,1)} %get-tuple-element.150.b, bf16[2048,384]{1,0:T(8,128)(2,1)} %get-tuple-element.151.c_, bf16[768,768]{1,0:T(8,128)(2,1)} %maximum_select_fusion.1.wa_ref.r_3_.r__2_.d_, ...), custom_call_target="tpu_custom_call" | custom-call | flops 9663676416 | bytes 15728640 | tf_op jit(solution)/shard_map/enc_grad/pallas_call | solution.py:76
  205.6 15.6 %cross_bwd.3 = (bf16[2048,384]{1,0:T(8,128)(2,1)}, bf16[2048,384]{1,0:T(8,128)(2,1)}, bf16[384,768]{1,0:T(8,128)(2,1)}, bf16[384,768]{1,0:T(8,128)(2,1)}, f32[512,768]{1,0:T(8,128)}) custom-call(bf16[512,768]{1,0:T(8,128)(2,1)} %get-tuple-element.118.r__0_, bf16[512,768]{1,0:T(8,128)(2,1)} %get-tuple-element.101.r_1_.r__1_, ...), custom_call_target="tpu_custom_call" | custom-call | flops 13287555072 | bytes 18874368 | tf_op jit(solution)/shard_map/cross_bwd/pallas_call | solution.py:76
  221.3 12.5 %enc_grad.3 = (bf16[384,768]{1,0:T(8,128)(2,1)}, bf16[384,768]{1,0:T(8,128)(2,1)}, f32[2048,768]{1,0:T(8,128)}) custom-call(bf16[2048,768]{1,0:T(8,128)(2,1)} %enc_ref.5, bf16[2048,384]{1,0:T(8,128)(2,1)} %get-tuple-element.148.gk_ref, bf16[2048,384]{1,0:T(8,128)(2,1)} %get-tuple-element.149.gv_ref, bf16[768,768]{1,0:T(8,128)(2,1)} %get-tuple-element.106.wa_ref.r_3_.r__2_, ...), custom_call_target="tpu_custom_call" | custom-call | flops 9663676416 | bytes 15728640 | tf_op jit(solution)/shard_map/enc_grad/pallas_call | solution.py:76
  234.5 11.5 %self_bwd.2 = (bf16[768,768]{1,0:T(8,128)(2,1)}, bf16[768,768]{1,0:T(8,128)(2,1)}, f32[6,256]{1,0:T(8,128)}, f32[512,768]{1,0:T(8,128)}) custom-call(f32[512,768]{1,0:T(8,128)} %get-tuple-element.109.r_7_.r__0_, f32[512,768]{1,0:T(8,128)} %get-tuple-element.117.r__1_, f32[512,768]{1,0:T(8,128)} %get-tuple-element.132.r__2_, ...), custom_call_target="tpu_custom_call" | custom-call | flops 10267656192 | bytes 14680064 | tf_op jit(solution)/shard_map/self_bwd/pallas_call | solution.py:76
  246.0 13.1 %self_bwd.3 = (bf16[768,768]{1,0:T(8,128)(2,1)}, bf16[768,768]{1,0:T(8,128)(2,1)}, f32[6,256]{1,0:T(8,128)}, f32[1,768]{1,0:T(1,128)}, f32[1,768]{1,0:T(1,128)}, /*index=5*/f32[512,768]{1,0:T(8,128)}) custom-call(f32[512,768]{1,0:T(8,128)} %get-tuple-element.109.r_7_.r__0_, f32[512,768]{1,0:T(8,128)} %get-tuple-element.117.r__1_, ...), custom_call_target="tpu_custom_call" | custom-call | flops 10267656192 | bytes 14680064 | tf_op jit(solution)/shard_map/self_bwd/pallas_call | solution.py:76
  264.3 49.5 %psum.7 = f32[4,768]{1,0:T(4,128)S(1)} all-reduce(f32[4,768]{1,0:T(4,128)S(1)} %select_maximum_fusion), channel_id=1, replica_groups=mesh['dp'=8,'tensor'=4] {'dp','tensor'}, use_global_device_ids=true, to_apply=%region_0.1 | all-reduce | flops 3072 | bytes 24576 | tf_op jit(solution)/shard_map/psum | solution.py:819
  319.9 8.3 %collective-permute-done.27 = bf16[384,768]{1,0:T(8,128)(2,1)S(1)} collective-permute-done((bf16[384,768]{1,0:T(8,128)(2,1)S(1)}, bf16[384,768]{1,0:T(8,128)(2,1)S(1)}, u32[]{:S(2)}, u32[]{:S(2)}) %collective-permute-start.27) | collective-permute-done | bytes 589856 | tf_op jit(solution)/shard_map/ppermute | solution.py:710
  332.1 6.1 %collective-permute-done.37 = bf16[192,768]{1,0:T(8,128)(2,1)S(1)} collective-permute-done((bf16[192,768]{1,0:T(8,128)(2,1)S(1)}, bf16[192,768]{1,0:T(8,128)(2,1)S(1)}, u32[]{:S(2)}, u32[]{:S(2)}) %collective-permute-start.37) | collective-permute-done | bytes 294944 | tf_op jit(solution)/shard_map/ppermute | solution.py:710
  359.6 6.4 %collective-permute-done.30 = bf16[48,768]{1,0:T(8,128)(2,1)S(1)} collective-permute-done((bf16[48,768]{1,0:T(8,128)(2,1)S(1)}, bf16[48,768]{1,0:T(8,128)(2,1)S(1)}, u32[]{:S(2)}, u32[]{:S(2)}) %collective-permute-start.30) | collective-permute-done | bytes 73760 | tf_op jit(solution)/shard_map/ppermute | solution.py:710
  391.0 15.7 %collective-permute-done.45 = bf16[768,768]{1,0:T(8,128)(2,1)S(1)} collective-permute-done((bf16[768,768]{1,0:T(8,128)(2,1)S(1)}, bf16[768,768]{1,0:T(8,128)(2,1)S(1)}, u32[]{:S(2)}, u32[]{:S(2)}) %collective-permute-start.45) | collective-permute-done | bytes 1179680 | tf_op jit(solution)/shard_map/ppermute | solution.py:710
  408.2 22.0 %collective-permute-done.18 = bf16[768,768]{1,0:T(8,128)(2,1)S(1)} collective-permute-done((bf16[768,768]{1,0:T(8,128)(2,1)S(1)}, bf16[768,768]{1,0:T(8,128)(2,1)S(1)}, u32[]{:S(2)}, u32[]{:S(2)}) %collective-permute-start.18) | collective-permute-done | bytes 1179680 | tf_op jit(solution)/shard_map/ppermute | solution.py:710
  434.6 9.9 %collective-permute-done.19 = bf16[384,768]{1,0:T(8,128)(2,1)S(1)} collective-permute-done((bf16[384,768]{1,0:T(8,128)(2,1)S(1)}, bf16[384,768]{1,0:T(8,128)(2,1)S(1)}, u32[]{:S(2)}, u32[]{:S(2)}) %collective-permute-start.19) | collective-permute-done | bytes 589856 | tf_op jit(solution)/shard_map/ppermute | solution.py:710
  448.8 9.1 %collective-permute-done.20 = bf16[192,768]{1,0:T(8,128)(2,1)S(1)} collective-permute-done((bf16[192,768]{1,0:T(8,128)(2,1)S(1)}, bf16[192,768]{1,0:T(8,128)(2,1)S(1)}, u32[]{:S(2)}, u32[]{:S(2)}) %collective-permute-start.20) | collective-permute-done | bytes 294944 | tf_op jit(solution)/shard_map/ppermute | solution.py:710
  461.1 8.7 %collective-permute-done.21 = bf16[96,768]{1,0:T(8,128)(2,1)S(1)} collective-permute-done((bf16[96,768]{1,0:T(8,128)(2,1)S(1)}, bf16[96,768]{1,0:T(8,128)(2,1)S(1)}, u32[]{:S(2)}, u32[]{:S(2)}) %collective-permute-start.21) | collective-permute-done | bytes 147488 | tf_op jit(solution)/shard_map/ppermute | solution.py:710
  473.0 6.3 %collective-permute-done.58 = bf16[96,768]{1,0:T(8,128)(2,1)S(1)} collective-permute-done((bf16[96,768]{1,0:T(8,128)(2,1)S(1)}, bf16[96,768]{1,0:T(8,128)(2,1)S(1)}, u32[]{:S(2)}, u32[]{:S(2)}) %collective-permute-start.58) | collective-permute-done | bytes 147488 | tf_op jit(solution)/shard_map/ppermute | solution.py:710
  485.9 12.4 %collective-permute-done.23 = bf16[192,768]{1,0:T(8,128)(2,1)S(1)} collective-permute-done((bf16[192,768]{1,0:T(8,128)(2,1)S(1)}, bf16[192,768]{1,0:T(8,128)(2,1)S(1)}, u32[]{:S(2)}, u32[]{:S(2)}) %collective-permute-start.23) | collective-permute-done | bytes 294944 | tf_op jit(solution)/shard_map/ppermute | solution.py:710
  504.8 10.0 %collective-permute-done.24 = bf16[384,768]{1,0:T(8,128)(2,1)S(1)} collective-permute-done((bf16[384,768]{1,0:T(8,128)(2,1)S(1)}, bf16[384,768]{1,0:T(8,128)(2,1)S(1)}, u32[]{:S(2)}, u32[]{:S(2)}) %collective-permute-start.24) | collective-permute-done | bytes 589856 | tf_op jit(solution)/shard_map/ppermute | solution.py:710
  515.2 12.2 %collective-permute-done.60 = bf16[384,768]{1,0:T(8,128)(2,1)S(1)} collective-permute-done((bf16[384,768]{1,0:T(8,128)(2,1)S(1)}, bf16[384,768]{1,0:T(8,128)(2,1)S(1)}, u32[]{:S(2)}, u32[]{:S(2)}) %collective-permute-start.60) | collective-permute-done | bytes 589856 | tf_op jit(solution)/shard_map/ppermute | solution.py:710
  530.5 8.5 %collective-permute-done.51 = bf16[384,768]{1,0:T(8,128)(2,1)S(1)} collective-permute-done((bf16[384,768]{1,0:T(8,128)(2,1)S(1)}, bf16[384,768]{1,0:T(8,128)(2,1)S(1)}, u32[]{:S(2)}, u32[]{:S(2)}) %collective-permute-start.51) | collective-permute-done | bytes 589856 | tf_op jit(solution)/shard_map/ppermute | solution.py:710
  (264 shorter events, 142.7 us)
Async XLA Ops:
  26.6 36.1 %collective-permute-start.9 = (bf16[768,768]{1,0:T(8,128)(2,1)}, bf16[768,768]{1,0:T(8,128)(2,1)}, u32[]{:S(2)}, u32[]{:S(2)}) collective-permute-start(bf16[768,768]{1,0:T(8,128)(2,1)} %get-tuple-element.106.wa_ref.r_3_.r__2_), channel_id=1, source_target_pairs={{0,1},{1,0},{2,3},{3,2},{4,5},{5,4},{6,7},{7,6},{8,9},{9,8},{10,11... | collective-permute-start | bytes 3538952 | tf_op jit(solution)/shard_map/ppermute | solution.py:710
  39.6 26.2 %collective-permute-start.12 = (bf16[768,768]{1,0:T(8,128)(2,1)S(1)}, bf16[768,768]{1,0:T(8,128)(2,1)S(1)}, u32[]{:S(2)}, u32[]{:S(2)}) collective-permute-start(bf16[768,768]{1,0:T(8,128)(2,1)S(1)} %broadcast_select_fusion.2), channel_id=1, source_target_pairs={{0,2},{1,3},{2,0},{3,1},{4,6},{5,7},{6,4},{7,5},{8,10},{9,11},{10,... | collective-permute-start | bytes 3538952 | tf_op jit(solution)/shard_map/ppermute | solution.py:710
  42.6 31.9 %collective-permute-start.5 = (bf16[768,768]{1,0:T(8,128)(2,1)}, bf16[768,768]{1,0:T(8,128)(2,1)}, u32[]{:S(2)}, u32[]{:S(2)}) collective-permute-start(bf16[768,768]{1,0:T(8,128)(2,1)} %get-tuple-element.99.r_4_.r__5_), channel_id=1, source_target_pairs={{0,1},{1,0},{2,3},{3,2},{4,5},{5,4},{6,7},{7,6},{8,9},{9,8},{10,11... | collective-permute-start | bytes 3538952 | tf_op jit(solution)/shard_map/ppermute | solution.py:710
  56.0 31.6 %collective-permute-start.2 = (bf16[768,768]{1,0:T(8,128)(2,1)S(1)}, bf16[768,768]{1,0:T(8,128)(2,1)}, u32[]{:S(2)}, u32[]{:S(2)}) collective-permute-start(bf16[768,768]{1,0:T(8,128)(2,1)S(1)} %maximum_select_fusion.r_4_.r__5_), channel_id=1, source_target_pairs={{0,1},{1,0},{2,3},{3,2},{4,5},{5,4},{6,7},{7,6},{8,9},{9,8},{10,11... | collective-permute-start | bytes 3538952 | tf_op jit(solution)/shard_map/ppermute | solution.py:710
  61.6 98.6 %collective-permute-start.10 = (bf16[768,768]{1,0:T(8,128)(2,1)}, bf16[768,768]{1,0:T(8,128)(2,1)}, u32[]{:S(2)}, u32[]{:S(2)}) collective-permute-start(bf16[768,768]{1,0:T(8,128)(2,1)} %r_2_.1), channel_id=1, source_target_pairs={{0,1},{1,0},{2,3},{3,2},{4,5},{5,4},{6,7},{7,6},{8,9},{9,8},{10,11... | collective-permute-start | bytes 3538952 | tf_op jit(solution)/shard_map/ppermute | solution.py:710
  62.7 20.3 %collective-permute-start.7 = (bf16[384,768]{1,0:T(8,128)(2,1)}, bf16[384,768]{1,0:T(8,128)(2,1)}, u32[]{:S(2)}, u32[]{:S(2)}) collective-permute-start(bf16[384,768]{1,0:T(8,128)(2,1)} %copy-done.11), channel_id=1, source_target_pairs={{0,4},{4,0},{8,12},{12,8},{16,20},{20,16},{24,28},{28,24},{1,5},{5... | collective-permute-start | bytes 1769480 | tf_op jit(solution)/shard_map/ppermute | solution.py:710
  65.8 37.7 %collective-permute-start.13 = (bf16[768,768]{1,0:T(8,128)(2,1)S(1)}, bf16[768,768]{1,0:T(8,128)(2,1)S(1)}, u32[]{:S(2)}, u32[]{:S(2)}) collective-permute-start(bf16[768,768]{1,0:T(8,128)(2,1)S(1)} %collective-permute-done.12), channel_id=1, source_target_pairs={{0,4},{4,0},{8,12},{12,8},{16,20},{20,16},{24,28},{28,24},{1,5},{5... | collective-permute-start | bytes 3538952 | tf_op jit(solution)/shard_map/ppermute | solution.py:710
  74.4 85.8 %collective-permute-start.11 = (bf16[768,768]{1,0:T(8,128)(2,1)}, bf16[768,768]{1,0:T(8,128)(2,1)}, u32[]{:S(2)}, u32[]{:S(2)}) collective-permute-start(bf16[768,768]{1,0:T(8,128)(2,1)} %r_3_.1), channel_id=1, source_target_pairs={{0,1},{1,0},{2,3},{3,2},{4,5},{5,4},{6,7},{7,6},{8,9},{9,8},{10,11... | collective-permute-start | bytes 3538952 | tf_op jit(solution)/shard_map/ppermute | solution.py:710
  87.4 34.0 %collective-permute-start.8 = (bf16[768,768]{1,0:T(8,128)(2,1)}, bf16[768,768]{1,0:T(8,128)(2,1)}, u32[]{:S(2)}, u32[]{:S(2)}) collective-permute-start(bf16[768,768]{1,0:T(8,128)(2,1)} %maximum_select_fusion.1.wa_ref.r_3_.r__2_.d_), channel_id=1, source_target_pairs={{0,1},{1,0},{2,3},{3,2},{4,5},{5,4},{6,7},{7,6},{8,9},{9,8},{10,11... | collective-permute-start | bytes 3538952 | tf_op jit(solution)/shard_map/ppermute | solution.py:710
  104.7 40.9 %collective-permute-start.14 = (bf16[768,768]{1,0:T(8,128)(2,1)}, bf16[768,768]{1,0:T(8,128)(2,1)S(1)}, u32[]{:S(2)}, u32[]{:S(2)}) collective-permute-start(bf16[768,768]{1,0:T(8,128)(2,1)} %get-tuple-element.183.r_2_), channel_id=1, source_target_pairs={{0,1},{1,0},{2,3},{3,2},{4,5},{5,4},{6,7},{7,6},{8,9},{9,8},{10,11... | collective-permute-start | bytes 3538952 | tf_op jit(solution)/shard_map/ppermute | solution.py:710
  104.7 40.9 %collective-permute-start.15 = (bf16[768,768]{1,0:T(8,128)(2,1)S(1)}, bf16[768,768]{1,0:T(8,128)(2,1)S(1)}, u32[]{:S(2)}, u32[]{:S(2)}) collective-permute-start(bf16[768,768]{1,0:T(8,128)(2,1)S(1)} %get-tuple-element.182.r_3_), channel_id=1, source_target_pairs={{0,1},{1,0},{2,3},{3,2},{4,5},{5,4},{6,7},{7,6},{8,9},{9,8},{10,11... | collective-permute-start | bytes 3538952 | tf_op jit(solution)/shard_map/ppermute | solution.py:710
  160.2 170.8 %collective-permute-start.53 = (bf16[768,768]{1,0:T(8,128)(2,1)}, bf16[768,768]{1,0:T(8,128)(2,1)S(1)}, u32[]{:S(2)}, u32[]{:S(2)}) collective-permute-start(bf16[768,768]{1,0:T(8,128)(2,1)} %get-tuple-element.178), channel_id=1, source_target_pairs={{0,1},{1,0},{2,3},{3,2},{4,5},{5,4},{6,7},{7,6},{8,9},{9,8},{10,11... | collective-permute-start | bytes 3538952 | tf_op jit(solution)/shard_map/ppermute | solution.py:710
  205.2 57.2 %collective-permute-start.35 = (bf16[384,768]{1,0:T(8,128)(2,1)}, bf16[384,768]{1,0:T(8,128)(2,1)S(1)}, u32[]{:S(2)}, u32[]{:S(2)}) collective-permute-start(bf16[384,768]{1,0:T(8,128)(2,1)} %get-tuple-element.170), channel_id=1, source_target_pairs={{0,1},{1,0},{2,3},{3,2},{4,5},{5,4},{6,7},{7,6},{8,9},{9,8},{10,11... | collective-permute-start | bytes 1769480 | tf_op jit(solution)/shard_map/ppermute | solution.py:710
  233.8 83.8 %collective-permute-start.34 = (bf16[384,768]{1,0:T(8,128)(2,1)}, bf16[384,768]{1,0:T(8,128)(2,1)}, u32[]{:S(2)}, u32[]{:S(2)}) collective-permute-start(bf16[384,768]{1,0:T(8,128)(2,1)} %get-tuple-element.168), channel_id=1, source_target_pairs={{0,1},{1,0},{2,3},{3,2},{4,5},{5,4},{6,7},{7,6},{8,9},{9,8},{10,11... | collective-permute-start | bytes 1769480 | tf_op jit(solution)/shard_map/ppermute | solution.py:710
  233.9 79.9 %collective-permute-start.26 = (bf16[384,768]{1,0:T(8,128)(2,1)}, bf16[384,768]{1,0:T(8,128)(2,1)S(1)}, u32[]{:S(2)}, u32[]{:S(2)}) collective-permute-start(bf16[384,768]{1,0:T(8,128)(2,1)} %get-tuple-element.166), channel_id=1, source_target_pairs={{0,1},{1,0},{2,3},{3,2},{4,5},{5,4},{6,7},{7,6},{8,9},{9,8},{10,11... | collective-permute-start | bytes 1769480 | tf_op jit(solution)/shard_map/ppermute | solution.py:710
  234.4 85.4 %collective-permute-start.25 = (bf16[384,768]{1,0:T(8,128)(2,1)}, bf16[384,768]{1,0:T(8,128)(2,1)}, u32[]{:S(2)}, u32[]{:S(2)}) collective-permute-start(bf16[384,768]{1,0:T(8,128)(2,1)} %get-tuple-element.164), channel_id=1, source_target_pairs={{0,1},{1,0},{2,3},{3,2},{4,5},{5,4},{6,7},{7,6},{8,9},{9,8},{10,11... | collective-permute-start | bytes 1769480 | tf_op jit(solution)/shard_map/ppermute | solution.py:710
  263.4 54.3 %collective-permute-start.36 = (bf16[384,768]{1,0:T(8,128)(2,1)}, bf16[384,768]{1,0:T(8,128)(2,1)}, u32[]{:S(2)}, u32[]{:S(2)}) collective-permute-start(bf16[384,768]{1,0:T(8,128)(2,1)} %add_convert_fusion.10), channel_id=1, source_target_pairs={{0,2},{1,3},{2,0},{3,1},{4,6},{5,7},{6,4},{7,5},{8,10},{9,11},{10,... | collective-permute-start | bytes 1769480 | tf_op jit(solution)/shard_map/ppermute | solution.py:710
  317.6 61.6 %collective-permute-start.52 = (bf16[768,768]{1,0:T(8,128)(2,1)}, bf16[768,768]{1,0:T(8,128)(2,1)S(1)}, u32[]{:S(2)}, u32[]{:S(2)}) collective-permute-start(bf16[768,768]{1,0:T(8,128)(2,1)} %get-tuple-element.176), channel_id=1, source_target_pairs={{0,1},{1,0},{2,3},{3,2},{4,5},{5,4},{6,7},{7,6},{8,9},{9,8},{10,11... | collective-permute-start | bytes 3538952 | tf_op jit(solution)/shard_map/ppermute | solution.py:710
  317.7 54.2 %collective-permute-start.44 = (bf16[768,768]{1,0:T(8,128)(2,1)}, bf16[768,768]{1,0:T(8,128)(2,1)S(1)}, u32[]{:S(2)}, u32[]{:S(2)}) collective-permute-start(bf16[768,768]{1,0:T(8,128)(2,1)} %get-tuple-element.174), channel_id=1, source_target_pairs={{0,1},{1,0},{2,3},{3,2},{4,5},{5,4},{6,7},{7,6},{8,9},{9,8},{10,11... | collective-permute-start | bytes 3538952 | tf_op jit(solution)/shard_map/ppermute | solution.py:710
  319.8 59.7 %collective-permute-start.17 = (bf16[768,768]{1,0:T(8,128)(2,1)S(1)}, bf16[768,768]{1,0:T(8,128)(2,1)S(1)}, u32[]{:S(2)}, u32[]{:S(2)}) collective-permute-start(bf16[768,768]{1,0:T(8,128)(2,1)S(1)} %copy-done.32), channel_id=1, source_target_pairs={{0,1},{1,0},{2,3},{3,2},{4,5},{5,4},{6,7},{7,6},{8,9},{9,8},{10,11... | collective-permute-start | bytes 3538952 | tf_op jit(solution)/shard_map/ppermute | solution.py:710
  338.2 50.1 %collective-permute-start.54 = (bf16[768,768]{1,0:T(8,128)(2,1)S(1)}, bf16[768,768]{1,0:T(8,128)(2,1)S(1)}, u32[]{:S(2)}, u32[]{:S(2)}) collective-permute-start(bf16[768,768]{1,0:T(8,128)(2,1)S(1)} %add_convert_fusion.1), channel_id=1, source_target_pairs={{0,2},{1,3},{2,0},{3,1},{4,6},{5,7},{6,4},{7,5},{8,10},{9,11},{10,... | collective-permute-start | bytes 3538952 | tf_op jit(solution)/shard_map/ppermute | solution.py:710
  377.8 28.9 %collective-permute-start.45 = (bf16[768,768]{1,0:T(8,128)(2,1)S(1)}, bf16[768,768]{1,0:T(8,128)(2,1)S(1)}, u32[]{:S(2)}, u32[]{:S(2)}) collective-permute-start(bf16[768,768]{1,0:T(8,128)(2,1)S(1)} %add_convert_fusion.4), channel_id=1, source_target_pairs={{0,2},{1,3},{2,0},{3,1},{4,6},{5,7},{6,4},{7,5},{8,10},{9,11},{10,... | collective-permute-start | bytes 3538952 | tf_op jit(solution)/shard_map/ppermute | solution.py:710
  384.5 23.7 %collective-permute-start.16 = (bf16[768,768]{1,0:T(8,128)(2,1)S(1)}, bf16[768,768]{1,0:T(8,128)(2,1)S(1)}, u32[]{:S(2)}, u32[]{:S(2)}) collective-permute-start(bf16[768,768]{1,0:T(8,128)(2,1)S(1)} %copy-done.31), channel_id=1, source_target_pairs={{0,1},{1,0},{2,3},{3,2},{4,5},{5,4},{6,7},{7,6},{8,9},{9,8},{10,11... | collective-permute-start | bytes 3538952 | tf_op jit(solution)/shard_map/ppermute | solution.py:710
  387.4 42.9 %collective-permute-start.18 = (bf16[768,768]{1,0:T(8,128)(2,1)S(1)}, bf16[768,768]{1,0:T(8,128)(2,1)S(1)}, u32[]{:S(2)}, u32[]{:S(2)}) collective-permute-start(bf16[768,768]{1,0:T(8,128)(2,1)S(1)} %add_convert_fusion.7), channel_id=1, source_target_pairs={{0,2},{1,3},{2,0},{3,1},{4,6},{5,7},{6,4},{7,5},{8,10},{9,11},{10,... | collective-permute-start | bytes 3538952 | tf_op jit(solution)/shard_map/ppermute | solution.py:710
  388.3 112.6 %collective-permute-start.33 = (bf16[192,768]{1,0:T(8,128)(2,1)S(1)}, bf16[192,768]{1,0:T(8,128)(2,1)S(1)}, u32[]{:S(2)}, u32[]{:S(2)}) collective-permute-start(bf16[192,768]{1,0:T(8,128)(2,1)S(1)} %maximum_select_fusion.11), channel_id=1, source_target_pairs={{0,4},{4,0},{8,12},{12,8},{16,20},{20,16},{24,28},{28,24},{1,5},{5... | collective-permute-start | bytes 884744 | tf_op jit(solution)/shard_map/ppermute | solution.py:710
  390.1 42.0 %collective-permute-start.55 = (bf16[384,768]{1,0:T(8,128)(2,1)S(1)}, bf16[384,768]{1,0:T(8,128)(2,1)S(1)}, u32[]{:S(2)}, u32[]{:S(2)}) collective-permute-start(bf16[384,768]{1,0:T(8,128)(2,1)S(1)} %dynamic-slice_bitcast_fusion), channel_id=1, source_target_pairs={{0,4},{4,0},{8,12},{12,8},{16,20},{20,16},{24,28},{28,24},{1,5},{5... | collective-permute-start | bytes 1769480 | tf_op jit(solution)/shard_map/ppermute | solution.py:710
  407.3 25.1 %collective-permute-start.46 = (bf16[384,768]{1,0:T(8,128)(2,1)S(1)}, bf16[384,768]{1,0:T(8,128)(2,1)S(1)}, u32[]{:S(2)}, u32[]{:S(2)}) collective-permute-start(bf16[384,768]{1,0:T(8,128)(2,1)S(1)} %dynamic-slice_bitcast_fusion.1), channel_id=1, source_target_pairs={{0,4},{4,0},{8,12},{12,8},{16,20},{20,16},{24,28},{28,24},{1,5},{5... | collective-permute-start | bytes 1769480 | tf_op jit(solution)/shard_map/ppermute | solution.py:710
  448.8 21.2 %collective-permute-start.48 = (bf16[96,768]{1,0:T(8,128)(2,1)S(1)}, bf16[96,768]{1,0:T(8,128)(2,1)S(1)}, u32[]{:S(2)}, u32[]{:S(2)}) collective-permute-start(bf16[96,768]{1,0:T(8,128)(2,1)S(1)} %dynamic-slice_bitcast_fusion.9), channel_id=1, source_target_pairs={{0,16},{4,20},{8,24},{12,28},{16,0},{20,4},{24,8},{28,12},{1,17},{... | collective-permute-start | bytes 442376 | tf_op jit(solution)/shard_map/ppermute | solution.py:710
  458.2 21.1 %collective-permute-start.58 = (bf16[96,768]{1,0:T(8,128)(2,1)S(1)}, bf16[96,768]{1,0:T(8,128)(2,1)S(1)}, u32[]{:S(2)}, u32[]{:S(2)}) collective-permute-start(bf16[96,768]{1,0:T(8,128)(2,1)S(1)} %fusion.10), channel_id=1, source_target_pairs={{0,16},{4,20},{8,24},{12,28},{16,0},{20,4},{24,8},{28,12},{1,17},{... | collective-permute-start | bytes 442376 | tf_op jit(solution)/shard_map/ppermute | solution.py:710
  479.4 19.2 %collective-permute-start.59 = (bf16[192,768]{1,0:T(8,128)(2,1)S(1)}, bf16[192,768]{1,0:T(8,128)(2,1)S(1)}, u32[]{:S(2)}, u32[]{:S(2)}) collective-permute-start(bf16[192,768]{1,0:T(8,128)(2,1)S(1)} %maximum_select_fusion.14), channel_id=1, source_target_pairs={{0,8},{4,12},{8,0},{12,4},{16,24},{20,28},{24,16},{28,20},{1,9},{5... | collective-permute-start | bytes 884744 | tf_op jit(solution)/shard_map/ppermute | solution.py:710
  498.8 28.6 %collective-permute-start.60 = (bf16[384,768]{1,0:T(8,128)(2,1)S(1)}, bf16[384,768]{1,0:T(8,128)(2,1)S(1)}, u32[]{:S(2)}, u32[]{:S(2)}) collective-permute-start(bf16[384,768]{1,0:T(8,128)(2,1)S(1)} %maximum_select_fusion.9), channel_id=1, source_target_pairs={{0,4},{4,0},{8,12},{12,8},{16,20},{20,16},{24,28},{28,24},{1,5},{5... | collective-permute-start | bytes 1769480 | tf_op jit(solution)/shard_map/ppermute | solution.py:710
  504.7 34.3 %collective-permute-start.51 = (bf16[384,768]{1,0:T(8,128)(2,1)S(1)}, bf16[384,768]{1,0:T(8,128)(2,1)S(1)}, u32[]{:S(2)}, u32[]{:S(2)}) collective-permute-start(bf16[384,768]{1,0:T(8,128)(2,1)S(1)} %maximum_select_fusion.8), channel_id=1, source_target_pairs={{0,4},{4,0},{8,12},{12,8},{16,20},{20,16},{24,28},{28,24},{1,5},{5... | collective-permute-start | bytes 1769480 | tf_op jit(solution)/shard_map/ppermute | solution.py:710
  (65 other events, 806.8 us)

commit v2 on v1

v2 whole, which is shorter than its diff:
```python
import math

import jax
import jax.numpy as jnp
import numpy as np
from jax import lax
from jax.experimental import pallas as pl
from jax.experimental.pallas import tpu as pltpu
from jax.sharding import PartitionSpec as P

BUCKETS = 32
MAX_DIST = 128
LEN = 256
ENC = 1024
DH = 64
KEYS = 256

norm_eps = 1e-06
masked_score = -1000000000.0
bf16 = jnp.bfloat16
f32 = jnp.float32
VMEM_CAP = 16 << 20
BIG_VMEM = 58 << 20


def bucket_of_distance():
    half_count = BUCKETS // 2
    growth_ratio = MAX_DIST / half_count
    limits = np.array(
        [int(math.ceil(half_count * growth_ratio ** (m / half_count))) for m in range(1, half_count)],
        dtype=np.int32,
    )
    distance = np.arange(LEN, dtype=np.int32)
    above = np.sum(distance[:, None] >= limits[None, :], axis=1)
    return np.where(distance < half_count, distance, half_count + above).astype(np.int32)


def nn(a, b):
    return lax.dot_general(a, b, (((1,), (0,)), ((), ())), preferred_element_type=f32)


def nt(a, b):
    return lax.dot_general(a, b, (((1,), (1,)), ((), ())), preferred_element_type=f32)


def tn(a, b):
    return lax.dot_general(a, b, (((0,), (0,)), ((), ())), preferred_element_type=f32)


def inv_rms(v):
    return lax.rsqrt(jnp.mean(v * v, axis=-1, keepdims=True) + norm_eps)


def normed(v, gain):
    return (v * inv_rms(v) * gain).astype(bf16)


def norm_back(v, gain, e):
    s = inv_rms(v)
    ge = gain * e
    dot = jnp.mean(ge * v, axis=-1, keepdims=True)
    grad_v = s * ge - v * (s * s * s * dot)
    grad_gain = jnp.sum(e * v * s, axis=0, keepdims=True)
    return grad_v, grad_gain


def lane_half(shape, h):
    lane = lax.broadcasted_iota(jnp.int32, shape, 1)
    return (lane < DH) if h == 0 else (lane >= DH)


def call(kernel, out_shape, args, *, grid=(), in_specs=None, out_specs=None, scratch=(), flops=0, nbytes=0, trans=0, name=None, vmem=VMEM_CAP):
    kw = {}
    if in_specs is not None:
        kw["in_specs"] = in_specs
    if out_specs is not None:
        kw["out_specs"] = out_specs
    return pl.pallas_call(
        kernel,
        out_shape=out_shape,
        grid=grid,
        scratch_shapes=scratch,
        compiler_params=pltpu.CompilerParams(vmem_limit_bytes=vmem),
        cost_estimate=pl.CostEstimate(flops=1, bytes_accessed=1, transcendentals=0),
        name=name,
        **kw,
    )(*args)


def whole(shape):
    return pl.BlockSpec(shape, lambda *_: (0,) * len(shape))


SMEM = pl.BlockSpec(memory_space=pltpu.SMEM)


def side_by_side(refs, i):
    w = refs[0].shape[0] // 4
    return jnp.concatenate([r[i * w : (i + 1) * w] for r in refs], axis=0)


def pair_rows(y_ref, refs, shared):
    def rows(i):
        if not shared:
            return side_by_side(refs, i)
        w = refs[0].shape[0] // 2
        first = y_ref[0] == i // 2
        part = slice((i % 2) * w, (i % 2 + 1) * w)
        return jnp.concatenate(
            [jnp.where(first, refs[0][part], refs[1][part]), jnp.where(first, refs[2][part], refs[3][part])], axis=0
        )

    return rows


def self_fwd_kernel(last, y_ref, len_ref, x_ref, g_ref, *rest):
    weights = rest[0:2]
    bias_ref = rest[2]
    rest = rest[3:]
    if last:
        xin_ref, q_ref, k_ref, vt_ref, e_ref, r_ref, at_ref, x1_ref, n1_ref, n2_ref, bs_ref = rest
    else:
        q_ref, k_ref, vt_ref, e_ref, r_ref, at_ref, x1_ref, bs_ref = rest
    nh = q_ref.shape[1] // DH
    nb = x_ref.shape[0] // LEN
    x = x_ref[...].astype(f32)
    n1 = normed(x, g_ref[0:1].astype(f32))
    if last:
        n1_ref[...] = n1

    q_ref[...] = nt(n1, side_by_side(weights, 0)).astype(bf16)
    k_ref[...] = nt(n1, side_by_side(weights, 1)).astype(bf16)
    vt_ref[...] = nt(side_by_side(weights, 2), n1).astype(bf16)
    key = lax.broadcasted_iota(jnp.int32, (LEN, LEN), 0)
    query = lax.broadcasted_iota(jnp.int32, (LEN, LEN), 1)
    for p in range(nh // 2):
        lanes = slice(p * 2 * DH, (p + 1) * 2 * DH)
        for h in range(2):
            row = jnp.broadcast_to(bias_ref[2 * p + h : 2 * p + h + 1, :], (LEN, LEN))
            bs_ref[h] = pltpu.roll(row, 0, 1, stride=1, stride_axis=0)
        for b in range(nb):
            tok = slice(b * LEN, (b + 1) * LEN)
            allowed = (key <= query) & (key < len_ref[y_ref[1] + b])
            kp = k_ref[tok, lanes]
            qp = q_ref[tok, lanes]
            outs = []
            for h in range(2):
                head = 2 * p + h
                qh = jnp.where(lane_half(qp.shape, h), qp, jnp.zeros_like(qp))
                s = nt(kp, qh) + bs_ref[h]
                s = jnp.where(allowed, s, masked_score)
                top = jnp.max(s, axis=0, keepdims=True)
                e = jnp.exp(s - top)
                r = 1.0 / jnp.sum(e, axis=0, keepdims=True)
                eb = e.astype(bf16)
                e_ref[b, head] = eb
                r_ref[b, head : head + 1, :] = r
                outs.append(nn(vt_ref[head * DH : (head + 1) * DH, tok], eb) * r)
            at_ref[lanes, tok] = jnp.concatenate(outs, axis=0).astype(bf16)
    mixed = tn(at_ref[...], side_by_side(weights, 3))
    if last:
        x1 = xin_ref[...] + mixed
        n2_ref[...] = normed(x1, g_ref[1:2].astype(f32))
    else:
        x1 = x + mixed
    x1_ref[...] = x1


def self_fwd(last, y, lens, x, g, weights, bias, xin=None):
    t, d = x.shape
    w = weights[0].shape[0] // 4
    c = 2 * w
    nh = c // DH
    nb = t // LEN
    outs = [
        jax.ShapeDtypeStruct((t, c), bf16),
        jax.ShapeDtypeStruct((t, c), bf16),
        jax.ShapeDtypeStruct((c, t), bf16),
        jax.ShapeDtypeStruct((nb, nh, LEN, LEN), bf16),
        jax.ShapeDtypeStruct((nb, nh, LEN), f32),
        jax.ShapeDtypeStruct((c, t), bf16),
        jax.ShapeDtypeStruct((t, d), f32),
    ]
    args = [y, lens, x, g, *weights, bias]
    if last:
        args.append(xin)
        outs += [jax.ShapeDtypeStruct((t, d), bf16)] * 2
    flops = 2 * t * d * c * 4 + 2 * t * LEN * nh * 128 * 2
    return call(
        lambda *r: self_fwd_kernel(last, *r),
        tuple(outs),
        args,
        in_specs=[SMEM, SMEM] + [whole(a.shape) for a in args[2:]],
        out_specs=tuple(whole(o.shape) for o in outs),
        scratch=[pltpu.VMEM((2, LEN, LEN), f32)],
        flops=flops * 3,
        nbytes=12 * 1024 * 1024,
        trans=t * LEN * nh,
        name="self_fwd",
    )


def enc_kv_kernel(shared, y_ref, enc_ref, *rest):
    k_ref, v_ref = rest[-2:]
    enc = enc_ref[...]
    rows = pair_rows(y_ref, rest[:-2], shared)
    k_ref[...] = nt(enc, rows(0)).astype(bf16)
    v_ref[...] = nt(enc, rows(1)).astype(bf16)


def enc_kv(shared, y, enc, kv):
    t, d = enc.shape
    c = kv[0].shape[0] if shared else kv[0].shape[0] // 2
    rows = 512
    half = pl.BlockSpec((rows, c), lambda i: (i, 0))
    return call(
        lambda *r: enc_kv_kernel(shared, *r),
        (jax.ShapeDtypeStruct((t, c), bf16),) * 2,
        (y, enc, *kv),
        grid=(t // rows,),
        in_specs=[SMEM, pl.BlockSpec((rows, d), lambda i: (i, 0))] + [whole(a.shape) for a in kv],
        out_specs=(half, half),
        flops=2 * t * d * c * 2 * 2,
        nbytes=t * d * 2 + 4 * t * c * 2,
        name="enc_kv",
    )


def cross_fwd_kernel(last, pairs, y_ref, len_ref, n2_ref, g_ref, *rest):
    n_w = 4 if last else 2
    weights = pair_rows(y_ref, rest[:n_w], last)
    k_ref, v_ref, xin_ref = rest[n_w : n_w + 3]
    rest = rest[n_w + 3 :]
    if last:
        q_ref, r_ref, at_ref, x2_ref, n3_ref, s_ref, e_ref = rest
    else:
        q_ref, r_ref, at_ref, x2_ref, s_ref, e_ref = rest
    step = pl.program_id(0)
    b = step // pairs
    p = lax.rem(step, pairs)

    @pl.when(step == 0)
    def _():
        q_ref[...] = nt(n2_ref[...], weights(2)).astype(bf16)

    tok = pl.ds(pl.multiple_of(b * LEN, LEN), LEN)
    lanes = pl.ds(pl.multiple_of(p * 2 * DH, 2 * DH), 2 * DH)
    qp = q_ref[tok, lanes]
    count = len_ref[y_ref[1] + b]
    key = lax.broadcasted_iota(jnp.int32, (KEYS, LEN), 0)
    queries = [jnp.where(lane_half(qp.shape, h), qp, jnp.zeros_like(qp)) for h in range(2)]
    tops = [None, None]
    for c in range(ENC // KEYS):
        part = slice(c * KEYS, (c + 1) * KEYS)
        for h in range(2):
            s = nt(k_ref[part], queries[h])
            s = jnp.where(key < count - c * KEYS, s, masked_score)
            s_ref[h, part] = s
            top = jnp.max(s.reshape(KEYS // 8, 8, LEN), axis=0)
            tops[h] = top if c == 0 else jnp.maximum(tops[h], top)
    outs = []
    for h in range(2):
        top = jnp.max(tops[h], axis=0, keepdims=True)
        total = None
        for c in range(ENC // KEYS):
            part = slice(c * KEYS, (c + 1) * KEYS)
            e = jnp.exp(s_ref[h, part] - top)
            t = jnp.sum(e.reshape(KEYS // 8, 8, LEN), axis=0)
            total = t if c == 0 else total + t
            e_ref[h, part] = e.astype(bf16)
        r = 1.0 / jnp.sum(total, axis=0, keepdims=True)
        r_ref[0, h : h + 1, :] = r
        r_ref[0, 2 + h : 3 + h, :] = top
        outs.append(tn(v_ref[...], e_ref[h])[h * DH : (h + 1) * DH] * r)
    at_ref[lanes, tok] = jnp.concatenate(outs, axis=0).astype(bf16)

    @pl.when(step == pl.num_programs(0) - 1)
    def _():
        x2 = xin_ref[...] + tn(at_ref[...], weights(3))
        x2_ref[...] = x2
        if last:
            n3_ref[...] = normed(x2, g_ref[2:3].astype(f32))


def cross_fwd(last, y, lens, n2, g, qo, k, v, xin):
    t, d = n2.shape
    c = k.shape[1]
    nb = t // LEN
    pairs = c // (2 * DH)
    outs = [
        jax.ShapeDtypeStruct((t, c), bf16),
        jax.ShapeDtypeStruct((nb * pairs, 4, LEN), f32),
        jax.ShapeDtypeStruct((c, t), bf16),
        jax.ShapeDtypeStruct((t, d), f32),
    ]
    specs = [
        whole((t, c)),
        pl.BlockSpec((1, 4, LEN), lambda i: (i, 0, 0)),
        whole((c, t)),
        whole((t, d)),
    ]
    if last:
        outs.append(jax.ShapeDtypeStruct((t, d), bf16))
        specs.append(whole((t, d)))
    return call(
        lambda *r: cross_fwd_kernel(last, pairs, *r),
        tuple(outs),
        (y, lens, n2, g, *qo, k, v, xin),
        grid=(nb * pairs,),
        in_specs=[
            SMEM,
            SMEM,
            whole(n2.shape),
            whole(g.shape),
            *[whole(a.shape) for a in qo],
            pl.BlockSpec((ENC, 2 * DH), lambda i: (i // pairs, i % pairs)),
            pl.BlockSpec((ENC, 2 * DH), lambda i: (i // pairs, i % pairs)),
            whole(xin.shape),
        ],
        out_specs=tuple(specs),
        scratch=[pltpu.VMEM((2, ENC, LEN), f32), pltpu.VMEM((2, ENC, LEN), bf16)],
        flops=3 * (2 * t * d * c * 2 + 2 * t * ENC * c * 2 * 2),
        nbytes=14 * 1024 * 1024,
        trans=t * ENC * (c // DH),
        name="cross_fwd",
    )


ROOT = math.sqrt(2.0 / math.pi)
CUBE = 0.044715


def ff_kernel(last, y_ref, n3_ref, gf_ref, *rest):
    if last:
        ha_in, ha_out, ga_in, ga_out, hb_in, hb_out, gb_in, gb_out = rest[:8]
        rest = rest[8:]
        first = y_ref[0] == 0

        def weights(h_in, h_out, g_in, g_out):
            return (
                lambda: jnp.where(first, h_in[...], g_in[...]),
                lambda: jnp.where(first, g_out[...], h_out[...]),
            )

        shards = (weights(ha_in, ha_out, ga_in, ga_out), weights(hb_in, hb_out, gb_in, gb_out))
    else:
        wia_ref, woa_ref, wib_ref, wob_ref = rest[:4]
        rest = rest[4:]
        shards = ((lambda: wia_ref[...], lambda: woa_ref[...]), (lambda: wib_ref[...], lambda: wob_ref[...]))
    if last:
        yin_ref, gin_ref, x2_ref, g_ref = rest[:4]
        gwia, gwoa, gwib, gwob, out_ref, gx2_ref, go2_ref, gg_ref, y_acc, gn_ref, n3t_ref = rest[4:]
    else:
        gwia, gwoa, gwib, gwob, y_acc, gn_ref, n3t_ref = rest
    step = pl.program_id(0)

    @pl.when(step == 0)
    def _():
        n3t_ref[...] = n3_ref[...].T
        if last:
            y_acc[...] = yin_ref[...]
            gn_ref[...] = gin_ref[...]
        else:
            y_acc[...] = jnp.zeros_like(y_acc)
            gn_ref[...] = jnp.zeros_like(gn_ref)

    n3 = n3_ref[...]
    gf = gf_ref[...]
    for (get_wi, get_wo), gwi, gwo in zip(shards, (gwia, gwib), (gwoa, gwob)):
        wi, wo = get_wi(), get_wo()
        u = nn(n3, wi)
        dh = nt(gf, wo)
        u2 = u * u
        th = jnp.tanh(ROOT * u * (1.0 + CUBE * u2))
        half = 0.5 * (1.0 + th)
        r = (u * half).astype(bf16)
        slope = half + 0.5 * u * (1.0 - th * th) * (ROOT * (1.0 + (3.0 * CUBE) * u2))
        gu = (dh * slope).astype(bf16)
        y_acc[...] += nn(r, wo)
        gn_ref[...] += nt(gu, wi)
        gwo[...] = tn(r, gf).astype(bf16)
        gwi[...] = nn(n3t_ref[...], gu).astype(bf16)

    if last:

        @pl.when(step == pl.num_programs(0) - 1)
        def _():
            x2 = x2_ref[...]
            out_ref[...] = (x2 + y_acc[...]).astype(bf16)
            gx, gg = norm_back(x2, g_ref[2:3].astype(f32), gn_ref[...])
            gx2 = gf.astype(f32) + gx
            gx2_ref[...] = gx2
            go2_ref[...] = gx2.astype(bf16)
            gg_ref[...] = gg


def ff(last, y, n3, gf, weights, yin=None, gin=None, x2=None, g=None):
    t, d = n3.shape
    hid = weights[0].shape[1]
    blk = 256
    args = [y, n3, gf]
    col = pl.BlockSpec((d, blk), lambda i: (0, i))
    row = pl.BlockSpec((blk, d), lambda i: (i, 0))
    in_specs = [SMEM, whole((t, d)), whole((t, d))]
    if last:
        for v in weights:
            args += [v, v]
            in_specs += [col, row]
    else:
        args += weights
        in_specs += [col, row, col, row]
    outs = [jax.ShapeDtypeStruct((d, hid), bf16), jax.ShapeDtypeStruct((hid, d), bf16)] * 2
    specs = [col, row, col, row]
    acc = jax.ShapeDtypeStruct((t, d), f32)
    scratch = [pltpu.VMEM((d, t), bf16)]
    if last:
        args += [yin, gin, x2, g]
        in_specs += [whole((t, d))] * 3 + [whole(g.shape)]
        outs += [jax.ShapeDtypeStruct((t, d), bf16), acc, jax.ShapeDtypeStruct((t, d), bf16), jax.ShapeDtypeStruct((1, d), f32)]
        specs += [whole((t, d))] * 3 + [whole((1, d))]
        scratch = [pltpu.VMEM((t, d), f32)] * 2 + scratch
    else:
        outs += [acc, acc]
        specs += [whole((t, d))] * 2
    return call(
        lambda *r: ff_kernel(last, *r),
        tuple(outs),
        args,
        grid=(hid // blk,),
        in_specs=in_specs,
        out_specs=tuple(specs),
        scratch=scratch,
        flops=2 * 6 * 2 * t * d * hid * 2,
        nbytes=12 * 1024 * 1024,
        trans=2 * t * hid,
        name="ff",
    )


def head_pair_back(k_t, v, q, ga, ga_t, a_t, es, rs, extra=None):
    gv = None
    gk = None
    gq_t = []
    for h in range(2):
        part = slice(h * DH, (h + 1) * DH)
        r = rs[h]
        gah = ga_t[part].astype(f32) * r
        delta = jnp.sum(gah * a_t[part].astype(f32), axis=0, keepdims=True)
        gah = gah.astype(bf16)
        zero = jnp.zeros_like(gah)
        rhs = jnp.concatenate([gah, zero] if h == 0 else [zero, gah], axis=0)
        gp = nn(v, rhs)
        e = es[h]
        gs = (e.astype(f32) * (gp - delta)).astype(bf16)
        if extra is not None:
            extra(h, gs)
        keep = lane_half(q.shape, h)
        term_v = nt(e, rhs)
        term_k = nn(gs, jnp.where(keep, q, jnp.zeros_like(q)))
        gv = term_v if gv is None else gv + term_v
        gk = term_k if gk is None else gk + term_k
        gq_t.append(nn(k_t[part], gs))
    return jnp.concatenate(gq_t, axis=0).astype(bf16), gk.astype(bf16), gv.astype(bf16)


def cross_bwd_kernel(pairs, steps, y_ref, len_ref, go_ref, n2_ref, *rest):
    weights = (pair_rows(y_ref, rest[0:2], False), pair_rows(y_ref, rest[2:6], True))
    sides = (rest[6:11], rest[11:16])
    gk0, gv0, gk1, gv1, outs, gn_ref, gat_ref, gqt_ref, e_ref, gs_ref = *rest[16:20], rest[20:24], *rest[24:]
    w = outs[0].shape[0] // 2
    step = pl.program_id(0)
    key = lax.broadcasted_iota(jnp.int32, (KEYS, LEN), 0)

    def half(side, local, gk_ref, gv_ref):
        q_ref, k_ref, v_ref, r_ref, at_ref = sides[side]
        b = local // pairs
        p = lax.rem(local, pairs)

        @pl.when(local == 0)
        def _():
            gat_ref[...] = nt(weights[side](3), go_ref[...]).astype(bf16)

        tok = pl.ds(pl.multiple_of(b * LEN, LEN), LEN)
        lanes = pl.ds(pl.multiple_of(p * 2 * DH, 2 * DH), 2 * DH)
        qp = q_ref[tok, lanes]
        ga_t = gat_ref[lanes, tok]
        a_t = at_ref[lanes, tok]
        count = len_ref[y_ref[1] + b]
        queries, grads, deltas = [], [], []
        for h in range(2):
            part = slice(h * DH, (h + 1) * DH)
            gah = ga_t[part].astype(f32) * r_ref[0, h : h + 1, :]
            deltas.append(jnp.sum(gah * a_t[part].astype(f32), axis=0, keepdims=True))
            gah = gah.astype(bf16)
            zero = jnp.zeros_like(gah)
            grads.append(jnp.concatenate([gah, zero] if h == 0 else [zero, gah], axis=0))
            queries.append(jnp.where(lane_half(qp.shape, h), qp, jnp.zeros_like(qp)))
        for c in range(ENC // KEYS):
            part = slice(c * KEYS, (c + 1) * KEYS)
            kc = k_ref[part]
            vc = v_ref[part]
            for h in range(2):
                s = jnp.where(key < count - c * KEYS, nt(kc, queries[h]), masked_score)
                e = jnp.exp(s - r_ref[0, 2 + h : 3 + h, :])
                gs_ref[h, part] = (e * (nn(vc, grads[h]) - deltas[h])).astype(bf16)
                e_ref[h, part] = e.astype(bf16)
            gv_ref[part] = (nt(e_ref[0, part], grads[0]) + nt(e_ref[1, part], grads[1])).astype(bf16)
            gk_ref[part] = (nn(gs_ref[0, part], queries[0]) + nn(gs_ref[1, part], queries[1])).astype(bf16)
        k = k_ref[...]
        gq = [tn(k, gs_ref[h])[h * DH : (h + 1) * DH] for h in range(2)]
        gqt_ref[lanes, tok] = jnp.concatenate(gq, axis=0).astype(bf16)

        @pl.when(local == steps - 1)
        def _():
            gqt = gqt_ref[...]
            gwq = nn(gqt, n2_ref[...]).astype(bf16)
            gwo = nn(at_ref[...], go_ref[...]).astype(bf16)
            for i in range(2):
                outs[2 * side + i][0:w] = gwq[i * w : (i + 1) * w]
                outs[2 * side + i][w:] = gwo[i * w : (i + 1) * w]
            gn = tn(gqt, weights[side](2))
            gn_ref[...] = gn if side == 1 else gn_ref[...] + gn

    @pl.when(step < steps)
    def _():
        half(1, step, gk1, gv1)

    @pl.when(step >= steps)
    def _():
        half(0, step - steps, gk0, gv0)


def cross_bwd(y, lens, go, n2, w0, w1, side0, side1):
    t, d = go.shape
    te, c = side0[1].shape
    nb = t // LEN
    pairs = c // (2 * DH)
    steps = nb * pairs

    def early(i):
        return jnp.minimum(i, steps - 1)

    def late(i):
        return jnp.maximum(i - steps, 0)

    def tokhead(when):
        return pl.BlockSpec((ENC, 2 * DH), lambda i: (when(i) // pairs, when(i) % pairs))

    def side_specs(when):
        return [whole((t, c)), tokhead(when), tokhead(when), pl.BlockSpec((1, 4, LEN), lambda i: (when(i), 0, 0)), whole((c, t))]

    grad = jax.ShapeDtypeStruct((te, c), bf16)
    out = jax.ShapeDtypeStruct((c, d), bf16)
    return call(
        lambda *r_: cross_bwd_kernel(pairs, steps, *r_),
        (grad,) * 4 + (out,) * 4 + (jax.ShapeDtypeStruct((t, d), f32),),
        (y, lens, go, n2, *w0, *w1, *side0, *side1),
        grid=(2 * steps,),
        in_specs=[SMEM, SMEM, whole((t, d)), whole((t, d))]
        + [whole(a.shape) for a in (*w0, *w1)]
        + side_specs(late)
        + side_specs(early),
        out_specs=(tokhead(late), tokhead(late), tokhead(early), tokhead(early)) + (whole((c, d)),) * 4 + (whole((t, d)),),
        scratch=[
            pltpu.VMEM((c, t), bf16),
            pltpu.VMEM((c, t), bf16),
            pltpu.VMEM((2, ENC, LEN), bf16),
            pltpu.VMEM((2, ENC, LEN), bf16),
        ],
        vmem=BIG_VMEM,
        name="cross_bwd",
    )


def enc_grad_kernel(y_ref, enc_ref, gk1_ref, gv1_ref, gk0_ref, gv0_ref, *rest):
    w0 = pair_rows(y_ref, rest[0:2], False)
    w1 = pair_rows(y_ref, rest[2:6], True)
    out_ref, outs, accs_ref = rest[6], rest[7:11], rest[11]
    w = outs[0].shape[0] // 2
    step = pl.program_id(0)
    enc = enc_ref[...]
    grads = [g[...] for g in (gk1_ref, gv1_ref, gk0_ref, gv0_ref)]
    out_ref[...] = (nn(grads[0], w1(0)) + nn(grads[1], w1(1))) + (nn(grads[2], w0(0)) + nn(grads[3], w0(1)))
    terms = [tn(g, enc) for g in grads]

    @pl.when(step == 0)
    def _():
        for i in range(4):
            accs_ref[i] = terms[i]

    @pl.when(step != 0)
    def _():
        for i in range(4):
            accs_ref[i] += terms[i]

    @pl.when(step == pl.num_programs(0) - 1)
    def _():
        for pair in range(2):
            for i in range(2):
                acc = accs_ref[2 * pair + i]
                outs[2 * pair][i * w : (i + 1) * w] = acc[0:w].astype(bf16)
                outs[2 * pair + 1][i * w : (i + 1) * w] = acc[w:].astype(bf16)


def enc_grad(y, enc, gk1, gv1, gk0, gv0, w0, w1):
    te, d = enc.shape
    c = gk1.shape[1]
    rows = 512
    half = pl.BlockSpec((rows, c), lambda i: (i, 0))
    block = pl.BlockSpec((rows, d), lambda i: (i, 0))
    out = jax.ShapeDtypeStruct((c, d), bf16)
    return call(
        enc_grad_kernel,
        (jax.ShapeDtypeStruct((te, d), f32),) + (out,) * 4,
        (y, enc, gk1, gv1, gk0, gv0, *w0, *w1),
        grid=(te // rows,),
        in_specs=[SMEM, block] + [half] * 4 + [whole(a.shape) for a in (*w0, *w1)],
        out_specs=(block,) + (whole((c, d)),) * 4,
        scratch=[pltpu.VMEM((4, c, d), f32)],
        vmem=BIG_VMEM,
        name="enc_grad",
    )


def self_bwd_kernel(x_ref, x1_ref, gx2_ref, gn2_ref, g_ref, n1_ref, *rest):
    weights = rest[0:4]
    sides = (rest[4:10], rest[10:16])
    outs = rest[16:20]
    gd_ref, gg2_ref, gg1_ref, gi_ref, gat_ref, gqt_ref, gk_ref, gv_ref, gx1_ref = rest[20:]
    w = outs[0].shape[0] // 4
    c = 2 * w
    nb = n1_ref.shape[0] // LEN
    gx, gg2 = norm_back(x1_ref[...], g_ref[1:2].astype(f32), gn2_ref[...])
    gx1 = gx2_ref[...] + gx
    gx1_ref[...] = gx1
    gg2_ref[...] = gg2
    go = gx1.astype(bf16)
    ri = lax.broadcasted_iota(jnp.int32, (LEN, LEN), 0)
    ci = lax.broadcasted_iota(jnp.int32, (LEN, LEN), 1)
    flip = jnp.where(ri + ci == LEN - 1, 1.0, 0.0).astype(bf16)
    n1 = n1_ref[...]
    gn = None
    for side in (1, 0):
        shards = weights[2 * side : 2 * side + 2]
        q_ref, k_ref, vt_ref, e_ref, r_ref, at_ref = sides[side]
        gat_ref[...] = nt(side_by_side(shards, 3), go).astype(bf16)
        gwo = nn(at_ref[...], go).astype(bf16)
        for p in range(c // (2 * DH)):
            lanes = slice(p * 2 * DH, (p + 1) * 2 * DH)
            for h in range(2):
                head = side * (c // DH) + 2 * p + h
                gd_ref[head : head + 1, :] = jnp.zeros((1, LEN), f32)
            for b in range(nb):
                tok = slice(b * LEN, (b + 1) * LEN)

                def extra(h, gs):
                    turned = pltpu.roll(nn(gs, flip), 0, 1, stride=1, stride_axis=0)
                    head = side * (c // DH) + 2 * p + h
                    gd_ref[head : head + 1, :] += jnp.sum(turned, axis=0, keepdims=True)

                gq, gk, gv = head_pair_back(
                    k_ref[tok, lanes].T, vt_ref[lanes, tok].T, q_ref[tok, lanes], None, gat_ref[lanes, tok], at_ref[lanes, tok],
                    [e_ref[b, 2 * p], e_ref[b, 2 * p + 1]],
                    [r_ref[b, 2 * p : 2 * p + 1, :], r_ref[b, 2 * p + 1 : 2 * p + 2, :]],
                    extra,
                )
                gqt_ref[lanes, tok] = gq
                gk_ref[tok, lanes] = gk
                gv_ref[tok, lanes] = gv
        gqt = gqt_ref[...]
        gk = gk_ref[...]
        gv = gv_ref[...]
        gwq = nn(gqt, n1).astype(bf16)
        gwk = tn(gk, n1).astype(bf16)
        gwv = tn(gv, n1).astype(bf16)
        for i, gw in enumerate((gwq, gwk, gwv, gwo)):
            for j in range(2):
                outs[2 * side + j][i * w : (i + 1) * w] = gw[j * w : (j + 1) * w]
        part = tn(gqt, side_by_side(shards, 0)) + nn(gk, side_by_side(shards, 1)) + nn(gv, side_by_side(shards, 2))
        gn = part if gn is None else gn + part
    gi, gg1 = norm_back(x_ref[...].astype(f32), g_ref[0:1].astype(f32), gn)
    gi_ref[...] = gx1_ref[...] + gi
    gg1_ref[...] = gg1


def self_bwd(x, x1, gx2, gn2, g, n1, weights, side0, side1):
    t, d = x1.shape
    c = weights[0].shape[0] // 2
    args = [x, x1, gx2, gn2, g, n1, *weights, *side0, *side1]
    outs = [jax.ShapeDtypeStruct((2 * c, d), bf16)] * 4 + [
        jax.ShapeDtypeStruct((2 * c // DH, LEN), f32),
        jax.ShapeDtypeStruct((1, d), f32),
        jax.ShapeDtypeStruct((1, d), f32),
        jax.ShapeDtypeStruct((t, d), f32),
    ]
    return call(
        self_bwd_kernel,
        tuple(outs),
        args,
        in_specs=[whole(a.shape) for a in args],
        out_specs=tuple(whole(o.shape) for o in outs),
        scratch=[
            pltpu.VMEM((c, t), bf16),
            pltpu.VMEM((c, t), bf16),
            pltpu.VMEM((t, c), bf16),
            pltpu.VMEM((t, c), bf16),
            pltpu.VMEM((t, d), f32),
        ],
        vmem=BIG_VMEM,
        name="self_bwd",
    )


def local_program(tensor_size, dp_size, *arrays):
    (block_in, enc_states, dec_len, enc_len, gain_self, self_query, self_key, self_value, self_out, rel_table,
     gain_cross, cross_query, cross_key, cross_value, cross_out, gain_ff, ff_in, ff_out, out_grad) = arrays
    t_index = lax.axis_index("tensor")
    d_index = lax.axis_index("dp")
    nb = block_in.shape[0] // LEN
    w, d = self_out.shape
    heads = w // DH

    def swap(v, axis, bit):
        n = tensor_size if axis == "tensor" else dp_size
        return lax.ppermute(v, axis, [(i, i ^ bit) for i in range(n)])

    def d_bit(bit):
        return (d_index // bit) % 2

    y = d_bit(1).astype(jnp.int32)
    y_is0 = y == 0
    place = jnp.stack([y, (t_index * nb).astype(jnp.int32)])

    def core(v):
        return swap(v, "tensor", 1)

    def over_x(v):
        return swap(v, "tensor", 2)

    def over_y(v):
        return swap(v, "dp", 1)

    def fence(*vals):
        return lax.optimization_barrier(vals)

    gains = jnp.stack([gain_self, gain_cross, gain_ff])

    buckets = np.eye(BUCKETS, dtype=np.float32)[bucket_of_distance()]
    rel_own = jnp.dot(rel_table.astype(f32).T, jnp.asarray(buckets.T), precision=lax.Precision.HIGHEST)
    rel_x = over_x(rel_own)
    own_s = jnp.concatenate([self_query.T, self_key.T, self_value.T, self_out], axis=0)
    own_s, rel_own = fence(own_s, rel_own)
    x_s = over_x(own_s)
    s_0 = [own_s, core(own_s)]
    bias0 = jnp.concatenate([rel_own, core(rel_own)], axis=0)
    own_c = jnp.concatenate([cross_key.T, cross_value.T, cross_query.T, cross_out], axis=0)
    c_0 = [own_c, core(own_c)]
    out = self_fwd(False, place, dec_len, block_in, gains, s_0, bias0)
    *out, c_0[1] = fence(*out, c_0[1])
    fq0, fk0, fv0, fe0, fr0, fa0, xp = out
    k0, v0 = enc_kv(False, place, enc_states, c_0)
    k0, v0, xp, x_s, rel_x = fence(k0, v0, xp, x_s, rel_x)
    s_1 = [x_s, core(x_s)]
    bias1 = jnp.concatenate([rel_x, core(rel_x)], axis=0)
    half = own_c.shape[0] // 2
    send_c, x_s = fence(jnp.where(y_is0, own_c[:half], own_c[half:]), x_s)
    x_c = over_x(send_c)
    out = self_fwd(True, place, dec_len, block_in, gains, s_1, bias1, xp)
    *out, x_c = fence(*out, x_c)
    fq1, fk1, fv1, fe1, fr1, fa1, x1, n1, n2 = out
    send_f, x_c = fence(jnp.where(y_is0, ff_in, ff_out), x_c)
    x_f = over_x(send_f)
    y_c, c_c = over_y(x_c), core(x_c)
    cq0, cr0, ca0, x2p = cross_fwd(False, place, enc_len, n2, gains, c_0, k0, v0, x1)
    x2p, y_c, c_c = fence(x2p, y_c, c_c)
    c_1 = [x_c, y_c, c_c, core(y_c)]
    wi1, wo1 = core(ff_in), core(ff_out)
    k1, v1 = enc_kv(True, place, enc_states, c_1)
    k1, v1, x_f = fence(k1, v1, x_f)
    y_f, c_f = over_y(x_f), core(x_f)
    cq1, cr1, ca1, x2, n3 = cross_fwd(True, place, enc_len, n2, gains, c_1, k1, v1, x2p)
    n3, x2, wi1, wo1, c_f = fence(n3, x2, wi1, wo1, c_f)

    rest_size = dp_size // 2
    m = d_index // 2
    rest_groups = [[2 * i + j for i in range(rest_size)] for j in range(2)]

    def plus(*vals):
        total = vals[0].astype(f32)
        for v in vals[1:]:
            total = total + v.astype(f32)
        return total.astype(bf16)

    def pick(v, n, i):
        v = v.reshape((n, v.shape[0] // n) + v.shape[1:])
        return lax.dynamic_index_in_dim(v, i, 0, keepdims=False)

    def ordered(a, b):
        return jnp.where(y_is0, jnp.concatenate([a, b], axis=0), jnp.concatenate([b, a], axis=0))

    def sent_y(*vals):
        return over_y(plus(*[pick(v, 2, 1 - y) for v in vals]))

    def kept_y(*vals):
        return [pick(v, 2, y) for v in vals]

    def sum_ordered(parts):
        while len(parts) > 1:
            parts = [a + b for a, b in zip(parts[0::2], parts[1::2])]
        return parts[0]

    def stage_z(v):
        return [pick(v, rest_size, m)] + [swap(pick(v, rest_size, m ^ j), "dp", 2 * j) for j in range(1, rest_size)]

    def stage_z_back(v):
        return [v] + [swap(v, "dp", 2 * j) for j in range(1, rest_size)]

    def ordered_z(parts):
        bit = 1
        while len(parts) > 1:
            low = (m // bit) % 2 == 0
            parts = [
                jnp.where(low, jnp.concatenate([a, b], axis=0), jnp.concatenate([b, a], axis=0))
                for a, b in zip(parts[0::2], parts[1::2])
            ]
            bit *= 2
        return parts[0]

    gwi0, gwo0, gwi1, gwo1, yp, gp = ff(False, place, n3, out_grad, [ff_in, ff_out, wi1, wo1])
    yp, y_f = fence(yp, y_f)
    a1, b1 = core(gwo1), core(gwi1)
    f_1 = [x_f, y_f, c_f, core(y_f)]
    out = ff(True, place, n3, out_grad, f_1, yp, gp, x2, gains)
    *out, a1, b1 = fence(*out, a1, b1)
    gwi2, gwo2, gwi3, gwo3, block_out, gx2, go2, gg3 = out
    a3, b3 = core(gwo3), core(gwi3)
    a3, b3, go2 = fence(a3, b3, go2)
    wo_s = plus(gwo2, a3)
    wi_send = jnp.concatenate(
        [plus(pick(gwi0, 2, 1 - y), pick(b1, 2, 1 - y)), plus(pick(gwi2, 2, 1 - y), pick(b3, 2, 1 - y))], axis=0
    )
    wo_s, wi_send, go2 = fence(wo_s, wi_send, go2)
    xo = over_x(wo_s)
    ywi = over_y(wi_send)
    out = cross_bwd(place, enc_len, go2, n2, c_0, c_1, (cq0, k0, v0, cr0, ca0), (cq1, k1, v1, cr1, ca1))
    *out, xo, ywi = fence(*out, xo, ywi)
    gk0, gv0, gk1, gv1, gqo0, gqo1, gqo2, gqo3, gn2 = out
    c3 = core(gqo3)
    hid = gwi0.shape[0] // 2
    wi_x = plus(pick(gwi2, 2, y), pick(b3, 2, y), ywi[hid:])
    wo_y = plus(*[pick(v, 2, 1 - y) for v in (gwo0, a1, xo)])
    wi_x, wo_y, c3, gn2 = fence(wi_x, wo_y, c3, gn2)
    wq_x = jnp.concatenate([wi_x, plus(gqo2, c3)], axis=0)
    wq_x, gn2 = fence(wq_x, gn2)
    xwq, ywo = over_x(wq_x), over_y(wo_y)
    out = self_bwd(
        block_in, x1, gx2, gn2, gains, n1, [*s_0, *s_1], (fq0, fk0, fv0, fe0, fr0, fa0), (fq1, fk1, fv1, fe1, fr1, fa1)
    )
    *out, xwq, ywo = fence(*out, xwq, ywo)
    gs0, gs1, gs2, gs3, gd, gg2, gg1, grad_in = out
    s3, c1 = core(gs3), core(gqo1)
    flipped = jnp.asarray(np.ascontiguousarray(buckets[::-1]))
    grel = jnp.dot(gd, flipped, precision=lax.Precision.HIGHEST)
    grel = grel.reshape(tensor_size, heads * BUCKETS)
    slots = jnp.arange(tensor_size)[:, None] ^ t_index
    order = (slots == jnp.arange(tensor_size)[None, :]).astype(f32)
    grel = jnp.dot(order.T, grel, precision=lax.Precision.HIGHEST)
    grel = jnp.pad(grel.reshape(1, -1), ((0, 0), (0, d - grel.size)))
    small = jnp.concatenate([gg1, gg2, gg3, grel], axis=0)
    small_got = core(small)
    xwi, xqo = xwq[:hid], xwq[hid:]
    f_u = jnp.concatenate(
        [plus(*kept_y(gwo0, a1, xo), ywo), plus(*kept_y(gwi0, b1), ywi[:hid], xwi)], axis=0
    )
    s3, c1, f_u, gk0 = fence(s3, c1, f_u, gk0)
    s_x = plus(gs2, s3)
    s_x, gk0 = fence(s_x, gk0)
    xs = over_x(s_x)
    s1 = core(gs1)
    zf = stage_z(f_u)
    grad_enc, gkv2, gkv3, gkv0, gkv1 = enc_grad(place, enc_states, gk1, gv1, gk0, gv0, c_0, c_1)
    gkv3, s1, small_got, *zf = fence(gkv3, s1, small_got, *zf)
    f_w = plus(*zf)
    bf = stage_z_back(f_w)
    k3, k1 = core(gkv3), core(gkv1)
    xs, f_w = fence(xs, f_w)
    small = small + small_got
    small_got = over_y(small)
    ys = sent_y(gs0, s1, xs)
    k3, small = fence(k3, small)
    xkv = over_x(plus(gkv2, k3))
    ys, xkv, k1, small_got = fence(ys, xkv, k1, small_got)
    zs = stage_z(plus(*kept_y(gs0, s1, xs), ys))
    qo_t, kv_t = (gqo0, c1, xqo), (gkv0, k1, xkv)
    yc = over_y(plus(*[jnp.where(y_is0, b_, a_) for a_, b_ in zip(qo_t, kv_t)]))
    small = small + small_got
    small_got = over_x(small)
    yc, small_got, *both = fence(yc, small_got, *zs, *bf)
    zs, bf = both[:rest_size], both[rest_size:]
    bs = stage_z_back(plus(*zs))
    zc = stage_z(plus(*[jnp.where(y_is0, a_, b_) for a_, b_ in zip(qo_t, kv_t)], yc))
    f_v = ordered_z(bf)
    f_f = over_y(f_v)
    small = small + small_got
    small_z = [small, *[swap(small, "dp", 2 * j) for j in range(1, rest_size)]]
    both = fence(*zc, *bs, *small_z)
    zc, bs, small_z = both[:rest_size], both[rest_size : 2 * rest_size], both[2 * rest_size :]
    bc = stage_z_back(plus(*zc))
    s_v = ordered_z(bs)
    s_f = over_y(s_v)
    small = sum_ordered(small_z)
    n_f = f_v.shape[0] // 2
    r_wo = ordered(f_v[:n_f], f_f[:n_f]).astype(f32)
    r_wi = ordered(f_v[n_f:], f_f[n_f:]).astype(f32)
    s_f, r_wo, r_wi, *bc = fence(s_f, r_wo, r_wi, *bc)
    c_v = ordered_z(bc)
    c_f = over_y(c_v)
    r_s = ordered(s_v, s_f)
    g_s = [r_s[i * w : (i + 1) * w].astype(f32) for i in range(4)]
    c_f, *g_s = fence(c_f, *g_s)
    c_w = [jnp.where(y_is0, a_, b_) for a_, b_ in ((c_v, c_f), (c_f, c_v))]
    g_c = [v[i * w : (i + 1) * w].astype(f32) for v in c_w for i in range(2)]
    grad_rel = lax.dynamic_slice(small[3], (t_index * heads * BUCKETS,), (heads * BUCKETS,)).reshape(heads, BUCKETS).T

    return (
        block_out,
        grad_in,
        grad_enc,
        small[0],
        g_s[0].T,
        g_s[1].T,
        g_s[2].T,
        g_s[3],
        grad_rel,
        small[1],
        g_c[0].T,
        g_c[2].T,
        g_c[3].T,
        g_c[1],
        small[2],
        r_wi,
        r_wo,
    )


def solution(mesh):
    tensor_size = mesh.shape["tensor"]
    dp_size = mesh.shape["dp"]
    both = P(("dp", "tensor"), None)
    col = P(None, "tensor")
    row = P("tensor", None)
    placed = (both, both, P("dp"), P("dp"), P(), col, col, col, row, col, P(), col, col, col, row, P(), col, row, both)
    outs = (both, both, both, P(), col, col, col, row, col, P(), col, col, col, row, P(), col, row)
    return jax.shard_map(
        lambda *a: local_program(tensor_size, dp_size, *a),
        mesh=mesh,
        in_specs=placed,
        out_specs=outs,
        check_vma=False,
    )
```

time: 545 us -> 391 us (0.72)
  waiting for transfers between devices: 215 us -> 107 us
  blocking collectives: 49.5 us -> 0 us
  Pallas kernels: 181 us -> 137 us
  starting transfers between devices: 47.9 us -> 67.8 us
  other arithmetic: 24.8 us -> 41.2 us
  local copies, waits for them, and re-layouts: 18.2 us -> 27 us
    ppermute x61 -> x62, waiting for transfers between devices: 215 us -> 107 us  [swap(): return lax.ppermute(v, axis, [(i, i ^ bit) for i in range(n)])]
    psum x1 -> x0, blocking collectives: 49.5 us -> none  [local_program(): small = lax.psum(small, ('dp', 'tensor'))]
    pallas_call x16 -> x11, Pallas kernels: 181 us -> 137 us  [call(): pl.pallas_call(kernel, out_shape=out_shape, grid=grid, scratch_shapes=scr...]
    ppermute x61 -> x62, starting transfers between devices: 47.9 us -> 67.8 us  [swap(): return lax.ppermute(v, axis, [(i, i ^ bit) for i in range(n)])]
    unnamed x78 -> x172, local copies, waits for them, and re-layouts: 9.38 us -> 22.6 us
    convert_element_type x29 -> x20, other arithmetic: 13.3 us -> 26.1 us  [the longest x17 21 us: plus(): return total.astype(bf16)]
  transfers between devices with their start and end apart: 61 -> 62, of which waited for: 31 -> 22; matrix products, arithmetic and copies ran while one was open for 7% -> 9% of each run, Pallas kernels for 33% -> 36%
where the time goes in v2:
time: 391 us; the launch traced here: 386 us
  Pallas kernels  137 us (35%)
  waiting for transfers between devices  107 us (27%)
  starting transfers between devices  67.8 us (17%)
  other arithmetic  41.2 us (11%)
  local copies, waits for them, and re-layouts  27 us (7%)
    pallas_call x11, Pallas kernels, call(): pl.pallas_call(kernel, out_shape=out_shape, grid=grid, scratch_shapes=scr...  137 us
    ppermute x62, waiting for transfers between devices, swap(): return lax.ppermute(v, axis, [(i, i ^ bit) for i in range(n)])  107 us
    ppermute x62, starting transfers between devices, swap(): return lax.ppermute(v, axis, [(i, i ^ bit) for i in range(n)])  67.8 us
    unnamed x172, local copies, waits for them, and re-layouts  22.6 us
    convert_element_type x17, other arithmetic, plus(): return total.astype(bf16)  21 us
  transfers between devices with their start and end apart: 62, of which 22 were waited for; matrix products, arithmetic and copies ran while one was open for 9% of the time, Pallas kernels for 36%

profile of v2, /device:TPU:0, one launch (start us, length us, event | category | flops | bytes accessed | tf_op | source)
XLA Modules:
  0.0 385.9 jit_solution(16261846244318525468)
XLA Ops:
  5.0 2.9 collective-permute-start.3
  12.7 6.5 %self_fwd.2 = (bf16[512,384]{1,0:T(8,128)(2,1)S(1)}, bf16[512,384]{1,0:T(8,128)(2,1)S(1)}, bf16[384,512]{1,0:T(8,128)(2,1)S(1)}, bf16[2,6,256,256]{3,2,1,0:T(8,1...) custom-call(s32[2]{0:T(128)S(1)} %pad_add_fusion.r_0_.r__0_.y_ref, ...), custom_call_target="tpu_custom_call" | custom-call | flops 1 | bytes 1 | tf_op jit(solution)/shard_map/self_fwd/pallas_call | solution.py:78
  21.6 4.7 %enc_kv.2 = (bf16[2048,384]{1,0:T(8,128)(2,1)S(1)}, bf16[2048,384]{1,0:T(8,128)(2,1)S(1)}) custom-call(s32[2]{0:T(128)S(1)} %pad_add_fusion.r_0_.r__0_.y_ref, bf16[2048,768]{1,0:T(8,128)(2,1)S(1)} %copy-done.3, bf16[768,768]{1,0:T(8,128)(2,1)S(1)} %pad_maximum_fusion.r_2_.r_4_.r__4_.rest_0_, bf16[768,768]{1,0:T(8,128)(2,1)S(1)} %collective-permute-done.2.r_3_.r_5_.r__5_.rest_1_), custom_call_target="tpu_custom_call" | custom-call | flops 1 | bytes 1 | tf_op jit(solution)/shard_map/enc_kv/pallas_call | solution.py:78
  28.6 5.7 %collective-permute-done.4 = f32[3,256]{1,0:T(4,128)} collective-permute-done((f32[3,256]{1,0:T(4,128)}, f32[3,256]{1,0:T(4,128)}, u32[]{:S(2)}, u32[]{:S(2)}) %collective-permute-start.4) | collective-permute-done | bytes 3104 | tf_op jit(solution)/shard_map/ppermute | solution.py:725
  40.0 7.2 %self_fwd.3 = (bf16[512,384]{1,0:T(8,128)(2,1)S(1)}, bf16[512,384]{1,0:T(8,128)(2,1)S(1)}, bf16[384,512]{1,0:T(8,128)(2,1)S(1)}, bf16[2,6,256,256]{3,2,1,0:T(8,1...) custom-call(s32[2]{0:T(128)S(1)} %pad_add_fusion.r_0_.r__0_.y_ref, ...), custom_call_target="tpu_custom_call" | custom-call | flops 1 | bytes 1 | tf_op jit(solution)/shard_map/self_fwd/pallas_call | solution.py:78
  54.9 8.9 %cross_fwd.2 = (bf16[512,384]{1,0:T(8,128)(2,1)S(1)}, f32[6,4,256]{2,1,0:T(4,128)S(1)}, bf16[384,512]{1,0:T(8,128)(2,1)S(1)}, f32[512,768]{1,0:T(8,128)S(1)}) custom-call(s32[2]{0:T(128)S(1)} %pad_add_fusion.r_0_.r__0_.y_ref, s32[8]{0:T(128)S(1)} %copy-done.51, bf16[512,768]{1,0:T(8,128)(2,1)S(1)} %get-tuple-element.246.r_2_.r__3_, ...), custom_call_target="tpu_custom_call" | custom-call | flops 1 | bytes 1 | tf_op jit(solution)/shard_map/cross_fwd/pallas_call | solution.py:78
  63.8 4.0 %collective-permute-done.8.r_3_.r_5_.r__7_.rest_3_ = bf16[384,768]{1,0:T(8,128)(2,1)S(1)} collective-permute-done((bf16[384,768]{1,0:T(8,128)(2,1)S(1)}, bf16[384,768]{1,0:T(8,128)(2,1)S(1)}, u32[]{:S(2)}, u32[]{:S(2)}) %collective-permute-start.8) | collective-permute-done | bytes 589856 | tf_op jit(solution)/shard_map/ppermute | solution.py:725
  69.9 4.5 %enc_kv.3 = (bf16[2048,384]{1,0:T(8,128)(2,1)S(1)}, bf16[2048,384]{1,0:T(8,128)(2,1)S(1)}) custom-call(s32[2]{0:T(128)S(1)} %pad_add_fusion.r_0_.r__0_.y_ref, bf16[2048,768]{1,0:T(8,128)(2,1)S(1)} %copy-done.4, bf16[384,768]{1,0:T(8,128)(2,1)S(1)} %collective-permute-done.7.r_2_.r_4_.r__6_.rest_2_, ...), custom_call_target="tpu_custom_call" | custom-call | flops 1 | bytes 1 | tf_op jit(solution)/shard_map/enc_kv/pallas_call | solution.py:78
  74.5 7.7 %collective-permute-done.11.r_3_.r_4_ = bf16[768,768]{1,0:T(8,128)(2,1)S(1)} collective-permute-done((bf16[768,768]{1,0:T(8,128)(2,1)S(1)}, bf16[768,768]{1,0:T(8,128)(2,1)S(1)}, u32[]{:S(2)}, u32[]{:S(2)}) %collective-permute-start.11) | collective-permute-done | bytes 1179680 | tf_op jit(solution)/shard_map/ppermute | solution.py:725
  82.7 9.0 %cross_fwd.3 = (bf16[512,384]{1,0:T(8,128)(2,1)S(1)}, f32[6,4,256]{2,1,0:T(4,128)S(1)}, bf16[384,512]{1,0:T(8,128)(2,1)S(1)}, f32[512,768]{1,0:T(8,128)S(1)}, bf16[512,768]{1,0:T(8,128)(2,1)S(1)}) custom-call(s32[2]{0:T(128)S(1)} %pad_add_fusion.r_0_.r__0_.y_ref, s32[8]{0:T(128)S(1)} %copy-done.51, bf16[512,768]{1,0:T(8,128)(2,1)S(1)} %get-tuple-element.246.r_2_.r__3_, ...), custom_call_target="tpu_custom_call" | custom-call | flops 1 | bytes 1 | tf_op jit(solution)/shard_map/cross_fwd/pallas_call | solution.py:78
  93.9 11.0 %ff.2 = (bf16[768,768]{1,0:T(8,128)(2,1)S(1)}, bf16[768,768]{1,0:T(8,128)(2,1)S(1)}, bf16[768,768]{1,0:T(8,128)(2,1)S(1)}, bf16[768,768]{1,0:T(8,128)(2,1)S(1)},...) custom-call(s32[2]{0:T(128)S(1)} %pad_add_fusion.r_0_.r__0_.y_ref, bf16[512,768]{1,0:T(8,128)(2,1)S(1)} %get-tuple-element.264.r_1_, ...), custom_call_target="tpu_custom_call" | custom-call | flops 1 | bytes 1 | tf_op jit(solution)/shard_map/ff/pallas_call | solution.py:78
  105.0 5.6 %collective-permute-done.15.r_5_.r_6_ = bf16[768,768]{1,0:T(8,128)(2,1)S(1)} collective-permute-done((bf16[768,768]{1,0:T(8,128)(2,1)S(1)}, bf16[768,768]{1,0:T(8,128)(2,1)S(1)}, u32[]{:S(2)}, u32[]{:S(2)}) %collective-permute-start.15) | collective-permute-done | bytes 1179680 | tf_op jit(solution)/shard_map/ppermute | solution.py:725
  113.4 12.7 %ff.3 = (bf16[768,768]{1,0:T(8,128)(2,1)S(1)}, bf16[768,768]{1,0:T(8,128)(2,1)S(1)}, bf16[768,768]{1,0:T(8,128)(2,1)}, bf16[768,768]{1,0:T(8,128)(2,1)}, bf16[51...) custom-call(s32[2]{0:T(128)S(1)} %pad_add_fusion.r_0_.r__0_.y_ref, ...), custom_call_target="tpu_custom_call" | custom-call | flops 1 | bytes 1 | tf_op jit(solution)/shard_map/ff/pallas_call | solution.py:78
  140.8 32.8 %cross_bwd.1 = (bf16[2048,384]{1,0:T(8,128)(2,1)}, bf16[2048,384]{1,0:T(8,128)(2,1)}, bf16[2048,384]{1,0:T(8,128)(2,1)}, bf16[2048,384]{1,0:T(8,128)(2,1)}, bf16...) custom-call(s32[2]{0:T(128)} %copy-done.46, ...), custom_call_target="tpu_custom_call" | custom-call | flops 1 | bytes 1 | tf_op jit(solution)/shard_map/cross_bwd/pallas_call | solution.py:78
  183.6 20.2 %self_bwd.1 = (bf16[768,768]{1,0:T(8,128)(2,1)}, bf16[768,768]{1,0:T(8,128)(2,1)}, bf16[768,768]{1,0:T(8,128)(2,1)}, bf16[768,768]{1,0:T(8,128)(2,1)}, f32[12,25...) custom-call(bf16[512,768]{1,0:T(8,128)(2,1)} %x_ref.1, f32[512,768]{1,0:T(8,128)} %copy-done.14, ...), custom_call_target="tpu_custom_call" | custom-call | flops 1 | bytes 1 | tf_op jit(solution)/shard_map/self_bwd/pallas_call | solution.py:78
  203.9 5.3 %collective-permute-done.24 = bf16[768,768]{1,0:T(8,128)(2,1)S(1)} collective-permute-done((bf16[768,768]{1,0:T(8,128)(2,1)}, bf16[768,768]{1,0:T(8,128)(2,1)S(1)}, u32[]{:S(2)}, u32[]{:S(2)}) %collective-permute-start.24) | collective-permute-done | bytes 1179680 | tf_op jit(solution)/shard_map/ppermute | solution.py:725
  224.6 19.6 %enc_grad.1 = (f32[2048,768]{1,0:T(8,128)}, bf16[384,768]{1,0:T(8,128)(2,1)}, bf16[384,768]{1,0:T(8,128)(2,1)}, bf16[384,768]{1,0:T(8,128)(2,1)}, bf16[384,768]{1,0:T(8,128)(2,1)}) custom-call(s32[2]{0:T(128)} %copy-done.46, bf16[2048,768]{1,0:T(8,128)(2,1)} %enc_ref.1, bf16[2048,384]{1,0:T(8,128)(2,1)} %get-tuple-element.348.gk1_ref, ...), custom_call_target="tpu_custom_call" | custom-call | flops 1 | bytes 1 | tf_op jit(solution)/shard_map/enc_grad/pallas_call | solution.py:78
  252.8 13.3 %collective-permute-done.38 = f32[4,768]{1,0:T(4,128)S(1)} collective-permute-done((f32[4,768]{1,0:T(4,128)S(1)}, f32[4,768]{1,0:T(4,128)S(1)}, u32[]{:S(2)}, u32[]{:S(2)}) %collective-permute-start.38) | collective-permute-done | bytes 12320 | tf_op jit(solution)/shard_map/ppermute | solution.py:725
  269.0 5.9 %collective-permute-start.44 = (bf16[192,768]{1,0:T(8,128)(2,1)S(1)}, bf16[192,768]{1,0:T(8,128)(2,1)S(1)}, u32[]{:S(2)}, u32[]{:S(2)}) collective-permute-start(bf16[192,768]{1,0:T(8,128)(2,1)S(1)} %add_convert_fusion.10), channel_id=1, source_target_pairs={{0,8},{4,12},{8,0},{12,4},{16,24},{20,28},{24,16},{28,20},{1,9},{5... | collective-permute-start | bytes 884744 | tf_op jit(solution)/shard_map/ppermute | solution.py:725
  280.6 7.0 %collective-permute-done.44 = bf16[192,768]{1,0:T(8,128)(2,1)S(1)} collective-permute-done((bf16[192,768]{1,0:T(8,128)(2,1)S(1)}, bf16[192,768]{1,0:T(8,128)(2,1)S(1)}, u32[]{:S(2)}, u32[]{:S(2)}) %collective-permute-start.44) | collective-permute-done | bytes 294944 | tf_op jit(solution)/shard_map/ppermute | solution.py:725
  288.0 12.3 %collective-permute-done.45 = bf16[192,768]{1,0:T(8,128)(2,1)S(1)} collective-permute-done((bf16[192,768]{1,0:T(8,128)(2,1)S(1)}, bf16[192,768]{1,0:T(8,128)(2,1)S(1)}, u32[]{:S(2)}, u32[]{:S(2)}) %collective-permute-start.45) | collective-permute-done | bytes 294944 | tf_op jit(solution)/shard_map/ppermute | solution.py:725
  300.2 5.3 %collective-permute-start.43 = (bf16[96,768]{1,0:T(8,128)(2,1)}, bf16[96,768]{1,0:T(8,128)(2,1)}, u32[]{:S(2)}, u32[]{:S(2)}) collective-permute-start(bf16[96,768]{1,0:T(8,128)(2,1)} %get-tuple-element.448), channel_id=1, source_target_pairs={{0,24},{4,28},{8,16},{12,20},{16,8},{20,12},{24,0},{28,4},{1,25},{... | collective-permute-start | bytes 442376 | tf_op jit(solution)/shard_map/ppermute | solution.py:725
  307.3 2.8 collective-permute-done.40
  310.1 3.1 collective-permute-done.42
  314.0 2.8 collective-permute-start.53
  331.2 6.5 %collective-permute-start.47 = (bf16[96,768]{1,0:T(8,128)(2,1)S(1)}, bf16[96,768]{1,0:T(8,128)(2,1)S(1)}, u32[]{:S(2)}, u32[]{:S(2)}) collective-permute-start(bf16[96,768]{1,0:T(8,128)(2,1)S(1)} %get-tuple-element.446), channel_id=1, source_target_pairs={{0,8},{4,12},{8,0},{12,4},{16,24},{20,28},{24,16},{28,20},{1,9},{5... | collective-permute-start | bytes 442376 | tf_op jit(solution)/shard_map/ppermute | solution.py:725
  341.2 9.2 %collective-permute-done.48 = bf16[96,768]{1,0:T(8,128)(2,1)S(1)} collective-permute-done((bf16[96,768]{1,0:T(8,128)(2,1)S(1)}, bf16[96,768]{1,0:T(8,128)(2,1)S(1)}, u32[]{:S(2)}, u32[]{:S(2)}) %collective-permute-start.48) | collective-permute-done | bytes 147488 | tf_op jit(solution)/shard_map/ppermute | solution.py:725
  350.5 3.8 collective-permute-start.58
  357.3 2.6 fusion
  360.0 3.1 collective-permute-done.59
  363.0 10.1 %collective-permute-done.56 = bf16[384,768]{1,0:T(8,128)(2,1)S(1)} collective-permute-done((bf16[384,768]{1,0:T(8,128)(2,1)S(1)}, bf16[384,768]{1,0:T(8,128)(2,1)S(1)}, u32[]{:S(2)}, u32[]{:S(2)}) %collective-permute-start.56) | collective-permute-done | bytes 589856 | tf_op jit(solution)/shard_map/ppermute | solution.py:725
  376.8 6.6 %collective-permute-done.61 = bf16[384,768]{1,0:T(8,128)(2,1)S(1)} collective-permute-done((bf16[384,768]{1,0:T(8,128)(2,1)S(1)}, bf16[384,768]{1,0:T(8,128)(2,1)S(1)}, u32[]{:S(2)}, u32[]{:S(2)}) %collective-permute-start.61) | collective-permute-done | bytes 589856 | tf_op jit(solution)/shard_map/ppermute | solution.py:725
  (339 shorter events, 120.9 us)
Async XLA Ops:
  4.9 16.6 %collective-permute-start.2 = (bf16[768,768]{1,0:T(8,128)(2,1)S(1)}, bf16[768,768]{1,0:T(8,128)(2,1)S(1)}, u32[]{:S(2)}, u32[]{:S(2)}) collective-permute-start(bf16[768,768]{1,0:T(8,128)(2,1)S(1)} %pad_maximum_fusion.r_2_.r_4_.r__4_.rest_0_), channel_id=1, source_target_pairs={{0,1},{1,0},{2,3},{3,2},{4,5},{5,4},{6,7},{7,6},{8,9},{9,8},{10,11... | collective-permute-start | bytes 3538952 | tf_op jit(solution)/shard_map/ppermute | solution.py:725
  5.0 29.3 %collective-permute-start.3 = (bf16[768,768]{1,0:T(8,128)(2,1)S(1)}, bf16[768,768]{1,0:T(8,128)(2,1)}, u32[]{:S(2)}, u32[]{:S(2)}) collective-permute-start(bf16[768,768]{1,0:T(8,128)(2,1)S(1)} %pad_maximum_fusion.1.r_4_.rest_0_), channel_id=1, source_target_pairs={{0,2},{1,3},{2,0},{3,1},{4,6},{5,7},{6,4},{7,5},{8,10},{9,11},{10,... | collective-permute-start | bytes 3538952 | tf_op jit(solution)/shard_map/ppermute | solution.py:725
  8.0 26.4 %collective-permute-start.4 = (f32[3,256]{1,0:T(4,128)}, f32[3,256]{1,0:T(4,128)}, u32[]{:S(2)}, u32[]{:S(2)}) collective-permute-start(f32[3,256]{1,0:T(4,128)} %convolution_bitcast_fusion), channel_id=1, source_target_pairs={{0,2},{1,3},{2,0},{3,1},{4,6},{5,7},{6,4},{7,5},{8,10},{9,11},{10,... | collective-permute-start | bytes 9224 | tf_op jit(solution)/shard_map/ppermute | solution.py:725
  35.8 16.4 %collective-permute-start.7 = (bf16[384,768]{1,0:T(8,128)(2,1)S(1)}, bf16[384,768]{1,0:T(8,128)(2,1)S(1)}, u32[]{:S(2)}, u32[]{:S(2)}) collective-permute-start(bf16[384,768]{1,0:T(8,128)(2,1)S(1)} %maximum_select_fusion.4), channel_id=1, source_target_pairs={{0,2},{1,3},{2,0},{3,1},{4,6},{5,7},{6,4},{7,5},{8,10},{9,11},{10,... | collective-permute-start | bytes 1769480 | tf_op jit(solution)/shard_map/ppermute | solution.py:725
  53.8 28.4 %collective-permute-start.11 = (bf16[768,768]{1,0:T(8,128)(2,1)S(1)}, bf16[768,768]{1,0:T(8,128)(2,1)S(1)}, u32[]{:S(2)}, u32[]{:S(2)}) collective-permute-start(bf16[768,768]{1,0:T(8,128)(2,1)S(1)} %broadcast_select_fusion), channel_id=1, source_target_pairs={{0,2},{1,3},{2,0},{3,1},{4,6},{5,7},{6,4},{7,5},{8,10},{9,11},{10,... | collective-permute-start | bytes 3538952 | tf_op jit(solution)/shard_map/ppermute | solution.py:725
  67.9 26.0 %collective-permute-start.12 = (bf16[768,768]{1,0:T(8,128)(2,1)S(1)}, bf16[768,768]{1,0:T(8,128)(2,1)S(1)}, u32[]{:S(2)}, u32[]{:S(2)}) collective-permute-start(bf16[768,768]{1,0:T(8,128)(2,1)S(1)} %copy-done.21), channel_id=1, source_target_pairs={{0,1},{1,0},{2,3},{3,2},{4,5},{5,4},{6,7},{7,6},{8,9},{9,8},{10,11... | collective-permute-start | bytes 3538952 | tf_op jit(solution)/shard_map/ppermute | solution.py:725
  68.4 25.5 %collective-permute-start.13 = (bf16[768,768]{1,0:T(8,128)(2,1)S(1)}, bf16[768,768]{1,0:T(8,128)(2,1)S(1)}, u32[]{:S(2)}, u32[]{:S(2)}) collective-permute-start(bf16[768,768]{1,0:T(8,128)(2,1)S(1)} %copy-done.22), channel_id=1, source_target_pairs={{0,1},{1,0},{2,3},{3,2},{4,5},{5,4},{6,7},{7,6},{8,9},{9,8},{10,11... | collective-permute-start | bytes 3538952 | tf_op jit(solution)/shard_map/ppermute | solution.py:725
  82.2 28.4 %collective-permute-start.15 = (bf16[768,768]{1,0:T(8,128)(2,1)S(1)}, bf16[768,768]{1,0:T(8,128)(2,1)S(1)}, u32[]{:S(2)}, u32[]{:S(2)}) collective-permute-start(bf16[768,768]{1,0:T(8,128)(2,1)S(1)} %collective-permute-done.11.r_3_.r_4_), channel_id=1, source_target_pairs={{0,4},{4,0},{8,12},{12,8},{16,20},{20,16},{24,28},{28,24},{1,5},{5... | collective-permute-start | bytes 3538952 | tf_op jit(solution)/shard_map/ppermute | solution.py:725
  110.6 17.6 %collective-permute-start.17 = (bf16[768,768]{1,0:T(8,128)(2,1)S(1)}, bf16[768,768]{1,0:T(8,128)(2,1)S(1)}, u32[]{:S(2)}, u32[]{:S(2)}) collective-permute-start(bf16[768,768]{1,0:T(8,128)(2,1)S(1)} %get-tuple-element.281), channel_id=1, source_target_pairs={{0,1},{1,0},{2,3},{3,2},{4,5},{5,4},{6,7},{7,6},{8,9},{9,8},{10,11... | collective-permute-start | bytes 3538952 | tf_op jit(solution)/shard_map/ppermute | solution.py:725
  111.1 17.1 %collective-permute-start.18 = (bf16[768,768]{1,0:T(8,128)(2,1)S(1)}, bf16[768,768]{1,0:T(8,128)(2,1)S(1)}, u32[]{:S(2)}, u32[]{:S(2)}) collective-permute-start(bf16[768,768]{1,0:T(8,128)(2,1)S(1)} %get-tuple-element.282), channel_id=1, source_target_pairs={{0,1},{1,0},{2,3},{3,2},{4,5},{5,4},{6,7},{7,6},{8,9},{9,8},{10,11... | collective-permute-start | bytes 3538952 | tf_op jit(solution)/shard_map/ppermute | solution.py:725
  139.1 34.5 %collective-permute-start.21 = (bf16[768,768]{1,0:T(8,128)(2,1)S(1)}, bf16[768,768]{1,0:T(8,128)(2,1)S(1)}, u32[]{:S(2)}, u32[]{:S(2)}) collective-permute-start(bf16[768,768]{1,0:T(8,128)(2,1)S(1)} %add_convert_fusion.1), channel_id=1, source_target_pairs={{0,2},{1,3},{2,0},{3,1},{4,6},{5,7},{6,4},{7,5},{8,10},{9,11},{10,... | collective-permute-start | bytes 3538952 | tf_op jit(solution)/shard_map/ppermute | solution.py:725
  140.2 34.4 %collective-permute-start.22 = (bf16[768,768]{1,0:T(8,128)(2,1)}, bf16[768,768]{1,0:T(8,128)(2,1)}, u32[]{:S(2)}, u32[]{:S(2)}) collective-permute-start(bf16[768,768]{1,0:T(8,128)(2,1)} %pad_maximum_fusion.2), channel_id=1, source_target_pairs={{0,4},{4,0},{8,12},{12,8},{16,20},{20,16},{24,28},{28,24},{1,5},{5... | collective-permute-start | bytes 3538952 | tf_op jit(solution)/shard_map/ppermute | solution.py:725
  180.6 28.6 %collective-permute-start.24 = (bf16[768,768]{1,0:T(8,128)(2,1)}, bf16[768,768]{1,0:T(8,128)(2,1)S(1)}, u32[]{:S(2)}, u32[]{:S(2)}) collective-permute-start(bf16[768,768]{1,0:T(8,128)(2,1)} %pad_maximum_fusion.3), channel_id=1, source_target_pairs={{0,2},{1,3},{2,0},{3,1},{4,6},{5,7},{6,4},{7,5},{8,10},{9,11},{10,... | collective-permute-start | bytes 3538952 | tf_op jit(solution)/shard_map/ppermute | solution.py:725
  181.6 22.3 %collective-permute-start.25 = (bf16[384,768]{1,0:T(8,128)(2,1)}, bf16[384,768]{1,0:T(8,128)(2,1)S(1)}, u32[]{:S(2)}, u32[]{:S(2)}) collective-permute-start(bf16[384,768]{1,0:T(8,128)(2,1)} %fusion.9), channel_id=1, source_target_pairs={{0,4},{4,0},{8,12},{12,8},{16,20},{20,16},{24,28},{28,24},{1,5},{5... | collective-permute-start | bytes 1769480 | tf_op jit(solution)/shard_map/ppermute | solution.py:725
  183.6 32.1 %collective-permute-start.27 = (bf16[384,768]{1,0:T(8,128)(2,1)}, bf16[384,768]{1,0:T(8,128)(2,1)S(1)}, u32[]{:S(2)}, u32[]{:S(2)}) collective-permute-start(bf16[384,768]{1,0:T(8,128)(2,1)} %get-tuple-element.352), channel_id=1, source_target_pairs={{0,1},{1,0},{2,3},{3,2},{4,5},{5,4},{6,7},{7,6},{8,9},{9,8},{10,11... | collective-permute-start | bytes 1769480 | tf_op jit(solution)/shard_map/ppermute | solution.py:725
  212.5 31.7 %collective-permute-start.28 = (bf16[768,768]{1,0:T(8,128)(2,1)}, bf16[768,768]{1,0:T(8,128)(2,1)}, u32[]{:S(2)}, u32[]{:S(2)}) collective-permute-start(bf16[768,768]{1,0:T(8,128)(2,1)} %get-tuple-element.366), channel_id=1, source_target_pairs={{0,1},{1,0},{2,3},{3,2},{4,5},{5,4},{6,7},{7,6},{8,9},{9,8},{10,11... | collective-permute-start | bytes 3538952 | tf_op jit(solution)/shard_map/ppermute | solution.py:725
  218.4 29.7 %collective-permute-start.33 = (bf16[768,768]{1,0:T(8,128)(2,1)S(1)}, bf16[768,768]{1,0:T(8,128)(2,1)S(1)}, u32[]{:S(2)}, u32[]{:S(2)}) collective-permute-start(bf16[768,768]{1,0:T(8,128)(2,1)S(1)} %add_convert_fusion), channel_id=1, source_target_pairs={{0,2},{1,3},{2,0},{3,1},{4,6},{5,7},{6,4},{7,5},{8,10},{9,11},{10,... | collective-permute-start | bytes 3538952 | tf_op jit(solution)/shard_map/ppermute | solution.py:725
  219.5 24.7 %collective-permute-start.30 = (bf16[192,768]{1,0:T(8,128)(2,1)S(1)}, bf16[192,768]{1,0:T(8,128)(2,1)S(1)}, u32[]{:S(2)}, u32[]{:S(2)}) collective-permute-start(bf16[192,768]{1,0:T(8,128)(2,1)S(1)} %get-tuple-element.438), channel_id=1, source_target_pairs={{0,8},{4,12},{8,0},{12,4},{16,24},{20,28},{24,16},{28,20},{1,9},{5... | collective-permute-start | bytes 884744 | tf_op jit(solution)/shard_map/ppermute | solution.py:725
  221.2 23.4 %collective-permute-start.31 = (bf16[192,768]{1,0:T(8,128)(2,1)S(1)}, bf16[192,768]{1,0:T(8,128)(2,1)S(1)}, u32[]{:S(2)}, u32[]{:S(2)}) collective-permute-start(bf16[192,768]{1,0:T(8,128)(2,1)S(1)} %get-tuple-element.437), channel_id=1, source_target_pairs={{0,16},{4,20},{8,24},{12,28},{16,0},{20,4},{24,8},{28,12},{1,17},{... | collective-permute-start | bytes 884744 | tf_op jit(solution)/shard_map/ppermute | solution.py:725
  224.3 20.2 %collective-permute-start.32 = (bf16[192,768]{1,0:T(8,128)(2,1)S(1)}, bf16[192,768]{1,0:T(8,128)(2,1)S(1)}, u32[]{:S(2)}, u32[]{:S(2)}) collective-permute-start(bf16[192,768]{1,0:T(8,128)(2,1)S(1)} %get-tuple-element.436), channel_id=1, source_target_pairs={{0,24},{4,28},{8,16},{12,20},{16,8},{20,12},{24,0},{28,4},{1,25},{... | collective-permute-start | bytes 884744 | tf_op jit(solution)/shard_map/ppermute | solution.py:725
  244.6 21.5 %collective-permute-start.37 = (bf16[384,768]{1,0:T(8,128)(2,1)}, bf16[384,768]{1,0:T(8,128)(2,1)S(1)}, u32[]{:S(2)}, u32[]{:S(2)}) collective-permute-start(bf16[384,768]{1,0:T(8,128)(2,1)} %get-tuple-element.383), channel_id=1, source_target_pairs={{0,1},{1,0},{2,3},{3,2},{4,5},{5,4},{6,7},{7,6},{8,9},{9,8},{10,11... | collective-permute-start | bytes 1769480 | tf_op jit(solution)/shard_map/ppermute | solution.py:725
  247.0 19.1 %collective-permute-start.36 = (bf16[384,768]{1,0:T(8,128)(2,1)S(1)}, bf16[384,768]{1,0:T(8,128)(2,1)S(1)}, u32[]{:S(2)}, u32[]{:S(2)}) collective-permute-start(bf16[384,768]{1,0:T(8,128)(2,1)S(1)} %add_convert_fusion.4), channel_id=1, source_target_pairs={{0,2},{1,3},{2,0},{3,1},{4,6},{5,7},{6,4},{7,5},{8,10},{9,11},{10,... | collective-permute-start | bytes 1769480 | tf_op jit(solution)/shard_map/ppermute | solution.py:725
  267.4 45.8 %collective-permute-start.39 = (bf16[384,768]{1,0:T(8,128)(2,1)}, bf16[384,768]{1,0:T(8,128)(2,1)}, u32[]{:S(2)}, u32[]{:S(2)}) collective-permute-start(bf16[384,768]{1,0:T(8,128)(2,1)} %add_convert_fusion.3), channel_id=1, source_target_pairs={{0,4},{4,0},{8,12},{12,8},{16,20},{20,16},{24,28},{28,24},{1,5},{5... | collective-permute-start | bytes 1769480 | tf_op jit(solution)/shard_map/ppermute | solution.py:725
  269.0 18.6 %collective-permute-start.44 = (bf16[192,768]{1,0:T(8,128)(2,1)S(1)}, bf16[192,768]{1,0:T(8,128)(2,1)S(1)}, u32[]{:S(2)}, u32[]{:S(2)}) collective-permute-start(bf16[192,768]{1,0:T(8,128)(2,1)S(1)} %add_convert_fusion.10), channel_id=1, source_target_pairs={{0,8},{4,12},{8,0},{12,4},{16,24},{20,28},{24,16},{28,20},{1,9},{5... | collective-permute-start | bytes 884744 | tf_op jit(solution)/shard_map/ppermute | solution.py:725
  274.9 25.4 %collective-permute-start.45 = (bf16[192,768]{1,0:T(8,128)(2,1)S(1)}, bf16[192,768]{1,0:T(8,128)(2,1)S(1)}, u32[]{:S(2)}, u32[]{:S(2)}) collective-permute-start(bf16[192,768]{1,0:T(8,128)(2,1)S(1)} %add_convert_fusion.10), channel_id=1, source_target_pairs={{0,16},{4,20},{8,24},{12,28},{16,0},{20,4},{24,8},{28,12},{1,17},{... | collective-permute-start | bytes 884744 | tf_op jit(solution)/shard_map/ppermute | solution.py:725
  275.9 29.7 %collective-permute-start.46 = (bf16[192,768]{1,0:T(8,128)(2,1)S(1)}, bf16[192,768]{1,0:T(8,128)(2,1)S(1)}, u32[]{:S(2)}, u32[]{:S(2)}) collective-permute-start(bf16[192,768]{1,0:T(8,128)(2,1)S(1)} %add_convert_fusion.10), channel_id=1, source_target_pairs={{0,24},{4,28},{8,16},{12,20},{16,8},{20,12},{24,0},{28,4},{1,25},{... | collective-permute-start | bytes 884744 | tf_op jit(solution)/shard_map/ppermute | solution.py:725
  279.6 30.6 %collective-permute-start.41 = (bf16[96,768]{1,0:T(8,128)(2,1)}, bf16[96,768]{1,0:T(8,128)(2,1)}, u32[]{:S(2)}, u32[]{:S(2)}) collective-permute-start(bf16[96,768]{1,0:T(8,128)(2,1)} %get-tuple-element.450), channel_id=1, source_target_pairs={{0,8},{4,12},{8,0},{12,4},{16,24},{20,28},{24,16},{28,20},{1,9},{5... | collective-permute-start | bytes 442376 | tf_op jit(solution)/shard_map/ppermute | solution.py:725
  287.6 25.7 %collective-permute-start.42 = (bf16[96,768]{1,0:T(8,128)(2,1)}, bf16[96,768]{1,0:T(8,128)(2,1)}, u32[]{:S(2)}, u32[]{:S(2)}) collective-permute-start(bf16[96,768]{1,0:T(8,128)(2,1)} %get-tuple-element.449), channel_id=1, source_target_pairs={{0,16},{4,20},{8,24},{12,28},{16,0},{20,4},{24,8},{28,12},{1,17},{... | collective-permute-start | bytes 442376 | tf_op jit(solution)/shard_map/ppermute | solution.py:725
  319.1 18.6 %collective-permute-start.50 = (bf16[96,768]{1,0:T(8,128)(2,1)S(1)}, bf16[96,768]{1,0:T(8,128)(2,1)S(1)}, u32[]{:S(2)}, u32[]{:S(2)}) collective-permute-start(bf16[96,768]{1,0:T(8,128)(2,1)S(1)} %add_convert_fusion.12), channel_id=1, source_target_pairs={{0,8},{4,12},{8,0},{12,4},{16,24},{20,28},{24,16},{28,20},{1,9},{5... | collective-permute-start | bytes 442376 | tf_op jit(solution)/shard_map/ppermute | solution.py:725
  321.1 16.5 %collective-permute-start.51 = (bf16[96,768]{1,0:T(8,128)(2,1)S(1)}, bf16[96,768]{1,0:T(8,128)(2,1)S(1)}, u32[]{:S(2)}, u32[]{:S(2)}) collective-permute-start(bf16[96,768]{1,0:T(8,128)(2,1)S(1)} %add_convert_fusion.12), channel_id=1, source_target_pairs={{0,16},{4,20},{8,24},{12,28},{16,0},{20,4},{24,8},{28,12},{1,17},{... | collective-permute-start | bytes 442376 | tf_op jit(solution)/shard_map/ppermute | solution.py:725
  323.2 34.0 %collective-permute-start.57 = (bf16[768,768]{1,0:T(8,128)(2,1)S(1)}, bf16[768,768]{1,0:T(8,128)(2,1)S(1)}, u32[]{:S(2)}, u32[]{:S(2)}) collective-permute-start(bf16[768,768]{1,0:T(8,128)(2,1)S(1)} %maximum_select_fusion), channel_id=1, source_target_pairs={{0,4},{4,0},{8,12},{12,8},{16,20},{20,16},{24,28},{28,24},{1,5},{5... | collective-permute-start | bytes 3538952 | tf_op jit(solution)/shard_map/ppermute | solution.py:725
  357.1 16.0 %collective-permute-start.56 = (bf16[384,768]{1,0:T(8,128)(2,1)S(1)}, bf16[384,768]{1,0:T(8,128)(2,1)S(1)}, u32[]{:S(2)}, u32[]{:S(2)}) collective-permute-start(bf16[384,768]{1,0:T(8,128)(2,1)S(1)} %maximum_select_fusion.5), channel_id=1, source_target_pairs={{0,4},{4,0},{8,12},{12,8},{16,20},{20,16},{24,28},{28,24},{1,5},{5... | collective-permute-start | bytes 1769480 | tf_op jit(solution)/shard_map/ppermute | solution.py:725
  (116 other events, 1226.9 us)

commit v3 on v2

--- a/solution.py
+++ b/solution.py
@@ -67,6 +67,11 @@
 def lane_half(shape, h):
     lane = lax.broadcasted_iota(jnp.int32, shape, 1)
     return (lane < DH) if h == 0 else (lane >= DH)
+
+
+def both_heads(rows):
+    zero = jnp.zeros_like(rows)
+    return jnp.concatenate([jnp.where(lane_half(rows.shape, h), rows, zero) for h in range(2)], axis=0)
 
 
 def call(kernel, out_shape, args, *, grid=(), in_specs=None, out_specs=None, scratch=(), flops=0, nbytes=0, trans=0, name=None, vmem=VMEM_CAP):
@@ -247,31 +252,31 @@
     lanes = pl.ds(pl.multiple_of(p * 2 * DH, 2 * DH), 2 * DH)
     qp = q_ref[tok, lanes]
     count = len_ref[y_ref[1] + b]
-    key = lax.broadcasted_iota(jnp.int32, (KEYS, LEN), 0)
-    queries = [jnp.where(lane_half(qp.shape, h), qp, jnp.zeros_like(qp)) for h in range(2)]
-    tops = [None, None]
+    key = lax.broadcasted_iota(jnp.int32, (KEYS, 2 * LEN), 0)
+    queries = both_heads(qp)
+    top = None
     for c in range(ENC // KEYS):
         part = slice(c * KEYS, (c + 1) * KEYS)
-        for h in range(2):
-            s = nt(k_ref[part], queries[h])
-            s = jnp.where(key < count - c * KEYS, s, masked_score)
-            s_ref[h, part] = s
-            top = jnp.max(s.reshape(KEYS // 8, 8, LEN), axis=0)
-            tops[h] = top if c == 0 else jnp.maximum(tops[h], top)
+        s = jnp.where(key < count - c * KEYS, nt(k_ref[part], queries), masked_score)
+        s_ref[part] = s
+        t = jnp.max(s.reshape(KEYS // 8, 8, 2 * LEN), axis=0)
+        top = t if c == 0 else jnp.maximum(top, t)
+    top = jnp.max(top, axis=0, keepdims=True)
+    total = None
+    for c in range(ENC // KEYS):
+        part = slice(c * KEYS, (c + 1) * KEYS)
+        e = jnp.exp(s_ref[part] - top)
+        t = jnp.sum(e.reshape(KEYS // 8, 8, 2 * LEN), axis=0)
+        total = t if c == 0 else total + t
+        e_ref[part] = e.astype(bf16)
+    r = 1.0 / jnp.sum(total, axis=0, keepdims=True)
+    mixed = tn(v_ref[...], e_ref[...]) * r
     outs = []
     for h in range(2):
-        top = jnp.max(tops[h], axis=0, keepdims=True)
-        total = None
-        for c in range(ENC // KEYS):
-            part = slice(c * KEYS, (c + 1) * KEYS)
-            e = jnp.exp(s_ref[h, part] - top)
-            t = jnp.sum(e.reshape(KEYS // 8, 8, LEN), axis=0)
-            total = t if c == 0 else total + t
-            e_ref[h, part] = e.astype(bf16)
-        r = 1.0 / jnp.sum(total, axis=0, keepdims=True)
-        r_ref[0, h : h + 1, :] = r
-        r_ref[0, 2 + h : 3 + h, :] = top
-        outs.append(tn(v_ref[...], e_ref[h])[h * DH : (h + 1) * DH] * r)
+        half = slice(h * LEN, (h + 1) * LEN)
+        r_ref[0, h : h + 1, :] = r[:, half]
+        r_ref[0, 2 + h : 3 + h, :] = top[:, half]
+        outs.append(mixed[h * DH : (h + 1) * DH, half])
     at_ref[lanes, tok] = jnp.concatenate(outs, axis=0).astype(bf16)
 
     @pl.when(step == pl.num_programs(0) - 1)
@@ -318,7 +323,7 @@
             whole(xin.shape),
         ],
         out_specs=tuple(specs),
-        scratch=[pltpu.VMEM((2, ENC, LEN), f32), pltpu.VMEM((2, ENC, LEN), bf16)],
+        scratch=[pltpu.VMEM((ENC, 2 * LEN), f32), pltpu.VMEM((ENC, 2 * LEN), bf16)],
         flops=3 * (2 * t * d * c * 2 + 2 * t * ENC * c * 2 * 2),
         nbytes=14 * 1024 * 1024,
         trans=t * ENC * (c // DH),
@@ -366,6 +371,7 @@
 
     n3 = n3_ref[...]
     gf = gf_ref[...]
+    kept = []
     for (get_wi, get_wo), gwi, gwo in zip(shards, (gwia, gwib), (gwoa, gwob)):
         wi, wo = get_wi(), get_wo()
         u = nn(n3, wi)
@@ -376,10 +382,12 @@
         r = (u * half).astype(bf16)
         slope = half + 0.5 * u * (1.0 - th * th) * (ROOT * (1.0 + (3.0 * CUBE) * u2))
         gu = (dh * slope).astype(bf16)
-        y_acc[...] += nn(r, wo)
-        gn_ref[...] += nt(gu, wi)
+        kept.append((r, wo, gu, wi))
         gwo[...] = tn(r, gf).astype(bf16)
         gwi[...] = nn(n3t_ref[...], gu).astype(bf16)
+    r, wo, gu, wi = [jnp.concatenate(v, axis=a) for v, a in zip(zip(*kept), (1, 0, 1, 1))]
+    y_acc[...] += nn(r, wo)
+    gn_ref[...] += nt(gu, wi)
 
     if last:
 
@@ -433,6 +441,7 @@
         flops=2 * 6 * 2 * t * d * hid * 2,
         nbytes=12 * 1024 * 1024,
         trans=2 * t * hid,
+        vmem=20 << 20,
         name="ff",
     )
 
@@ -469,7 +478,7 @@
     gk0, gv0, gk1, gv1, outs, gn_ref, gat_ref, gqt_ref, e_ref, gs_ref = *rest[16:20], rest[20:24], *rest[24:]
     w = outs[0].shape[0] // 2
     step = pl.program_id(0)
-    key = lax.broadcasted_iota(jnp.int32, (KEYS, LEN), 0)
+    key = lax.broadcasted_iota(jnp.int32, (KEYS, 2 * LEN), 0)
 
     def half(side, local, gk_ref, gv_ref):
         q_ref, k_ref, v_ref, r_ref, at_ref = sides[side]
@@ -486,7 +495,7 @@
         ga_t = gat_ref[lanes, tok]
         a_t = at_ref[lanes, tok]
         count = len_ref[y_ref[1] + b]
-        queries, grads, deltas = [], [], []
+        grads, deltas = [], []
         for h in range(2):
             part = slice(h * DH, (h + 1) * DH)
             gah = ga_t[part].astype(f32) * r_ref[0, h : h + 1, :]
@@ -494,21 +503,20 @@
             gah = gah.astype(bf16)
             zero = jnp.zeros_like(gah)
             grads.append(jnp.concatenate([gah, zero] if h == 0 else [zero, gah], axis=0))
-            queries.append(jnp.where(lane_half(qp.shape, h), qp, jnp.zeros_like(qp)))
+        grads = jnp.concatenate(grads, axis=1)
+        delta = jnp.concatenate(deltas, axis=1)
+        top = jnp.concatenate([r_ref[0, 2:3, :], r_ref[0, 3:4, :]], axis=1)
+        queries = both_heads(qp)
         for c in range(ENC // KEYS):
             part = slice(c * KEYS, (c + 1) * KEYS)
-            kc = k_ref[part]
-            vc = v_ref[part]
-            for h in range(2):
-                s = jnp.where(key < count - c * KEYS, nt(kc, queries[h]), masked_score)
-                e = jnp.exp(s - r_ref[0, 2 + h : 3 + h, :])
-                gs_ref[h, part] = (e * (nn(vc, grads[h]) - deltas[h])).astype(bf16)
-                e_ref[h, part] = e.astype(bf16)
-            gv_ref[part] = (nt(e_ref[0, part], grads[0]) + nt(e_ref[1, part], grads[1])).astype(bf16)
-            gk_ref[part] = (nn(gs_ref[0, part], queries[0]) + nn(gs_ref[1, part], queries[1])).astype(bf16)
-        k = k_ref[...]
-        gq = [tn(k, gs_ref[h])[h * DH : (h + 1) * DH] for h in range(2)]
-        gqt_ref[lanes, tok] = jnp.concatenate(gq, axis=0).astype(bf16)
+            s = jnp.where(key < count - c * KEYS, nt(k_ref[part], queries), masked_score)
+            e = jnp.exp(s - top)
+            gs_ref[part] = (e * (nn(v_ref[part], grads) - delta)).astype(bf16)
+            e_ref[part] = e.astype(bf16)
+        gv_ref[...] = nt(e_ref[...], grads).astype(bf16)
+        gk_ref[...] = nn(gs_ref[...], queries).astype(bf16)
+        gq = tn(k_ref[...], gs_ref[...])
+        gqt_ref[lanes, tok] = jnp.concatenate([gq[0:DH, 0:LEN], gq[DH:, LEN:]], axis=0).astype(bf16)
 
         @pl.when(local == steps - 1)
         def _():
@@ -564,8 +572,8 @@
         scratch=[
             pltpu.VMEM((c, t), bf16),
             pltpu.VMEM((c, t), bf16),
-            pltpu.VMEM((2, ENC, LEN), bf16),
-            pltpu.VMEM((2, ENC, LEN), bf16),
+            pltpu.VMEM((ENC, 2 * LEN), bf16),
+            pltpu.VMEM((ENC, 2 * LEN), bf16),
         ],
         vmem=BIG_VMEM,
         name="cross_bwd",
@@ -580,7 +588,8 @@
     step = pl.program_id(0)
     enc = enc_ref[...]
     grads = [g[...] for g in (gk1_ref, gv1_ref, gk0_ref, gv0_ref)]
-    out_ref[...] = (nn(grads[0], w1(0)) + nn(grads[1], w1(1))) + (nn(grads[2], w0(0)) + nn(grads[3], w0(1)))
+    rhs = jnp.concatenate([w1(0), w1(1), w0(0), w0(1)], axis=0)
+    out_ref[...] = nn(jnp.concatenate(grads, axis=1), rhs)
     terms = [tn(g, enc) for g in grads]
 
     @pl.when(step == 0)
@@ -765,11 +774,11 @@
     half = own_c.shape[0] // 2
     send_c, x_s = fence(jnp.where(y_is0, own_c[:half], own_c[half:]), x_s)
     x_c = over_x(send_c)
+    send_f, s_1[1], xp = fence(jnp.where(y_is0, ff_in, ff_out), s_1[1], xp)
+    x_f = over_x(send_f)
     out = self_fwd(True, place, dec_len, block_in, gains, s_1, bias1, xp)
     *out, x_c = fence(*out, x_c)
     fq1, fk1, fv1, fe1, fr1, fa1, x1, n1, n2 = out
-    send_f, x_c = fence(jnp.where(y_is0, ff_in, ff_out), x_c)
-    x_f = over_x(send_f)
     y_c, c_c = over_y(x_c), core(x_c)
     cq0, cr0, ca0, x2p = cross_fwd(False, place, enc_len, n2, gains, c_0, k0, v0, x1)
     x2p, y_c, c_c = fence(x2p, y_c, c_c)
@@ -849,16 +858,36 @@
     hid = gwi0.shape[0] // 2
     wi_x = plus(pick(gwi2, 2, y), pick(b3, 2, y), ywi[hid:])
     wo_y = plus(*[pick(v, 2, 1 - y) for v in (gwo0, a1, xo)])
-    wi_x, wo_y, c3, gn2 = fence(wi_x, wo_y, c3, gn2)
-    wq_x = jnp.concatenate([wi_x, plus(gqo2, c3)], axis=0)
-    wq_x, gn2 = fence(wq_x, gn2)
-    xwq, ywo = over_x(wq_x), over_y(wo_y)
+    wi_x, wo_y, c3, gk0 = fence(wi_x, wo_y, c3, gk0)
+    xwi, ywo = over_x(wi_x), over_y(wo_y)
+    qo_x, gk0 = fence(plus(gqo2, c3), gk0)
+    xqo = over_x(qo_x)
+    grad_enc, gkv2, gkv3, gkv0, gkv1 = enc_grad(place, enc_states, gk1, gv1, gk0, gv0, c_0, c_1)
+    gkv3, gn2, xwi, ywo = fence(gkv3, gn2, xwi, ywo)
+    k3, k1, c1 = core(gkv3), core(gkv1), core(gqo1)
+    f_u = jnp.concatenate(
+        [plus(*kept_y(gwo0, a1, xo), ywo), plus(*kept_y(gwi0, b1), ywi[:hid], xwi)], axis=0
+    )
+    f_u, k3, k1, gn2 = fence(f_u, k3, k1, gn2)
+    kv_x, gn2 = fence(plus(gkv2, k3), gn2)
+    xkv = over_x(kv_x)
+    zf = stage_z(f_u)
     out = self_bwd(
         block_in, x1, gx2, gn2, gains, n1, [*s_0, *s_1], (fq0, fk0, fv0, fe0, fr0, fa0), (fq1, fk1, fv1, fe1, fr1, fa1)
     )
-    *out, xwq, ywo = fence(*out, xwq, ywo)
     gs0, gs1, gs2, gs3, gd, gg2, gg1, grad_in = out
-    s3, c1 = core(gs3), core(gqo1)
+    gs0, gs3, gd, gg1, xqo, xkv, c1, *zf = fence(gs0, gs3, gd, gg1, xqo, xkv, c1, *zf)
+    s3 = core(gs3)
+    qo_t, kv_t = (gqo0, c1, xqo), (gkv0, k1, xkv)
+    c_y = plus(*[jnp.where(y_is0, b_, a_) for a_, b_ in zip(qo_t, kv_t)])
+    f_w = plus(*zf)
+    s3, c_y, f_w = fence(s3, c_y, f_w)
+    s_x = plus(gs2, s3)
+    s_x, c_y, f_w, gs1, gd, gg1 = fence(s_x, c_y, f_w, gs1, gd, gg1)
+    xs = over_x(s_x)
+    yc = over_y(c_y)
+    bf = stage_z_back(f_w)
+    s1 = core(gs1)
     flipped = jnp.asarray(np.ascontiguousarray(buckets[::-1]))
     grel = jnp.dot(gd, flipped, precision=lax.Precision.HIGHEST)
     grel = grel.reshape(tensor_size, heads * BUCKETS)
@@ -868,53 +897,39 @@
     grel = jnp.pad(grel.reshape(1, -1), ((0, 0), (0, d - grel.size)))
     small = jnp.concatenate([gg1, gg2, gg3, grel], axis=0)
     small_got = core(small)
-    xwi, xqo = xwq[:hid], xwq[hid:]
-    f_u = jnp.concatenate(
-        [plus(*kept_y(gwo0, a1, xo), ywo), plus(*kept_y(gwi0, b1), ywi[:hid], xwi)], axis=0
-    )
-    s3, c1, f_u, gk0 = fence(s3, c1, f_u, gk0)
-    s_x = plus(gs2, s3)
-    s_x, gk0 = fence(s_x, gk0)
-    xs = over_x(s_x)
-    s1 = core(gs1)
-    zf = stage_z(f_u)
-    grad_enc, gkv2, gkv3, gkv0, gkv1 = enc_grad(place, enc_states, gk1, gv1, gk0, gv0, c_0, c_1)
-    gkv3, s1, small_got, *zf = fence(gkv3, s1, small_got, *zf)
-    f_w = plus(*zf)
-    bf = stage_z_back(f_w)
-    k3, k1 = core(gkv3), core(gkv1)
-    xs, f_w = fence(xs, f_w)
+    yc, small_got, s1, xs, *bf = fence(yc, small_got, s1, xs, *bf)
+    ys = sent_y(gs0, s1, xs)
+    zc = stage_z(plus(*[jnp.where(y_is0, a_, b_) for a_, b_ in zip(qo_t, kv_t)], yc))
+    small = small + small_got
+    small_got = over_x(small)
+    f_v = ordered_z(bf)
+    ys, small_got, f_v, *zc = fence(ys, small_got, f_v, *zc)
+    zs = stage_z(plus(*kept_y(gs0, s1, xs), ys))
     small = small + small_got
     small_got = over_y(small)
-    ys = sent_y(gs0, s1, xs)
-    k3, small = fence(k3, small)
-    xkv = over_x(plus(gkv2, k3))
-    ys, xkv, k1, small_got = fence(ys, xkv, k1, small_got)
-    zs = stage_z(plus(*kept_y(gs0, s1, xs), ys))
-    qo_t, kv_t = (gqo0, c1, xqo), (gkv0, k1, xkv)
-    yc = over_y(plus(*[jnp.where(y_is0, b_, a_) for a_, b_ in zip(qo_t, kv_t)]))
+    f_y, small_got = fence(f_v, small_got)
+    f_f = over_y(f_y)
+    c_w = plus(*zc)
+    small_got, c_w, *zs = fence(small_got, c_w, *zs)
+    bc = stage_z_back(c_w)
+    bit = 2
     small = small + small_got
-    small_got = over_x(small)
-    yc, small_got, *both = fence(yc, small_got, *zs, *bf)
-    zs, bf = both[:rest_size], both[rest_size:]
+    small_got = swap(small, "dp", bit)
     bs = stage_z_back(plus(*zs))
-    zc = stage_z(plus(*[jnp.where(y_is0, a_, b_) for a_, b_ in zip(qo_t, kv_t)], yc))
-    f_v = ordered_z(bf)
-    f_f = over_y(f_v)
+    both = fence(small_got, *bs, *bc)
+    small_got, bs, bc = both[0], both[1 : 1 + rest_size], both[1 + rest_size :]
     small = small + small_got
-    small_z = [small, *[swap(small, "dp", 2 * j) for j in range(1, rest_size)]]
-    both = fence(*zc, *bs, *small_z)
-    zc, bs, small_z = both[:rest_size], both[rest_size : 2 * rest_size], both[2 * rest_size :]
-    bc = stage_z_back(plus(*zc))
+    while 2 * bit < dp_size:
+        bit *= 2
+        small = small + swap(small, "dp", bit)
+    c_v = ordered_z(bc)
+    c_f = over_y(c_v)
     s_v = ordered_z(bs)
     s_f = over_y(s_v)
-    small = sum_ordered(small_z)
     n_f = f_v.shape[0] // 2
     r_wo = ordered(f_v[:n_f], f_f[:n_f]).astype(f32)
     r_wi = ordered(f_v[n_f:], f_f[n_f:]).astype(f32)
-    s_f, r_wo, r_wi, *bc = fence(s_f, r_wo, r_wi, *bc)
-    c_v = ordered_z(bc)
-    c_f = over_y(c_v)
+    s_f, r_wo, r_wi = fence(s_f, r_wo, r_wi)
     r_s = ordered(s_v, s_f)
     g_s = [r_s[i * w : (i + 1) * w].astype(f32) for i in range(4)]
     c_f, *g_s = fence(c_f, *g_s)

time: 391 us -> 375 us (0.959)
  waiting for transfers between devices: 107 us -> 91 us
  Pallas kernels: 137 us -> 132 us
    ppermute x62, waiting for transfers between devices: 107 us -> 91 us  [swap(): return lax.ppermute(v, axis, [(i, i ^ bit) for i in range(n)])]
    pallas_call x11, Pallas kernels: 137 us -> 132 us  [call(): pl.pallas_call(kernel, out_shape=out_shape, grid=grid, scratch_shapes=scr...]
    ppermute x62, starting transfers between devices: 67.8 us -> 71.7 us  [swap(): return lax.ppermute(v, axis, [(i, i ^ bit) for i in range(n)])]
    unnamed x172 -> x162, local copies, waits for them, and re-layouts: 22.6 us -> 20.7 us
  transfers between devices with their start and end apart: 62 -> 62, of which waited for: 22 -> 23; matrix products, arithmetic and copies ran while one was open for 9% -> 11% of each run, Pallas kernels for 36% -> 36%
where the time goes in v3:
time: 375 us; the launch traced here: 369 us
  Pallas kernels  132 us (35%)
  waiting for transfers between devices  91 us (24%)
  starting transfers between devices  71.7 us (19%)
  other arithmetic  43.9 us (12%)
  local copies, waits for them, and re-layouts  26.3 us (7%)
    pallas_call x11, Pallas kernels, call(): pl.pallas_call(kernel, out_shape=out_shape, grid=grid, scratch_shapes=scr...  132 us
    ppermute x62, waiting for transfers between devices, swap(): return lax.ppermute(v, axis, [(i, i ^ bit) for i in range(n)])  91 us
    ppermute x62, starting transfers between devices, swap(): return lax.ppermute(v, axis, [(i, i ^ bit) for i in range(n)])  71.7 us
    convert_element_type x17, other arithmetic, plus(): return total.astype(bf16)  22 us
    unnamed x162, local copies, waits for them, and re-layouts  20.7 us
  transfers between devices with their start and end apart: 62, of which 23 were waited for; matrix products, arithmetic and copies ran while one was open for 11% of the time, Pallas kernels for 36%

profile of v3, /device:TPU:0, one launch (start us, length us, event | category | flops | bytes accessed | tf_op | source)
XLA Modules:
  0.0 369.2 jit_solution(13532423193125531147)
XLA Ops:
  5.0 2.9 collective-permute-start.3
  12.7 6.5 %self_fwd.2 = (bf16[512,384]{1,0:T(8,128)(2,1)S(1)}, bf16[512,384]{1,0:T(8,128)(2,1)S(1)}, bf16[384,512]{1,0:T(8,128)(2,1)S(1)}, bf16[2,6,256,256]{3,2,1,0:T(8,1...) custom-call(s32[2]{0:T(128)S(1)} %pad_add_fusion.r_0_.r__0_.y_ref, ...), custom_call_target="tpu_custom_call" | custom-call | flops 1 | bytes 1 | tf_op jit(solution)/shard_map/self_fwd/pallas_call | solution.py:83
  21.6 4.7 %enc_kv.2 = (bf16[2048,384]{1,0:T(8,128)(2,1)S(1)}, bf16[2048,384]{1,0:T(8,128)(2,1)S(1)}) custom-call(s32[2]{0:T(128)S(1)} %pad_add_fusion.r_0_.r__0_.y_ref, bf16[2048,768]{1,0:T(8,128)(2,1)S(1)} %copy-done.3, bf16[768,768]{1,0:T(8,128)(2,1)S(1)} %pad_maximum_fusion.r_2_.r_4_.r__4_.rest_0_, bf16[768,768]{1,0:T(8,128)(2,1)S(1)} %collective-permute-done.2.r_3_.r_5_.r__5_.rest_1_), custom_call_target="tpu_custom_call" | custom-call | flops 1 | bytes 1 | tf_op jit(solution)/shard_map/enc_kv/pallas_call | solution.py:83
  28.6 5.8 %collective-permute-done.4 = f32[3,256]{1,0:T(4,128)} collective-permute-done((f32[3,256]{1,0:T(4,128)}, f32[3,256]{1,0:T(4,128)}, u32[]{:S(2)}, u32[]{:S(2)}) %collective-permute-start.4) | collective-permute-done | bytes 3104 | tf_op jit(solution)/shard_map/ppermute | solution.py:734
  40.0 7.2 %self_fwd.3 = (bf16[512,384]{1,0:T(8,128)(2,1)S(1)}, bf16[512,384]{1,0:T(8,128)(2,1)S(1)}, bf16[384,512]{1,0:T(8,128)(2,1)S(1)}, bf16[2,6,256,256]{3,2,1,0:T(8,1...) custom-call(s32[2]{0:T(128)S(1)} %pad_add_fusion.r_0_.r__0_.y_ref, ...), custom_call_target="tpu_custom_call" | custom-call | flops 1 | bytes 1 | tf_op jit(solution)/shard_map/self_fwd/pallas_call | solution.py:83
  54.9 8.9 %cross_fwd.2 = (bf16[512,384]{1,0:T(8,128)(2,1)S(1)}, f32[6,4,256]{2,1,0:T(4,128)S(1)}, bf16[384,512]{1,0:T(8,128)(2,1)S(1)}, f32[512,768]{1,0:T(8,128)S(1)}) custom-call(s32[2]{0:T(128)S(1)} %pad_add_fusion.r_0_.r__0_.y_ref, s32[8]{0:T(128)S(1)} %copy-done.51, bf16[512,768]{1,0:T(8,128)(2,1)S(1)} %get-tuple-element.255.r_2_.r__3_, ...), custom_call_target="tpu_custom_call" | custom-call | flops 1 | bytes 1 | tf_op jit(solution)/shard_map/cross_fwd/pallas_call | solution.py:83
  69.1 4.6 %enc_kv.3 = (bf16[2048,384]{1,0:T(8,128)(2,1)S(1)}, bf16[2048,384]{1,0:T(8,128)(2,1)S(1)}) custom-call(s32[2]{0:T(128)S(1)} %pad_add_fusion.r_0_.r__0_.y_ref, bf16[2048,768]{1,0:T(8,128)(2,1)S(1)} %copy-done.4, bf16[384,768]{1,0:T(8,128)(2,1)S(1)} %collective-permute-done.7.r_2_.r_4_.r__6_.rest_2_, ...), custom_call_target="tpu_custom_call" | custom-call | flops 1 | bytes 1 | tf_op jit(solution)/shard_map/enc_kv/pallas_call | solution.py:83
  73.7 8.0 %collective-permute-done.11.r_3_.r_4_ = bf16[768,768]{1,0:T(8,128)(2,1)S(1)} collective-permute-done((bf16[768,768]{1,0:T(8,128)(2,1)S(1)}, bf16[768,768]{1,0:T(8,128)(2,1)S(1)}, u32[]{:S(2)}, u32[]{:S(2)}) %collective-permute-start.11) | collective-permute-done | bytes 1179680 | tf_op jit(solution)/shard_map/ppermute | solution.py:734
  82.0 9.1 %cross_fwd.3 = (bf16[512,384]{1,0:T(8,128)(2,1)S(1)}, f32[6,4,256]{2,1,0:T(4,128)S(1)}, bf16[384,512]{1,0:T(8,128)(2,1)S(1)}, f32[512,768]{1,0:T(8,128)S(1)}, bf16[512,768]{1,0:T(8,128)(2,1)S(1)}) custom-call(s32[2]{0:T(128)S(1)} %pad_add_fusion.r_0_.r__0_.y_ref, s32[8]{0:T(128)S(1)} %copy-done.51, bf16[512,768]{1,0:T(8,128)(2,1)S(1)} %get-tuple-element.255.r_2_.r__3_, ...), custom_call_target="tpu_custom_call" | custom-call | flops 1 | bytes 1 | tf_op jit(solution)/shard_map/cross_fwd/pallas_call | solution.py:83
  93.3 10.6 %ff.2 = (bf16[768,768]{1,0:T(8,128)(2,1)S(1)}, bf16[768,768]{1,0:T(8,128)(2,1)S(1)}, bf16[768,768]{1,0:T(8,128)(2,1)S(1)}, bf16[768,768]{1,0:T(8,128)(2,1)S(1)},...) custom-call(s32[2]{0:T(128)S(1)} %pad_add_fusion.r_0_.r__0_.y_ref, bf16[512,768]{1,0:T(8,128)(2,1)S(1)} %get-tuple-element.272.r_1_, ...), custom_call_target="tpu_custom_call" | custom-call | flops 1 | bytes 1 | tf_op jit(solution)/shard_map/ff/pallas_call | solution.py:83
  103.9 6.2 %collective-permute-done.15.r_5_.r_6_ = bf16[768,768]{1,0:T(8,128)(2,1)S(1)} collective-permute-done((bf16[768,768]{1,0:T(8,128)(2,1)S(1)}, bf16[768,768]{1,0:T(8,128)(2,1)S(1)}, u32[]{:S(2)}, u32[]{:S(2)}) %collective-permute-start.15) | collective-permute-done | bytes 1179680 | tf_op jit(solution)/shard_map/ppermute | solution.py:734
  113.0 12.4 %ff.3 = (bf16[768,768]{1,0:T(8,128)(2,1)S(1)}, bf16[768,768]{1,0:T(8,128)(2,1)S(1)}, bf16[768,768]{1,0:T(8,128)(2,1)}, bf16[768,768]{1,0:T(8,128)(2,1)}, bf16[51...) custom-call(s32[2]{0:T(128)S(1)} %pad_add_fusion.r_0_.r__0_.y_ref, ...), custom_call_target="tpu_custom_call" | custom-call | flops 1 | bytes 1 | tf_op jit(solution)/shard_map/ff/pallas_call | solution.py:83
  140.6 29.5 %cross_bwd.1 = (bf16[2048,384]{1,0:T(8,128)(2,1)}, bf16[2048,384]{1,0:T(8,128)(2,1)}, bf16[2048,384]{1,0:T(8,128)(2,1)}, bf16[2048,384]{1,0:T(8,128)(2,1)}, bf16...) custom-call(s32[2]{0:T(128)} %copy-done.46, ...), custom_call_target="tpu_custom_call" | custom-call | flops 1 | bytes 1 | tf_op jit(solution)/shard_map/cross_bwd/pallas_call | solution.py:83
  178.9 18.1 %enc_grad.1 = (f32[2048,768]{1,0:T(8,128)}, bf16[384,768]{1,0:T(8,128)(2,1)}, bf16[384,768]{1,0:T(8,128)(2,1)}, bf16[384,768]{1,0:T(8,128)(2,1)}, bf16[384,768]{1,0:T(8,128)(2,1)}) custom-call(s32[2]{0:T(128)} %copy-done.46, bf16[2048,768]{1,0:T(8,128)(2,1)} %enc_ref.1, bf16[2048,384]{1,0:T(8,128)(2,1)} %get-tuple-element.321.gk1_ref, ...), custom_call_target="tpu_custom_call" | custom-call | flops 1 | bytes 1 | tf_op jit(solution)/shard_map/enc_grad/pallas_call | solution.py:83
  206.6 2.6 collective-permute-start.32
  209.5 20.3 %self_bwd.1 = (bf16[768,768]{1,0:T(8,128)(2,1)}, bf16[768,768]{1,0:T(8,128)(2,1)}, bf16[768,768]{1,0:T(8,128)(2,1)}, bf16[768,768]{1,0:T(8,128)(2,1)}, f32[12,25...) custom-call(bf16[512,768]{1,0:T(8,128)(2,1)} %x_ref.1, f32[512,768]{1,0:T(8,128)} %copy-done.14, ...), custom_call_target="tpu_custom_call" | custom-call | flops 1 | bytes 1 | tf_op jit(solution)/shard_map/self_bwd/pallas_call | solution.py:83
  238.1 5.5 %collective-permute-start.39 = (bf16[192,768]{1,0:T(8,128)(2,1)}, bf16[192,768]{1,0:T(8,128)(2,1)}, u32[]{:S(2)}, u32[]{:S(2)}) collective-permute-start(bf16[192,768]{1,0:T(8,128)(2,1)} %add_convert_fusion.10), channel_id=1, source_target_pairs={{0,8},{4,12},{8,0},{12,4},{16,24},{20,28},{24,16},{28,20},{1,9},{5... | collective-permute-start | bytes 884744 | tf_op jit(solution)/shard_map/ppermute | solution.py:734
  248.2 3.2 collective-permute-done.39
  251.3 2.5 collective-permute-start.41
  253.8 17.0 %collective-permute-done.40 = bf16[192,768]{1,0:T(8,128)(2,1)} collective-permute-done((bf16[192,768]{1,0:T(8,128)(2,1)}, bf16[192,768]{1,0:T(8,128)(2,1)}, u32[]{:S(2)}, u32[]{:S(2)}) %collective-permute-start.40) | collective-permute-done | bytes 294944 | tf_op jit(solution)/shard_map/ppermute | solution.py:734
  272.5 6.2 %collective-permute-start.44 = (bf16[96,768]{1,0:T(8,128)(2,1)S(1)}, bf16[96,768]{1,0:T(8,128)(2,1)S(1)}, u32[]{:S(2)}, u32[]{:S(2)}) collective-permute-start(bf16[96,768]{1,0:T(8,128)(2,1)S(1)} %get-tuple-element.464), channel_id=1, source_target_pairs={{0,8},{4,12},{8,0},{12,4},{16,24},{20,28},{24,16},{28,20},{1,9},{5... | collective-permute-start | bytes 442376 | tf_op jit(solution)/shard_map/ppermute | solution.py:734
  288.1 4.3 %collective-permute-done.45 = bf16[96,768]{1,0:T(8,128)(2,1)S(1)} collective-permute-done((bf16[96,768]{1,0:T(8,128)(2,1)S(1)}, bf16[96,768]{1,0:T(8,128)(2,1)S(1)}, u32[]{:S(2)}, u32[]{:S(2)}) %collective-permute-start.45) | collective-permute-done | bytes 147488 | tf_op jit(solution)/shard_map/ppermute | solution.py:734
  292.4 4.6 %collective-permute-done.42 = bf16[384,768]{1,0:T(8,128)(2,1)S(1)} collective-permute-done((bf16[384,768]{1,0:T(8,128)(2,1)S(1)}, bf16[384,768]{1,0:T(8,128)(2,1)S(1)}, u32[]{:S(2)}, u32[]{:S(2)}) %collective-permute-start.42) | collective-permute-done | bytes 589856 | tf_op jit(solution)/shard_map/ppermute | solution.py:734
  306.2 6.8 %collective-permute-done.49 = bf16[96,768]{1,0:T(8,128)(2,1)S(1)} collective-permute-done((bf16[96,768]{1,0:T(8,128)(2,1)S(1)}, bf16[96,768]{1,0:T(8,128)(2,1)S(1)}, u32[]{:S(2)}, u32[]{:S(2)}) %collective-permute-start.49) | collective-permute-done | bytes 147488 | tf_op jit(solution)/shard_map/ppermute | solution.py:734
  319.6 3.4 collective-permute-done.51
  323.0 2.5 collective-permute-start.55
  326.8 5.6 %collective-permute-start.57 = (bf16[96,768]{1,0:T(8,128)(2,1)S(1)}, bf16[96,768]{1,0:T(8,128)(2,1)S(1)}, u32[]{:S(2)}, u32[]{:S(2)}) collective-permute-start(bf16[96,768]{1,0:T(8,128)(2,1)S(1)} %add_convert_fusion.12), channel_id=1, source_target_pairs={{0,24},{4,28},{8,16},{12,20},{16,8},{20,12},{24,0},{28,4},{1,25},{... | collective-permute-start | bytes 442376 | tf_op jit(solution)/shard_map/ppermute | solution.py:734
  332.5 8.1 %collective-permute-done.56 = bf16[96,768]{1,0:T(8,128)(2,1)S(1)} collective-permute-done((bf16[96,768]{1,0:T(8,128)(2,1)S(1)}, bf16[96,768]{1,0:T(8,128)(2,1)S(1)}, u32[]{:S(2)}, u32[]{:S(2)}) %collective-permute-start.56) | collective-permute-done | bytes 147488 | tf_op jit(solution)/shard_map/ppermute | solution.py:734
  341.6 3.1 collective-permute-start.58
  349.3 2.7 fusion
  352.0 5.4 %collective-permute-done.60 = bf16[384,768]{1,0:T(8,128)(2,1)} collective-permute-done((bf16[384,768]{1,0:T(8,128)(2,1)S(1)}, bf16[384,768]{1,0:T(8,128)(2,1)}, u32[]{:S(2)}, u32[]{:S(2)}) %collective-permute-start.60) | collective-permute-done | bytes 589856 | tf_op jit(solution)/shard_map/ppermute | solution.py:734
  360.5 5.2 %collective-permute-done.59 = bf16[384,768]{1,0:T(8,128)(2,1)} collective-permute-done((bf16[384,768]{1,0:T(8,128)(2,1)S(1)}, bf16[384,768]{1,0:T(8,128)(2,1)}, u32[]{:S(2)}, u32[]{:S(2)}) %collective-permute-start.59) | collective-permute-done | bytes 589856 | tf_op jit(solution)/shard_map/ppermute | solution.py:734
  (328 shorter events, 124.0 us)
Async XLA Ops:
  4.9 16.6 %collective-permute-start.2 = (bf16[768,768]{1,0:T(8,128)(2,1)S(1)}, bf16[768,768]{1,0:T(8,128)(2,1)S(1)}, u32[]{:S(2)}, u32[]{:S(2)}) collective-permute-start(bf16[768,768]{1,0:T(8,128)(2,1)S(1)} %pad_maximum_fusion.r_2_.r_4_.r__4_.rest_0_), channel_id=1, source_target_pairs={{0,1},{1,0},{2,3},{3,2},{4,5},{5,4},{6,7},{7,6},{8,9},{9,8},{10,11... | collective-permute-start | bytes 3538952 | tf_op jit(solution)/shard_map/ppermute | solution.py:734
  5.0 29.3 %collective-permute-start.3 = (bf16[768,768]{1,0:T(8,128)(2,1)S(1)}, bf16[768,768]{1,0:T(8,128)(2,1)}, u32[]{:S(2)}, u32[]{:S(2)}) collective-permute-start(bf16[768,768]{1,0:T(8,128)(2,1)S(1)} %pad_maximum_fusion.1.r_4_.rest_0_), channel_id=1, source_target_pairs={{0,2},{1,3},{2,0},{3,1},{4,6},{5,7},{6,4},{7,5},{8,10},{9,11},{10,... | collective-permute-start | bytes 3538952 | tf_op jit(solution)/shard_map/ppermute | solution.py:734
  8.0 26.4 %collective-permute-start.4 = (f32[3,256]{1,0:T(4,128)}, f32[3,256]{1,0:T(4,128)}, u32[]{:S(2)}, u32[]{:S(2)}) collective-permute-start(f32[3,256]{1,0:T(4,128)} %convolution_bitcast_fusion), channel_id=1, source_target_pairs={{0,2},{1,3},{2,0},{3,1},{4,6},{5,7},{6,4},{7,5},{8,10},{9,11},{10,... | collective-permute-start | bytes 9224 | tf_op jit(solution)/shard_map/ppermute | solution.py:734
  35.8 15.8 %collective-permute-start.7 = (bf16[384,768]{1,0:T(8,128)(2,1)S(1)}, bf16[384,768]{1,0:T(8,128)(2,1)S(1)}, u32[]{:S(2)}, u32[]{:S(2)}) collective-permute-start(bf16[384,768]{1,0:T(8,128)(2,1)S(1)} %maximum_select_fusion.4), channel_id=1, source_target_pairs={{0,2},{1,3},{2,0},{3,1},{4,6},{5,7},{6,4},{7,5},{8,10},{9,11},{10,... | collective-permute-start | bytes 1769480 | tf_op jit(solution)/shard_map/ppermute | solution.py:734
  51.6 15.4 %collective-permute-start.8 = (bf16[384,768]{1,0:T(8,128)(2,1)S(1)}, bf16[384,768]{1,0:T(8,128)(2,1)S(1)}, u32[]{:S(2)}, u32[]{:S(2)}) collective-permute-start(bf16[384,768]{1,0:T(8,128)(2,1)S(1)} %collective-permute-done.7.r_2_.r_4_.r__6_.rest_2_), channel_id=1, source_target_pairs={{0,4},{4,0},{8,12},{12,8},{16,20},{20,16},{24,28},{28,24},{1,5},{5... | collective-permute-start | bytes 1769480 | tf_op jit(solution)/shard_map/ppermute | solution.py:734
  53.4 28.4 %collective-permute-start.11 = (bf16[768,768]{1,0:T(8,128)(2,1)S(1)}, bf16[768,768]{1,0:T(8,128)(2,1)S(1)}, u32[]{:S(2)}, u32[]{:S(2)}) collective-permute-start(bf16[768,768]{1,0:T(8,128)(2,1)S(1)} %broadcast_select_fusion), channel_id=1, source_target_pairs={{0,2},{1,3},{2,0},{3,1},{4,6},{5,7},{6,4},{7,5},{8,10},{9,11},{10,... | collective-permute-start | bytes 3538952 | tf_op jit(solution)/shard_map/ppermute | solution.py:734
  67.1 26.2 %collective-permute-start.12 = (bf16[768,768]{1,0:T(8,128)(2,1)S(1)}, bf16[768,768]{1,0:T(8,128)(2,1)S(1)}, u32[]{:S(2)}, u32[]{:S(2)}) collective-permute-start(bf16[768,768]{1,0:T(8,128)(2,1)S(1)} %copy-done.21), channel_id=1, source_target_pairs={{0,1},{1,0},{2,3},{3,2},{4,5},{5,4},{6,7},{7,6},{8,9},{9,8},{10,11... | collective-permute-start | bytes 3538952 | tf_op jit(solution)/shard_map/ppermute | solution.py:734
  67.6 25.7 %collective-permute-start.13 = (bf16[768,768]{1,0:T(8,128)(2,1)S(1)}, bf16[768,768]{1,0:T(8,128)(2,1)S(1)}, u32[]{:S(2)}, u32[]{:S(2)}) collective-permute-start(bf16[768,768]{1,0:T(8,128)(2,1)S(1)} %copy-done.22), channel_id=1, source_target_pairs={{0,1},{1,0},{2,3},{3,2},{4,5},{5,4},{6,7},{7,6},{8,9},{9,8},{10,11... | collective-permute-start | bytes 3538952 | tf_op jit(solution)/shard_map/ppermute | solution.py:734
  81.8 28.4 %collective-permute-start.15 = (bf16[768,768]{1,0:T(8,128)(2,1)S(1)}, bf16[768,768]{1,0:T(8,128)(2,1)S(1)}, u32[]{:S(2)}, u32[]{:S(2)}) collective-permute-start(bf16[768,768]{1,0:T(8,128)(2,1)S(1)} %collective-permute-done.11.r_3_.r_4_), channel_id=1, source_target_pairs={{0,4},{4,0},{8,12},{12,8},{16,20},{20,16},{24,28},{28,24},{1,5},{5... | collective-permute-start | bytes 3538952 | tf_op jit(solution)/shard_map/ppermute | solution.py:734
  110.1 17.4 %collective-permute-start.17 = (bf16[768,768]{1,0:T(8,128)(2,1)S(1)}, bf16[768,768]{1,0:T(8,128)(2,1)S(1)}, u32[]{:S(2)}, u32[]{:S(2)}) collective-permute-start(bf16[768,768]{1,0:T(8,128)(2,1)S(1)} %get-tuple-element.289), channel_id=1, source_target_pairs={{0,1},{1,0},{2,3},{3,2},{4,5},{5,4},{6,7},{7,6},{8,9},{9,8},{10,11... | collective-permute-start | bytes 3538952 | tf_op jit(solution)/shard_map/ppermute | solution.py:734
  110.7 16.9 %collective-permute-start.18 = (bf16[768,768]{1,0:T(8,128)(2,1)S(1)}, bf16[768,768]{1,0:T(8,128)(2,1)S(1)}, u32[]{:S(2)}, u32[]{:S(2)}) collective-permute-start(bf16[768,768]{1,0:T(8,128)(2,1)S(1)} %get-tuple-element.290), channel_id=1, source_target_pairs={{0,1},{1,0},{2,3},{3,2},{4,5},{5,4},{6,7},{7,6},{8,9},{9,8},{10,11... | collective-permute-start | bytes 3538952 | tf_op jit(solution)/shard_map/ppermute | solution.py:734
  138.5 31.6 %collective-permute-start.21 = (bf16[768,768]{1,0:T(8,128)(2,1)S(1)}, bf16[768,768]{1,0:T(8,128)(2,1)S(1)}, u32[]{:S(2)}, u32[]{:S(2)}) collective-permute-start(bf16[768,768]{1,0:T(8,128)(2,1)S(1)} %add_convert_fusion.1), channel_id=1, source_target_pairs={{0,2},{1,3},{2,0},{3,1},{4,6},{5,7},{6,4},{7,5},{8,10},{9,11},{10,... | collective-permute-start | bytes 3538952 | tf_op jit(solution)/shard_map/ppermute | solution.py:734
  140.1 31.1 %collective-permute-start.22 = (bf16[768,768]{1,0:T(8,128)(2,1)}, bf16[768,768]{1,0:T(8,128)(2,1)}, u32[]{:S(2)}, u32[]{:S(2)}) collective-permute-start(bf16[768,768]{1,0:T(8,128)(2,1)} %pad_maximum_fusion.2), channel_id=1, source_target_pairs={{0,4},{4,0},{8,12},{12,8},{16,20},{20,16},{24,28},{28,24},{1,5},{5... | collective-permute-start | bytes 3538952 | tf_op jit(solution)/shard_map/ppermute | solution.py:734
  174.7 24.3 %collective-permute-start.24 = (bf16[384,768]{1,0:T(8,128)(2,1)S(1)}, bf16[384,768]{1,0:T(8,128)(2,1)}, u32[]{:S(2)}, u32[]{:S(2)}) collective-permute-start(bf16[384,768]{1,0:T(8,128)(2,1)S(1)} %fusion.6), channel_id=1, source_target_pairs={{0,2},{1,3},{2,0},{3,1},{4,6},{5,7},{6,4},{7,5},{8,10},{9,11},{10,... | collective-permute-start | bytes 1769480 | tf_op jit(solution)/shard_map/ppermute | solution.py:734
  175.1 23.9 %collective-permute-start.25 = (bf16[384,768]{1,0:T(8,128)(2,1)}, bf16[384,768]{1,0:T(8,128)(2,1)}, u32[]{:S(2)}, u32[]{:S(2)}) collective-permute-start(bf16[384,768]{1,0:T(8,128)(2,1)} %fusion.9), channel_id=1, source_target_pairs={{0,4},{4,0},{8,12},{12,8},{16,20},{20,16},{24,28},{28,24},{1,5},{5... | collective-permute-start | bytes 1769480 | tf_op jit(solution)/shard_map/ppermute | solution.py:734
  176.9 32.4 %collective-permute-start.30 = (bf16[384,768]{1,0:T(8,128)(2,1)}, bf16[384,768]{1,0:T(8,128)(2,1)S(1)}, u32[]{:S(2)}, u32[]{:S(2)}) collective-permute-start(bf16[384,768]{1,0:T(8,128)(2,1)} %get-tuple-element.369), channel_id=1, source_target_pairs={{0,1},{1,0},{2,3},{3,2},{4,5},{5,4},{6,7},{7,6},{8,9},{9,8},{10,11... | collective-permute-start | bytes 1769480 | tf_op jit(solution)/shard_map/ppermute | solution.py:734
  197.6 32.2 %collective-permute-start.28 = (bf16[384,768]{1,0:T(8,128)(2,1)}, bf16[384,768]{1,0:T(8,128)(2,1)S(1)}, u32[]{:S(2)}, u32[]{:S(2)}) collective-permute-start(bf16[384,768]{1,0:T(8,128)(2,1)} %add_convert_fusion.6), channel_id=1, source_target_pairs={{0,2},{1,3},{2,0},{3,1},{4,6},{5,7},{6,4},{7,5},{8,10},{9,11},{10,... | collective-permute-start | bytes 1769480 | tf_op jit(solution)/shard_map/ppermute | solution.py:734
  204.4 25.7 %collective-permute-start.29 = (bf16[384,768]{1,0:T(8,128)(2,1)}, bf16[384,768]{1,0:T(8,128)(2,1)S(1)}, u32[]{:S(2)}, u32[]{:S(2)}) collective-permute-start(bf16[384,768]{1,0:T(8,128)(2,1)} %add_convert_fusion.5), channel_id=1, source_target_pairs={{0,2},{1,3},{2,0},{3,1},{4,6},{5,7},{6,4},{7,5},{8,10},{9,11},{10,... | collective-permute-start | bytes 1769480 | tf_op jit(solution)/shard_map/ppermute | solution.py:734
  205.0 24.8 %collective-permute-start.31 = (bf16[192,768]{1,0:T(8,128)(2,1)S(1)}, bf16[192,768]{1,0:T(8,128)(2,1)S(1)}, u32[]{:S(2)}, u32[]{:S(2)}) collective-permute-start(bf16[192,768]{1,0:T(8,128)(2,1)S(1)} %get-tuple-element.452), channel_id=1, source_target_pairs={{0,8},{4,12},{8,0},{12,4},{16,24},{20,28},{24,16},{28,20},{1,9},{5... | collective-permute-start | bytes 884744 | tf_op jit(solution)/shard_map/ppermute | solution.py:734
  206.6 23.5 %collective-permute-start.32 = (bf16[192,768]{1,0:T(8,128)(2,1)S(1)}, bf16[192,768]{1,0:T(8,128)(2,1)S(1)}, u32[]{:S(2)}, u32[]{:S(2)}) collective-permute-start(bf16[192,768]{1,0:T(8,128)(2,1)S(1)} %get-tuple-element.451), channel_id=1, source_target_pairs={{0,16},{4,20},{8,24},{12,28},{16,0},{20,4},{24,8},{28,12},{1,17},{... | collective-permute-start | bytes 884744 | tf_op jit(solution)/shard_map/ppermute | solution.py:734
  209.2 20.9 %collective-permute-start.33 = (bf16[192,768]{1,0:T(8,128)(2,1)S(1)}, bf16[192,768]{1,0:T(8,128)(2,1)S(1)}, u32[]{:S(2)}, u32[]{:S(2)}) collective-permute-start(bf16[192,768]{1,0:T(8,128)(2,1)S(1)} %get-tuple-element.450), channel_id=1, source_target_pairs={{0,24},{4,28},{8,16},{12,20},{16,8},{20,12},{24,0},{28,4},{1,25},{... | collective-permute-start | bytes 884744 | tf_op jit(solution)/shard_map/ppermute | solution.py:734
  234.6 36.3 %collective-permute-start.37 = (bf16[768,768]{1,0:T(8,128)(2,1)}, bf16[768,768]{1,0:T(8,128)(2,1)}, u32[]{:S(2)}, u32[]{:S(2)}) collective-permute-start(bf16[768,768]{1,0:T(8,128)(2,1)} %get-tuple-element.393), channel_id=1, source_target_pairs={{0,1},{1,0},{2,3},{3,2},{4,5},{5,4},{6,7},{7,6},{8,9},{9,8},{10,11... | collective-permute-start | bytes 3538952 | tf_op jit(solution)/shard_map/ppermute | solution.py:734
  234.7 36.2 %collective-permute-start.38 = (bf16[768,768]{1,0:T(8,128)(2,1)}, bf16[768,768]{1,0:T(8,128)(2,1)}, u32[]{:S(2)}, u32[]{:S(2)}) collective-permute-start(bf16[768,768]{1,0:T(8,128)(2,1)} %add_convert_fusion), channel_id=1, source_target_pairs={{0,2},{1,3},{2,0},{3,1},{4,6},{5,7},{6,4},{7,5},{8,10},{9,11},{10,... | collective-permute-start | bytes 3538952 | tf_op jit(solution)/shard_map/ppermute | solution.py:734
  237.6 33.3 %collective-permute-start.35 = (bf16[384,768]{1,0:T(8,128)(2,1)}, bf16[384,768]{1,0:T(8,128)(2,1)}, u32[]{:S(2)}, u32[]{:S(2)}) collective-permute-start(bf16[384,768]{1,0:T(8,128)(2,1)} %add_convert_fusion.4), channel_id=1, source_target_pairs={{0,4},{4,0},{8,12},{12,8},{16,20},{20,16},{24,28},{28,24},{1,5},{5... | collective-permute-start | bytes 1769480 | tf_op jit(solution)/shard_map/ppermute | solution.py:734
  247.2 23.7 %collective-permute-start.40 = (bf16[192,768]{1,0:T(8,128)(2,1)}, bf16[192,768]{1,0:T(8,128)(2,1)}, u32[]{:S(2)}, u32[]{:S(2)}) collective-permute-start(bf16[192,768]{1,0:T(8,128)(2,1)} %add_convert_fusion.10), channel_id=1, source_target_pairs={{0,16},{4,20},{8,24},{12,28},{16,0},{20,4},{24,8},{28,12},{1,17},{... | collective-permute-start | bytes 884744 | tf_op jit(solution)/shard_map/ppermute | solution.py:734
  251.3 19.5 %collective-permute-start.41 = (bf16[192,768]{1,0:T(8,128)(2,1)}, bf16[192,768]{1,0:T(8,128)(2,1)}, u32[]{:S(2)}, u32[]{:S(2)}) collective-permute-start(bf16[192,768]{1,0:T(8,128)(2,1)} %add_convert_fusion.10), channel_id=1, source_target_pairs={{0,24},{4,28},{8,16},{12,20},{16,8},{20,12},{24,0},{28,4},{1,25},{... | collective-permute-start | bytes 884744 | tf_op jit(solution)/shard_map/ppermute | solution.py:734
  272.5 15.5 %collective-permute-start.44 = (bf16[96,768]{1,0:T(8,128)(2,1)S(1)}, bf16[96,768]{1,0:T(8,128)(2,1)S(1)}, u32[]{:S(2)}, u32[]{:S(2)}) collective-permute-start(bf16[96,768]{1,0:T(8,128)(2,1)S(1)} %get-tuple-element.464), channel_id=1, source_target_pairs={{0,8},{4,12},{8,0},{12,4},{16,24},{20,28},{24,16},{28,20},{1,9},{5... | collective-permute-start | bytes 442376 | tf_op jit(solution)/shard_map/ppermute | solution.py:734
  282.7 14.3 %collective-permute-start.42 = (bf16[384,768]{1,0:T(8,128)(2,1)S(1)}, bf16[384,768]{1,0:T(8,128)(2,1)S(1)}, u32[]{:S(2)}, u32[]{:S(2)}) collective-permute-start(bf16[384,768]{1,0:T(8,128)(2,1)S(1)} %fusion.10), channel_id=1, source_target_pairs={{0,4},{4,0},{8,12},{12,8},{16,20},{20,16},{24,28},{28,24},{1,5},{5... | collective-permute-start | bytes 1769480 | tf_op jit(solution)/shard_map/ppermute | solution.py:734
  304.8 43.2 %collective-permute-start.61 = (bf16[768,768]{1,0:T(8,128)(2,1)S(1)}, bf16[768,768]{1,0:T(8,128)(2,1)}, u32[]{:S(2)}, u32[]{:S(2)}) collective-permute-start(bf16[768,768]{1,0:T(8,128)(2,1)S(1)} %maximum_select_fusion), channel_id=1, source_target_pairs={{0,4},{4,0},{8,12},{12,8},{16,20},{20,16},{24,28},{28,24},{1,5},{5... | collective-permute-start | bytes 3538952 | tf_op jit(solution)/shard_map/ppermute | solution.py:734
  325.5 15.1 %collective-permute-start.56 = (bf16[96,768]{1,0:T(8,128)(2,1)S(1)}, bf16[96,768]{1,0:T(8,128)(2,1)S(1)}, u32[]{:S(2)}, u32[]{:S(2)}) collective-permute-start(bf16[96,768]{1,0:T(8,128)(2,1)S(1)} %add_convert_fusion.12), channel_id=1, source_target_pairs={{0,16},{4,20},{8,24},{12,28},{16,0},{20,4},{24,8},{28,12},{1,17},{... | collective-permute-start | bytes 442376 | tf_op jit(solution)/shard_map/ppermute | solution.py:734
  341.0 16.4 %collective-permute-start.60 = (bf16[384,768]{1,0:T(8,128)(2,1)S(1)}, bf16[384,768]{1,0:T(8,128)(2,1)}, u32[]{:S(2)}, u32[]{:S(2)}) collective-permute-start(bf16[384,768]{1,0:T(8,128)(2,1)S(1)} %maximum_select_fusion.8), channel_id=1, source_target_pairs={{0,4},{4,0},{8,12},{12,8},{16,20},{20,16},{24,28},{28,24},{1,5},{5... | collective-permute-start | bytes 1769480 | tf_op jit(solution)/shard_map/ppermute | solution.py:734
  345.0 20.6 %collective-permute-start.59 = (bf16[384,768]{1,0:T(8,128)(2,1)S(1)}, bf16[384,768]{1,0:T(8,128)(2,1)}, u32[]{:S(2)}, u32[]{:S(2)}) collective-permute-start(bf16[384,768]{1,0:T(8,128)(2,1)S(1)} %maximum_select_fusion.7), channel_id=1, source_target_pairs={{0,4},{4,0},{8,12},{12,8},{16,20},{20,16},{24,28},{28,24},{1,5},{5... | collective-permute-start | bytes 1769480 | tf_op jit(solution)/shard_map/ppermute | solution.py:734
  (111 other events, 1051.0 us)

commit v4 on v3

--- a/solution.py
+++ b/solution.py
@@ -136,31 +136,29 @@
     q_ref[...] = nt(n1, side_by_side(weights, 0)).astype(bf16)
     k_ref[...] = nt(n1, side_by_side(weights, 1)).astype(bf16)
     vt_ref[...] = nt(side_by_side(weights, 2), n1).astype(bf16)
-    key = lax.broadcasted_iota(jnp.int32, (LEN, LEN), 0)
-    query = lax.broadcasted_iota(jnp.int32, (LEN, LEN), 1)
+    key = lax.broadcasted_iota(jnp.int32, (LEN, 2 * LEN), 0)
+    query = lax.broadcasted_iota(jnp.int32, (LEN, 2 * LEN), 1)
+    query = jnp.where(query < LEN, query, query - LEN)
     for p in range(nh // 2):
         lanes = slice(p * 2 * DH, (p + 1) * 2 * DH)
         for h in range(2):
             row = jnp.broadcast_to(bias_ref[2 * p + h : 2 * p + h + 1, :], (LEN, LEN))
-            bs_ref[h] = pltpu.roll(row, 0, 1, stride=1, stride_axis=0)
+            bs_ref[:, h * LEN : (h + 1) * LEN] = pltpu.roll(row, 0, 1, stride=1, stride_axis=0)
         for b in range(nb):
             tok = slice(b * LEN, (b + 1) * LEN)
             allowed = (key <= query) & (key < len_ref[y_ref[1] + b])
-            kp = k_ref[tok, lanes]
-            qp = q_ref[tok, lanes]
+            s = nt(k_ref[tok, lanes], both_heads(q_ref[tok, lanes])) + bs_ref[...]
+            s = jnp.where(allowed, s, masked_score)
+            e = jnp.exp(s - jnp.max(s, axis=0, keepdims=True))
+            r = 1.0 / jnp.sum(e, axis=0, keepdims=True)
+            e = e.astype(bf16)
             outs = []
             for h in range(2):
                 head = 2 * p + h
-                qh = jnp.where(lane_half(qp.shape, h), qp, jnp.zeros_like(qp))
-                s = nt(kp, qh) + bs_ref[h]
-                s = jnp.where(allowed, s, masked_score)
-                top = jnp.max(s, axis=0, keepdims=True)
-                e = jnp.exp(s - top)
-                r = 1.0 / jnp.sum(e, axis=0, keepdims=True)
-                eb = e.astype(bf16)
-                e_ref[b, head] = eb
-                r_ref[b, head : head + 1, :] = r
-                outs.append(nn(vt_ref[head * DH : (head + 1) * DH, tok], eb) * r)
+                half = slice(h * LEN, (h + 1) * LEN)
+                e_ref[b, head] = e[:, half]
+                r_ref[b, head : head + 1, :] = r[:, half]
+                outs.append(nn(vt_ref[head * DH : (head + 1) * DH, tok], e[:, half]) * r[:, half])
             at_ref[lanes, tok] = jnp.concatenate(outs, axis=0).astype(bf16)
     mixed = tn(at_ref[...], side_by_side(weights, 3))
     if last:
@@ -197,7 +195,7 @@
         args,
         in_specs=[SMEM, SMEM] + [whole(a.shape) for a in args[2:]],
         out_specs=tuple(whole(o.shape) for o in outs),
-        scratch=[pltpu.VMEM((2, LEN, LEN), f32)],
+        scratch=[pltpu.VMEM((LEN, 2 * LEN), f32)],
         flops=flops * 3,
         nbytes=12 * 1024 * 1024,
         trans=t * LEN * nh,
@@ -446,32 +444,6 @@
     )
 
 
-def head_pair_back(k_t, v, q, ga, ga_t, a_t, es, rs, extra=None):
-    gv = None
-    gk = None
-    gq_t = []
-    for h in range(2):
-        part = slice(h * DH, (h + 1) * DH)
-        r = rs[h]
-        gah = ga_t[part].astype(f32) * r
-        delta = jnp.sum(gah * a_t[part].astype(f32), axis=0, keepdims=True)
-        gah = gah.astype(bf16)
-        zero = jnp.zeros_like(gah)
-        rhs = jnp.concatenate([gah, zero] if h == 0 else [zero, gah], axis=0)
-        gp = nn(v, rhs)
-        e = es[h]
-        gs = (e.astype(f32) * (gp - delta)).astype(bf16)
-        if extra is not None:
-            extra(h, gs)
-        keep = lane_half(q.shape, h)
-        term_v = nt(e, rhs)
-        term_k = nn(gs, jnp.where(keep, q, jnp.zeros_like(q)))
-        gv = term_v if gv is None else gv + term_v
-        gk = term_k if gk is None else gk + term_k
-        gq_t.append(nn(k_t[part], gs))
-    return jnp.concatenate(gq_t, axis=0).astype(bf16), gk.astype(bf16), gv.astype(bf16)
-
-
 def cross_bwd_kernel(pairs, steps, y_ref, len_ref, go_ref, n2_ref, *rest):
     weights = (pair_rows(y_ref, rest[0:2], False), pair_rows(y_ref, rest[2:6], True))
     sides = (rest[6:11], rest[11:16])
@@ -635,7 +607,15 @@
     weights = rest[0:4]
     sides = (rest[4:10], rest[10:16])
     outs = rest[16:20]
-    gd_ref, gg2_ref, gg1_ref, gi_ref, gat_ref, gqt_ref, gk_ref, gv_ref, gx1_ref = rest[20:]
+    gd_ref, gg2_ref, gg1_ref, gi_ref, gat_ref, gqt_ref, gk_ref, gv_ref, gx1_ref = rest[20:29]
+    held, sems = rest[29:37], rest[37]
+    arrivals = [
+        pltpu.make_async_copy(src, dst, sems.at[i]) for i, (src, dst) in enumerate(zip((*weights[0:2], *sides[0]), held))
+    ]
+    for copy in arrivals:
+        copy.start()
+    weights = (*held[0:2], *weights[2:4])
+    sides = (held[2:8], sides[1])
     w = outs[0].shape[0] // 4
     c = 2 * w
     nb = n1_ref.shape[0] // LEN
@@ -650,6 +630,9 @@
     n1 = n1_ref[...]
     gn = None
     for side in (1, 0):
+        if side == 0:
+            for copy in arrivals:
+                copy.wait()
         shards = weights[2 * side : 2 * side + 2]
         q_ref, k_ref, vt_ref, e_ref, r_ref, at_ref = sides[side]
         gat_ref[...] = nt(side_by_side(shards, 3), go).astype(bf16)
@@ -661,21 +644,26 @@
                 gd_ref[head : head + 1, :] = jnp.zeros((1, LEN), f32)
             for b in range(nb):
                 tok = slice(b * LEN, (b + 1) * LEN)
-
-                def extra(h, gs):
-                    turned = pltpu.roll(nn(gs, flip), 0, 1, stride=1, stride_axis=0)
+                grads, deltas = [], []
+                for h in range(2):
+                    rows = slice(lanes.start + h * DH, lanes.start + (h + 1) * DH)
+                    gah = gat_ref[rows, tok].astype(f32) * r_ref[b, 2 * p + h : 2 * p + h + 1, :]
+                    deltas.append(jnp.sum(gah * at_ref[rows, tok].astype(f32), axis=0, keepdims=True))
+                    gah = gah.astype(bf16)
+                    zero = jnp.zeros_like(gah)
+                    grads.append(jnp.concatenate([gah, zero] if h == 0 else [zero, gah], axis=0))
+                grads = jnp.concatenate(grads, axis=1)
+                delta = jnp.concatenate(deltas, axis=1)
+                e = jnp.concatenate([e_ref[b, 2 * p], e_ref[b, 2 * p + 1]], axis=1)
+                gs = (e.astype(f32) * (tn(vt_ref[lanes, tok], grads) - delta)).astype(bf16)
+                for h in range(2):
+                    turned = pltpu.roll(nn(gs[:, h * LEN : (h + 1) * LEN], flip), 0, 1, stride=1, stride_axis=0)
                     head = side * (c // DH) + 2 * p + h
                     gd_ref[head : head + 1, :] += jnp.sum(turned, axis=0, keepdims=True)
-
-                gq, gk, gv = head_pair_back(
-                    k_ref[tok, lanes].T, vt_ref[lanes, tok].T, q_ref[tok, lanes], None, gat_ref[lanes, tok], at_ref[lanes, tok],
-                    [e_ref[b, 2 * p], e_ref[b, 2 * p + 1]],
-                    [r_ref[b, 2 * p : 2 * p + 1, :], r_ref[b, 2 * p + 1 : 2 * p + 2, :]],
-                    extra,
-                )
-                gqt_ref[lanes, tok] = gq
-                gk_ref[tok, lanes] = gk
-                gv_ref[tok, lanes] = gv
+                gv_ref[tok, lanes] = nt(e, grads).astype(bf16)
+                gk_ref[tok, lanes] = nn(gs, both_heads(q_ref[tok, lanes])).astype(bf16)
+                gq = tn(k_ref[tok, lanes], gs)
+                gqt_ref[lanes, tok] = jnp.concatenate([gq[0:DH, 0:LEN], gq[DH:, LEN:]], axis=0).astype(bf16)
         gqt = gqt_ref[...]
         gk = gk_ref[...]
         gv = gv_ref[...]
@@ -695,6 +683,7 @@
 def self_bwd(x, x1, gx2, gn2, g, n1, weights, side0, side1):
     t, d = x1.shape
     c = weights[0].shape[0] // 2
+    late = pl.BlockSpec(memory_space=pl.ANY)
     args = [x, x1, gx2, gn2, g, n1, *weights, *side0, *side1]
     outs = [jax.ShapeDtypeStruct((2 * c, d), bf16)] * 4 + [
         jax.ShapeDtypeStruct((2 * c // DH, LEN), f32),
@@ -706,7 +695,11 @@
         self_bwd_kernel,
         tuple(outs),
         args,
-        in_specs=[whole(a.shape) for a in args],
+        in_specs=[whole(a.shape) for a in args[:6]]
+        + [late] * 2
+        + [whole(a.shape) for a in weights[2:4]]
+        + [late] * 6
+        + [whole(a.shape) for a in side1],
         out_specs=tuple(whole(o.shape) for o in outs),
         scratch=[
             pltpu.VMEM((c, t), bf16),
@@ -714,7 +707,9 @@
             pltpu.VMEM((t, c), bf16),
             pltpu.VMEM((t, c), bf16),
             pltpu.VMEM((t, d), f32),
-        ],
+        ]
+        + [pltpu.VMEM(a.shape, a.dtype) for a in (*weights[0:2], *side0)]
+        + [pltpu.SemaphoreType.DMA((8,))],
         vmem=BIG_VMEM,
         name="self_bwd",
     )
@@ -758,7 +753,6 @@
     rel_own = jnp.dot(rel_table.astype(f32).T, jnp.asarray(buckets.T), precision=lax.Precision.HIGHEST)
     rel_x = over_x(rel_own)
     own_s = jnp.concatenate([self_query.T, self_key.T, self_value.T, self_out], axis=0)
-    own_s, rel_own = fence(own_s, rel_own)
     x_s = over_x(own_s)
     s_0 = [own_s, core(own_s)]
     bias0 = jnp.concatenate([rel_own, core(rel_own)], axis=0)
@@ -813,6 +807,20 @@
     def kept_y(*vals):
         return [pick(v, 2, y) for v in vals]
 
+    z_bits = [1 << i for i in range(1, dp_size.bit_length() - 1)]
+
+    def reversed_bits(i):
+        return sum(((i >> a) & 1) << (len(z_bits) - 1 - a) for a in range(len(z_bits)))
+
+    def stage_z_reversed(v):
+        return [pick(v, rest_size, reversed_bits(m))] + [
+            swap(pick(v, rest_size, reversed_bits(m ^ j)), "dp", 2 * j) for j in range(1, rest_size)
+        ]
+
+    def in_order(v, got, bit):
+        low = d_bit(bit) == 0
+        return jnp.where(low, jnp.concatenate([v, got], axis=0), jnp.concatenate([got, v], axis=0))
+
     def sum_ordered(parts):
         while len(parts) > 1:
             parts = [a + b for a, b in zip(parts[0::2], parts[1::2])]
@@ -871,7 +879,7 @@
     f_u, k3, k1, gn2 = fence(f_u, k3, k1, gn2)
     kv_x, gn2 = fence(plus(gkv2, k3), gn2)
     xkv = over_x(kv_x)
-    zf = stage_z(f_u)
+    zf = stage_z_reversed(f_u)
     out = self_bwd(
         block_in, x1, gx2, gn2, gains, n1, [*s_0, *s_1], (fq0, fk0, fv0, fe0, fr0, fa0), (fq1, fk1, fv1, fe1, fr1, fa1)
     )
@@ -886,7 +894,9 @@
     s_x, c_y, f_w, gs1, gd, gg1 = fence(s_x, c_y, f_w, gs1, gd, gg1)
     xs = over_x(s_x)
     yc = over_y(c_y)
-    bf = stage_z_back(f_w)
+    for bit in z_bits[:1:-1]:
+        f_w = in_order(f_w, swap(f_w, "dp", bit), bit)
+    f_got = swap(f_w, "dp", z_bits[1])
     s1 = core(gs1)
     flipped = jnp.asarray(np.ascontiguousarray(buckets[::-1]))
     grel = jnp.dot(gd, flipped, precision=lax.Precision.HIGHEST)
@@ -897,20 +907,21 @@
     grel = jnp.pad(grel.reshape(1, -1), ((0, 0), (0, d - grel.size)))
     small = jnp.concatenate([gg1, gg2, gg3, grel], axis=0)
     small_got = core(small)
-    yc, small_got, s1, xs, *bf = fence(yc, small_got, s1, xs, *bf)
+    yc, small_got, s1, xs, f_got = fence(yc, small_got, s1, xs, f_got)
     ys = sent_y(gs0, s1, xs)
     zc = stage_z(plus(*[jnp.where(y_is0, a_, b_) for a_, b_ in zip(qo_t, kv_t)], yc))
     small = small + small_got
     small_got = over_x(small)
-    f_v = ordered_z(bf)
-    ys, small_got, f_v, *zc = fence(ys, small_got, f_v, *zc)
+    f_w = in_order(f_w, f_got, z_bits[1])
+    f_got = swap(f_w, "dp", 2)
+    ys, small_got, *zc = fence(ys, small_got, *zc)
     zs = stage_z(plus(*kept_y(gs0, s1, xs), ys))
     small = small + small_got
     small_got = over_y(small)
-    f_y, small_got = fence(f_v, small_got)
-    f_f = over_y(f_y)
     c_w = plus(*zc)
-    small_got, c_w, *zs = fence(small_got, c_w, *zs)
+    small_got, c_w, f_got, *zs = fence(small_got, c_w, f_got, *zs)
+    f_v = in_order(f_w, f_got, 2)
+    f_f = over_y(f_v)
     bc = stage_z_back(c_w)
     bit = 2
     small = small + small_got

time: 375 us -> 365 us (0.973)
  starting transfers between devices: 71.7 us -> 63.1 us
  waiting for transfers between devices: 91 us -> 97 us
  Pallas kernels: 132 us -> 127 us
    ppermute x62 -> x61, starting transfers between devices: 71.7 us -> 63.1 us  [swap(): return lax.ppermute(v, axis, [(i, i ^ bit) for i in range(n)])]
    ppermute x62 -> x61, waiting for transfers between devices: 91 us -> 97 us  [swap(): return lax.ppermute(v, axis, [(i, i ^ bit) for i in range(n)])]
    pallas_call x11, Pallas kernels: 132 us -> 127 us  [call(): pl.pallas_call(kernel, out_shape=out_shape, grid=grid, scratch_shapes=scr...]
    unnamed x162 -> x164, local copies, waits for them, and re-layouts: 20.7 us -> 20.7 us
  transfers between devices with their start and end apart: 62 -> 61, of which waited for: 23 -> 25; matrix products, arithmetic and copies ran while one was open for 11% -> 11% of each run, Pallas kernels for 36% -> 35%
where the time goes in v4:
time: 365 us; the launch traced here: 360 us
  Pallas kernels  127 us (35%)
  waiting for transfers between devices  97 us (27%)
  starting transfers between devices  63.1 us (17%)
  other arithmetic  43.2 us (12%)
  local copies, waits for them, and re-layouts  25.7 us (7%)
    pallas_call x11, Pallas kernels, call(): pl.pallas_call(kernel, out_shape=out_shape, grid=grid, scratch_shapes=scr...  127 us
    ppermute x61, waiting for transfers between devices, swap(): return lax.ppermute(v, axis, [(i, i ^ bit) for i in range(n)])  97 us
    ppermute x61, starting transfers between devices, swap(): return lax.ppermute(v, axis, [(i, i ^ bit) for i in range(n)])  63.1 us
    convert_element_type x17, other arithmetic, plus(): return total.astype(bf16)  22.2 us
    unnamed x164, local copies, waits for them, and re-layouts  20.7 us
  transfers between devices with their start and end apart: 61, of which 25 were waited for; matrix products, arithmetic and copies ran while one was open for 11% of the time, Pallas kernels for 35%

profile of v4, /device:TPU:0, one launch (start us, length us, event | category | flops | bytes accessed | tf_op | source)
XLA Modules:
  0.0 360.1 jit_solution(10895383468007507823)
XLA Ops:
  2.9 2.9 collective-permute-start.3
  11.9 5.2 %self_fwd.2 = (bf16[512,384]{1,0:T(8,128)(2,1)S(1)}, bf16[512,384]{1,0:T(8,128)(2,1)S(1)}, bf16[384,512]{1,0:T(8,128)(2,1)S(1)}, bf16[2,6,256,256]{3,2,1,0:T(8,1...) custom-call(s32[2]{0:T(128)S(1)} %pad_add_fusion.r_0_.r__0_.y_ref, ...), custom_call_target="tpu_custom_call" | custom-call | flops 1 | bytes 1 | tf_op jit(solution)/shard_map/self_fwd/pallas_call | solution.py:83
  19.4 4.8 %enc_kv.2 = (bf16[2048,384]{1,0:T(8,128)(2,1)S(1)}, bf16[2048,384]{1,0:T(8,128)(2,1)S(1)}) custom-call(s32[2]{0:T(128)S(1)} %pad_add_fusion.r_0_.r__0_.y_ref, bf16[2048,768]{1,0:T(8,128)(2,1)S(1)} %copy-done.3, bf16[768,768]{1,0:T(8,128)(2,1)S(1)} %pad_maximum_fusion.r_2_.r_4_.r__4_.rest_0_, bf16[768,768]{1,0:T(8,128)(2,1)S(1)} %collective-permute-done.2.r_3_.r_5_.r__5_.rest_1_), custom_call_target="tpu_custom_call" | custom-call | flops 1 | bytes 1 | tf_op jit(solution)/shard_map/enc_kv/pallas_call | solution.py:83
  26.6 5.7 %collective-permute-done.4 = f32[3,256]{1,0:T(4,128)} collective-permute-done((f32[3,256]{1,0:T(4,128)}, f32[3,256]{1,0:T(4,128)}, u32[]{:S(2)}, u32[]{:S(2)}) %collective-permute-start.4) | collective-permute-done | bytes 3104 | tf_op jit(solution)/shard_map/ppermute | solution.py:729
  37.9 5.9 %self_fwd.3 = (bf16[512,384]{1,0:T(8,128)(2,1)S(1)}, bf16[512,384]{1,0:T(8,128)(2,1)S(1)}, bf16[384,512]{1,0:T(8,128)(2,1)S(1)}, bf16[2,6,256,256]{3,2,1,0:T(8,1...) custom-call(s32[2]{0:T(128)S(1)} %pad_add_fusion.r_0_.r__0_.y_ref, ...), custom_call_target="tpu_custom_call" | custom-call | flops 1 | bytes 1 | tf_op jit(solution)/shard_map/self_fwd/pallas_call | solution.py:83
  52.8 8.9 %cross_fwd.2 = (bf16[512,384]{1,0:T(8,128)(2,1)S(1)}, f32[6,4,256]{2,1,0:T(4,128)S(1)}, bf16[384,512]{1,0:T(8,128)(2,1)S(1)}, f32[512,768]{1,0:T(8,128)S(1)}) custom-call(s32[2]{0:T(128)S(1)} %pad_add_fusion.r_0_.r__0_.y_ref, s32[8]{0:T(128)S(1)} %copy-done.51, bf16[512,768]{1,0:T(8,128)(2,1)S(1)} %get-tuple-element.246.r_2_.r__3_, ...), custom_call_target="tpu_custom_call" | custom-call | flops 1 | bytes 1 | tf_op jit(solution)/shard_map/cross_fwd/pallas_call | solution.py:83
  66.5 4.6 %enc_kv.3 = (bf16[2048,384]{1,0:T(8,128)(2,1)S(1)}, bf16[2048,384]{1,0:T(8,128)(2,1)S(1)}) custom-call(s32[2]{0:T(128)S(1)} %pad_add_fusion.r_0_.r__0_.y_ref, bf16[2048,768]{1,0:T(8,128)(2,1)S(1)} %copy-done.4, bf16[384,768]{1,0:T(8,128)(2,1)S(1)} %collective-permute-done.7.r_2_.r_4_.r__6_.rest_2_, ...), custom_call_target="tpu_custom_call" | custom-call | flops 1 | bytes 1 | tf_op jit(solution)/shard_map/enc_kv/pallas_call | solution.py:83
  71.2 8.5 %collective-permute-done.11.r_3_.r_4_ = bf16[768,768]{1,0:T(8,128)(2,1)S(1)} collective-permute-done((bf16[768,768]{1,0:T(8,128)(2,1)S(1)}, bf16[768,768]{1,0:T(8,128)(2,1)S(1)}, u32[]{:S(2)}, u32[]{:S(2)}) %collective-permute-start.11) | collective-permute-done | bytes 1179680 | tf_op jit(solution)/shard_map/ppermute | solution.py:729
  79.9 9.1 %cross_fwd.3 = (bf16[512,384]{1,0:T(8,128)(2,1)S(1)}, f32[6,4,256]{2,1,0:T(4,128)S(1)}, bf16[384,512]{1,0:T(8,128)(2,1)S(1)}, f32[512,768]{1,0:T(8,128)S(1)}, bf16[512,768]{1,0:T(8,128)(2,1)S(1)}) custom-call(s32[2]{0:T(128)S(1)} %pad_add_fusion.r_0_.r__0_.y_ref, s32[8]{0:T(128)S(1)} %copy-done.51, bf16[512,768]{1,0:T(8,128)(2,1)S(1)} %get-tuple-element.246.r_2_.r__3_, ...), custom_call_target="tpu_custom_call" | custom-call | flops 1 | bytes 1 | tf_op jit(solution)/shard_map/cross_fwd/pallas_call | solution.py:83
  91.2 10.9 %ff.2 = (bf16[768,768]{1,0:T(8,128)(2,1)S(1)}, bf16[768,768]{1,0:T(8,128)(2,1)S(1)}, bf16[768,768]{1,0:T(8,128)(2,1)S(1)}, bf16[768,768]{1,0:T(8,128)(2,1)S(1)},...) custom-call(s32[2]{0:T(128)S(1)} %pad_add_fusion.r_0_.r__0_.y_ref, bf16[512,768]{1,0:T(8,128)(2,1)S(1)} %get-tuple-element.263.r_1_, ...), custom_call_target="tpu_custom_call" | custom-call | flops 1 | bytes 1 | tf_op jit(solution)/shard_map/ff/pallas_call | solution.py:83
  102.1 5.9 %collective-permute-done.15.r_5_.r_6_ = bf16[768,768]{1,0:T(8,128)(2,1)S(1)} collective-permute-done((bf16[768,768]{1,0:T(8,128)(2,1)S(1)}, bf16[768,768]{1,0:T(8,128)(2,1)S(1)}, u32[]{:S(2)}, u32[]{:S(2)}) %collective-permute-start.15) | collective-permute-done | bytes 1179680 | tf_op jit(solution)/shard_map/ppermute | solution.py:729
  110.9 12.4 %ff.3 = (bf16[768,768]{1,0:T(8,128)(2,1)S(1)}, bf16[768,768]{1,0:T(8,128)(2,1)S(1)}, bf16[768,768]{1,0:T(8,128)(2,1)}, bf16[768,768]{1,0:T(8,128)(2,1)}, bf16[51...) custom-call(s32[2]{0:T(128)S(1)} %pad_add_fusion.r_0_.r__0_.y_ref, ...), custom_call_target="tpu_custom_call" | custom-call | flops 1 | bytes 1 | tf_op jit(solution)/shard_map/ff/pallas_call | solution.py:83
  138.5 29.3 %cross_bwd.1 = (bf16[2048,384]{1,0:T(8,128)(2,1)}, bf16[2048,384]{1,0:T(8,128)(2,1)}, bf16[2048,384]{1,0:T(8,128)(2,1)}, bf16[2048,384]{1,0:T(8,128)(2,1)}, bf16...) custom-call(s32[2]{0:T(128)} %copy-done.46, ...), custom_call_target="tpu_custom_call" | custom-call | flops 1 | bytes 1 | tf_op jit(solution)/shard_map/cross_bwd/pallas_call | solution.py:83
  176.6 18.1 %enc_grad.1 = (f32[2048,768]{1,0:T(8,128)}, bf16[384,768]{1,0:T(8,128)(2,1)}, bf16[384,768]{1,0:T(8,128)(2,1)}, bf16[384,768]{1,0:T(8,128)(2,1)}, bf16[384,768]{1,0:T(8,128)(2,1)}) custom-call(s32[2]{0:T(128)} %copy-done.46, bf16[2048,768]{1,0:T(8,128)(2,1)} %enc_ref.1, bf16[2048,384]{1,0:T(8,128)(2,1)} %get-tuple-element.312.gk1_ref, ...), custom_call_target="tpu_custom_call" | custom-call | flops 1 | bytes 1 | tf_op jit(solution)/shard_map/enc_grad/pallas_call | solution.py:83
  204.4 2.6 collective-permute-start.32
  207.2 18.2 %self_bwd.1 = (bf16[768,768]{1,0:T(8,128)(2,1)}, bf16[768,768]{1,0:T(8,128)(2,1)}, bf16[768,768]{1,0:T(8,128)(2,1)}, bf16[768,768]{1,0:T(8,128)(2,1)}, f32[12,25...) custom-call(bf16[512,768]{1,0:T(8,128)(2,1)} %x_ref.1, f32[512,768]{1,0:T(8,128)} %copy-done.14, ...), custom_call_target="tpu_custom_call" | custom-call | flops 1 | bytes 1 | tf_op jit(solution)/shard_map/self_bwd/pallas_call | solution.py:83
  225.5 2.4 collective-permute-done.32
  235.9 6.5 %collective-permute-start.39 = (bf16[192,768]{1,0:T(8,128)(2,1)}, bf16[192,768]{1,0:T(8,128)(2,1)}, u32[]{:S(2)}, u32[]{:S(2)}) collective-permute-start(bf16[192,768]{1,0:T(8,128)(2,1)} %add_convert_fusion.10), channel_id=1, source_target_pairs={{0,16},{4,20},{8,24},{12,28},{16,0},{20,4},{24,8},{28,12},{1,17},{... | collective-permute-start | bytes 884744 | tf_op jit(solution)/shard_map/ppermute | solution.py:729
  246.7 9.3 %collective-permute-done.39 = bf16[192,768]{1,0:T(8,128)(2,1)} collective-permute-done((bf16[192,768]{1,0:T(8,128)(2,1)}, bf16[192,768]{1,0:T(8,128)(2,1)}, u32[]{:S(2)}, u32[]{:S(2)}) %collective-permute-start.39) | collective-permute-done | bytes 294944 | tf_op jit(solution)/shard_map/ppermute | solution.py:729
  256.0 5.0 %collective-permute-done.38 = bf16[768,768]{1,0:T(8,128)(2,1)} collective-permute-done((bf16[768,768]{1,0:T(8,128)(2,1)}, bf16[768,768]{1,0:T(8,128)(2,1)}, u32[]{:S(2)}, u32[]{:S(2)}) %collective-permute-start.38) | collective-permute-done | bytes 1179680 | tf_op jit(solution)/shard_map/ppermute | solution.py:729
  265.0 5.6 %collective-permute-start.42 = (bf16[96,768]{1,0:T(8,128)(2,1)S(1)}, bf16[96,768]{1,0:T(8,128)(2,1)S(1)}, u32[]{:S(2)}, u32[]{:S(2)}) collective-permute-start(bf16[96,768]{1,0:T(8,128)(2,1)S(1)} %get-tuple-element.450), channel_id=1, source_target_pairs={{0,8},{4,12},{8,0},{12,4},{16,24},{20,28},{24,16},{28,20},{1,9},{5... | collective-permute-start | bytes 442376 | tf_op jit(solution)/shard_map/ppermute | solution.py:729
  277.8 6.3 %collective-permute-done.43 = bf16[96,768]{1,0:T(8,128)(2,1)S(1)} collective-permute-done((bf16[96,768]{1,0:T(8,128)(2,1)S(1)}, bf16[96,768]{1,0:T(8,128)(2,1)S(1)}, u32[]{:S(2)}, u32[]{:S(2)}) %collective-permute-start.43) | collective-permute-done | bytes 147488 | tf_op jit(solution)/shard_map/ppermute | solution.py:729
  292.1 6.7 %collective-permute-done.46 = bf16[384,768]{1,0:T(8,128)(2,1)S(1)} collective-permute-done((bf16[384,768]{1,0:T(8,128)(2,1)S(1)}, bf16[384,768]{1,0:T(8,128)(2,1)S(1)}, u32[]{:S(2)}, u32[]{:S(2)}) %collective-permute-start.46) | collective-permute-done | bytes 589856 | tf_op jit(solution)/shard_map/ppermute | solution.py:729
  298.8 2.5 collective-permute-done.47
  301.3 3.1 collective-permute-done.49
  311.2 3.2 collective-permute-done.50
  314.4 2.5 collective-permute-start.54
  316.9 4.1 %collective-permute-done.52 = bf16[96,768]{1,0:T(8,128)(2,1)S(1)} collective-permute-done((bf16[96,768]{1,0:T(8,128)(2,1)S(1)}, bf16[96,768]{1,0:T(8,128)(2,1)S(1)}, u32[]{:S(2)}, u32[]{:S(2)}) %collective-permute-start.52) | collective-permute-done | bytes 147488 | tf_op jit(solution)/shard_map/ppermute | solution.py:729
  322.6 9.2 %collective-permute-done.55 = bf16[96,768]{1,0:T(8,128)(2,1)S(1)} collective-permute-done((bf16[96,768]{1,0:T(8,128)(2,1)S(1)}, bf16[96,768]{1,0:T(8,128)(2,1)S(1)}, u32[]{:S(2)}, u32[]{:S(2)}) %collective-permute-start.55) | collective-permute-done | bytes 147488 | tf_op jit(solution)/shard_map/ppermute | solution.py:729
  340.0 2.7 fusion
  342.7 5.9 %collective-permute-done.59 = bf16[384,768]{1,0:T(8,128)(2,1)} collective-permute-done((bf16[384,768]{1,0:T(8,128)(2,1)S(1)}, bf16[384,768]{1,0:T(8,128)(2,1)}, u32[]{:S(2)}, u32[]{:S(2)}) %collective-permute-start.59) | collective-permute-done | bytes 589856 | tf_op jit(solution)/shard_map/ppermute | solution.py:729
  351.6 4.9 %collective-permute-done.58 = bf16[384,768]{1,0:T(8,128)(2,1)} collective-permute-done((bf16[384,768]{1,0:T(8,128)(2,1)S(1)}, bf16[384,768]{1,0:T(8,128)(2,1)}, u32[]{:S(2)}, u32[]{:S(2)}) %collective-permute-start.58) | collective-permute-done | bytes 589856 | tf_op jit(solution)/shard_map/ppermute | solution.py:729
  (327 shorter events, 125.2 us)
Async XLA Ops:
  2.8 16.6 %collective-permute-start.2 = (bf16[768,768]{1,0:T(8,128)(2,1)S(1)}, bf16[768,768]{1,0:T(8,128)(2,1)S(1)}, u32[]{:S(2)}, u32[]{:S(2)}) collective-permute-start(bf16[768,768]{1,0:T(8,128)(2,1)S(1)} %pad_maximum_fusion.r_2_.r_4_.r__4_.rest_0_), channel_id=1, source_target_pairs={{0,1},{1,0},{2,3},{3,2},{4,5},{5,4},{6,7},{7,6},{8,9},{9,8},{10,11... | collective-permute-start | bytes 3538952 | tf_op jit(solution)/shard_map/ppermute | solution.py:729
  2.9 29.3 %collective-permute-start.3 = (bf16[768,768]{1,0:T(8,128)(2,1)S(1)}, bf16[768,768]{1,0:T(8,128)(2,1)}, u32[]{:S(2)}, u32[]{:S(2)}) collective-permute-start(bf16[768,768]{1,0:T(8,128)(2,1)S(1)} %pad_maximum_fusion.1.r_4_.rest_0_), channel_id=1, source_target_pairs={{0,2},{1,3},{2,0},{3,1},{4,6},{5,7},{6,4},{7,5},{8,10},{9,11},{10,... | collective-permute-start | bytes 3538952 | tf_op jit(solution)/shard_map/ppermute | solution.py:729
  6.6 25.7 %collective-permute-start.4 = (f32[3,256]{1,0:T(4,128)}, f32[3,256]{1,0:T(4,128)}, u32[]{:S(2)}, u32[]{:S(2)}) collective-permute-start(f32[3,256]{1,0:T(4,128)} %convolution_bitcast_fusion), channel_id=1, source_target_pairs={{0,2},{1,3},{2,0},{3,1},{4,6},{5,7},{6,4},{7,5},{8,10},{9,11},{10,... | collective-permute-start | bytes 9224 | tf_op jit(solution)/shard_map/ppermute | solution.py:729
  33.7 15.8 %collective-permute-start.7 = (bf16[384,768]{1,0:T(8,128)(2,1)S(1)}, bf16[384,768]{1,0:T(8,128)(2,1)S(1)}, u32[]{:S(2)}, u32[]{:S(2)}) collective-permute-start(bf16[384,768]{1,0:T(8,128)(2,1)S(1)} %maximum_select_fusion.4), channel_id=1, source_target_pairs={{0,2},{1,3},{2,0},{3,1},{4,6},{5,7},{6,4},{7,5},{8,10},{9,11},{10,... | collective-permute-start | bytes 1769480 | tf_op jit(solution)/shard_map/ppermute | solution.py:729
  49.5 15.0 %collective-permute-start.8 = (bf16[384,768]{1,0:T(8,128)(2,1)S(1)}, bf16[384,768]{1,0:T(8,128)(2,1)S(1)}, u32[]{:S(2)}, u32[]{:S(2)}) collective-permute-start(bf16[384,768]{1,0:T(8,128)(2,1)S(1)} %collective-permute-done.7.r_2_.r_4_.r__6_.rest_2_), channel_id=1, source_target_pairs={{0,4},{4,0},{8,12},{12,8},{16,20},{20,16},{24,28},{28,24},{1,5},{5... | collective-permute-start | bytes 1769480 | tf_op jit(solution)/shard_map/ppermute | solution.py:729
  51.3 28.4 %collective-permute-start.11 = (bf16[768,768]{1,0:T(8,128)(2,1)S(1)}, bf16[768,768]{1,0:T(8,128)(2,1)S(1)}, u32[]{:S(2)}, u32[]{:S(2)}) collective-permute-start(bf16[768,768]{1,0:T(8,128)(2,1)S(1)} %broadcast_select_fusion), channel_id=1, source_target_pairs={{0,2},{1,3},{2,0},{3,1},{4,6},{5,7},{6,4},{7,5},{8,10},{9,11},{10,... | collective-permute-start | bytes 3538952 | tf_op jit(solution)/shard_map/ppermute | solution.py:729
  64.6 26.6 %collective-permute-start.12 = (bf16[768,768]{1,0:T(8,128)(2,1)S(1)}, bf16[768,768]{1,0:T(8,128)(2,1)S(1)}, u32[]{:S(2)}, u32[]{:S(2)}) collective-permute-start(bf16[768,768]{1,0:T(8,128)(2,1)S(1)} %copy-done.21), channel_id=1, source_target_pairs={{0,1},{1,0},{2,3},{3,2},{4,5},{5,4},{6,7},{7,6},{8,9},{9,8},{10,11... | collective-permute-start | bytes 3538952 | tf_op jit(solution)/shard_map/ppermute | solution.py:729
  65.1 26.1 %collective-permute-start.13 = (bf16[768,768]{1,0:T(8,128)(2,1)S(1)}, bf16[768,768]{1,0:T(8,128)(2,1)S(1)}, u32[]{:S(2)}, u32[]{:S(2)}) collective-permute-start(bf16[768,768]{1,0:T(8,128)(2,1)S(1)} %copy-done.22), channel_id=1, source_target_pairs={{0,1},{1,0},{2,3},{3,2},{4,5},{5,4},{6,7},{7,6},{8,9},{9,8},{10,11... | collective-permute-start | bytes 3538952 | tf_op jit(solution)/shard_map/ppermute | solution.py:729
  79.6 28.4 %collective-permute-start.15 = (bf16[768,768]{1,0:T(8,128)(2,1)S(1)}, bf16[768,768]{1,0:T(8,128)(2,1)S(1)}, u32[]{:S(2)}, u32[]{:S(2)}) collective-permute-start(bf16[768,768]{1,0:T(8,128)(2,1)S(1)} %collective-permute-done.11.r_3_.r_4_), channel_id=1, source_target_pairs={{0,4},{4,0},{8,12},{12,8},{16,20},{20,16},{24,28},{28,24},{1,5},{5... | collective-permute-start | bytes 3538952 | tf_op jit(solution)/shard_map/ppermute | solution.py:729
  108.0 17.4 %collective-permute-start.17 = (bf16[768,768]{1,0:T(8,128)(2,1)S(1)}, bf16[768,768]{1,0:T(8,128)(2,1)S(1)}, u32[]{:S(2)}, u32[]{:S(2)}) collective-permute-start(bf16[768,768]{1,0:T(8,128)(2,1)S(1)} %get-tuple-element.280), channel_id=1, source_target_pairs={{0,1},{1,0},{2,3},{3,2},{4,5},{5,4},{6,7},{7,6},{8,9},{9,8},{10,11... | collective-permute-start | bytes 3538952 | tf_op jit(solution)/shard_map/ppermute | solution.py:729
  108.5 16.9 %collective-permute-start.18 = (bf16[768,768]{1,0:T(8,128)(2,1)S(1)}, bf16[768,768]{1,0:T(8,128)(2,1)S(1)}, u32[]{:S(2)}, u32[]{:S(2)}) collective-permute-start(bf16[768,768]{1,0:T(8,128)(2,1)S(1)} %get-tuple-element.281), channel_id=1, source_target_pairs={{0,1},{1,0},{2,3},{3,2},{4,5},{5,4},{6,7},{7,6},{8,9},{9,8},{10,11... | collective-permute-start | bytes 3538952 | tf_op jit(solution)/shard_map/ppermute | solution.py:729
  136.4 31.4 %collective-permute-start.21 = (bf16[768,768]{1,0:T(8,128)(2,1)S(1)}, bf16[768,768]{1,0:T(8,128)(2,1)S(1)}, u32[]{:S(2)}, u32[]{:S(2)}) collective-permute-start(bf16[768,768]{1,0:T(8,128)(2,1)S(1)} %add_convert_fusion.1), channel_id=1, source_target_pairs={{0,2},{1,3},{2,0},{3,1},{4,6},{5,7},{6,4},{7,5},{8,10},{9,11},{10,... | collective-permute-start | bytes 3538952 | tf_op jit(solution)/shard_map/ppermute | solution.py:729
  137.9 30.9 %collective-permute-start.22 = (bf16[768,768]{1,0:T(8,128)(2,1)}, bf16[768,768]{1,0:T(8,128)(2,1)}, u32[]{:S(2)}, u32[]{:S(2)}) collective-permute-start(bf16[768,768]{1,0:T(8,128)(2,1)} %pad_maximum_fusion.2), channel_id=1, source_target_pairs={{0,4},{4,0},{8,12},{12,8},{16,20},{20,16},{24,28},{28,24},{1,5},{5... | collective-permute-start | bytes 3538952 | tf_op jit(solution)/shard_map/ppermute | solution.py:729
  172.5 24.3 %collective-permute-start.24 = (bf16[384,768]{1,0:T(8,128)(2,1)S(1)}, bf16[384,768]{1,0:T(8,128)(2,1)}, u32[]{:S(2)}, u32[]{:S(2)}) collective-permute-start(bf16[384,768]{1,0:T(8,128)(2,1)S(1)} %fusion.6), channel_id=1, source_target_pairs={{0,2},{1,3},{2,0},{3,1},{4,6},{5,7},{6,4},{7,5},{8,10},{9,11},{10,... | collective-permute-start | bytes 1769480 | tf_op jit(solution)/shard_map/ppermute | solution.py:729
  172.8 24.0 %collective-permute-start.25 = (bf16[384,768]{1,0:T(8,128)(2,1)}, bf16[384,768]{1,0:T(8,128)(2,1)}, u32[]{:S(2)}, u32[]{:S(2)}) collective-permute-start(bf16[384,768]{1,0:T(8,128)(2,1)} %fusion.9), channel_id=1, source_target_pairs={{0,4},{4,0},{8,12},{12,8},{16,20},{20,16},{24,28},{28,24},{1,5},{5... | collective-permute-start | bytes 1769480 | tf_op jit(solution)/shard_map/ppermute | solution.py:729
  174.6 32.4 %collective-permute-start.30 = (bf16[384,768]{1,0:T(8,128)(2,1)}, bf16[384,768]{1,0:T(8,128)(2,1)S(1)}, u32[]{:S(2)}, u32[]{:S(2)}) collective-permute-start(bf16[384,768]{1,0:T(8,128)(2,1)} %get-tuple-element.360), channel_id=1, source_target_pairs={{0,1},{1,0},{2,3},{3,2},{4,5},{5,4},{6,7},{7,6},{8,9},{9,8},{10,11... | collective-permute-start | bytes 1769480 | tf_op jit(solution)/shard_map/ppermute | solution.py:729
  195.3 30.2 %collective-permute-start.28 = (bf16[384,768]{1,0:T(8,128)(2,1)}, bf16[384,768]{1,0:T(8,128)(2,1)S(1)}, u32[]{:S(2)}, u32[]{:S(2)}) collective-permute-start(bf16[384,768]{1,0:T(8,128)(2,1)} %add_convert_fusion.6), channel_id=1, source_target_pairs={{0,2},{1,3},{2,0},{3,1},{4,6},{5,7},{6,4},{7,5},{8,10},{9,11},{10,... | collective-permute-start | bytes 1769480 | tf_op jit(solution)/shard_map/ppermute | solution.py:729
  202.2 25.7 %collective-permute-start.29 = (bf16[384,768]{1,0:T(8,128)(2,1)}, bf16[384,768]{1,0:T(8,128)(2,1)S(1)}, u32[]{:S(2)}, u32[]{:S(2)}) collective-permute-start(bf16[384,768]{1,0:T(8,128)(2,1)} %add_convert_fusion.5), channel_id=1, source_target_pairs={{0,2},{1,3},{2,0},{3,1},{4,6},{5,7},{6,4},{7,5},{8,10},{9,11},{10,... | collective-permute-start | bytes 1769480 | tf_op jit(solution)/shard_map/ppermute | solution.py:729
  202.8 22.7 %collective-permute-start.31 = (bf16[192,768]{1,0:T(8,128)(2,1)S(1)}, bf16[192,768]{1,0:T(8,128)(2,1)S(1)}, u32[]{:S(2)}, u32[]{:S(2)}) collective-permute-start(bf16[192,768]{1,0:T(8,128)(2,1)S(1)} %get-tuple-element.438), channel_id=1, source_target_pairs={{0,8},{4,12},{8,0},{12,4},{16,24},{20,28},{24,16},{28,20},{1,9},{5... | collective-permute-start | bytes 884744 | tf_op jit(solution)/shard_map/ppermute | solution.py:729
  204.4 23.5 %collective-permute-start.32 = (bf16[192,768]{1,0:T(8,128)(2,1)S(1)}, bf16[192,768]{1,0:T(8,128)(2,1)S(1)}, u32[]{:S(2)}, u32[]{:S(2)}) collective-permute-start(bf16[192,768]{1,0:T(8,128)(2,1)S(1)} %get-tuple-element.437), channel_id=1, source_target_pairs={{0,16},{4,20},{8,24},{12,28},{16,0},{20,4},{24,8},{28,12},{1,17},{... | collective-permute-start | bytes 884744 | tf_op jit(solution)/shard_map/ppermute | solution.py:729
  207.0 20.9 %collective-permute-start.33 = (bf16[192,768]{1,0:T(8,128)(2,1)S(1)}, bf16[192,768]{1,0:T(8,128)(2,1)S(1)}, u32[]{:S(2)}, u32[]{:S(2)}) collective-permute-start(bf16[192,768]{1,0:T(8,128)(2,1)S(1)} %get-tuple-element.436), channel_id=1, source_target_pairs={{0,24},{4,28},{8,16},{12,20},{16,8},{20,12},{24,0},{28,4},{1,25},{... | collective-permute-start | bytes 884744 | tf_op jit(solution)/shard_map/ppermute | solution.py:729
  232.3 23.7 %collective-permute-start.37 = (bf16[768,768]{1,0:T(8,128)(2,1)}, bf16[768,768]{1,0:T(8,128)(2,1)}, u32[]{:S(2)}, u32[]{:S(2)}) collective-permute-start(bf16[768,768]{1,0:T(8,128)(2,1)} %get-tuple-element.384), channel_id=1, source_target_pairs={{0,1},{1,0},{2,3},{3,2},{4,5},{5,4},{6,7},{7,6},{8,9},{9,8},{10,11... | collective-permute-start | bytes 3538952 | tf_op jit(solution)/shard_map/ppermute | solution.py:729
  232.5 28.6 %collective-permute-start.38 = (bf16[768,768]{1,0:T(8,128)(2,1)}, bf16[768,768]{1,0:T(8,128)(2,1)}, u32[]{:S(2)}, u32[]{:S(2)}) collective-permute-start(bf16[768,768]{1,0:T(8,128)(2,1)} %add_convert_fusion), channel_id=1, source_target_pairs={{0,2},{1,3},{2,0},{3,1},{4,6},{5,7},{6,4},{7,5},{8,10},{9,11},{10,... | collective-permute-start | bytes 3538952 | tf_op jit(solution)/shard_map/ppermute | solution.py:729
  234.0 22.0 %collective-permute-start.35 = (bf16[384,768]{1,0:T(8,128)(2,1)}, bf16[384,768]{1,0:T(8,128)(2,1)}, u32[]{:S(2)}, u32[]{:S(2)}) collective-permute-start(bf16[384,768]{1,0:T(8,128)(2,1)} %add_convert_fusion.4), channel_id=1, source_target_pairs={{0,4},{4,0},{8,12},{12,8},{16,20},{20,16},{24,28},{28,24},{1,5},{5... | collective-permute-start | bytes 1769480 | tf_op jit(solution)/shard_map/ppermute | solution.py:729
  235.9 20.1 %collective-permute-start.39 = (bf16[192,768]{1,0:T(8,128)(2,1)}, bf16[192,768]{1,0:T(8,128)(2,1)}, u32[]{:S(2)}, u32[]{:S(2)}) collective-permute-start(bf16[192,768]{1,0:T(8,128)(2,1)} %add_convert_fusion.10), channel_id=1, source_target_pairs={{0,16},{4,20},{8,24},{12,28},{16,0},{20,4},{24,8},{28,12},{1,17},{... | collective-permute-start | bytes 884744 | tf_op jit(solution)/shard_map/ppermute | solution.py:729
  262.7 21.5 %collective-permute-start.40 = (bf16[384,768]{1,0:T(8,128)(2,1)S(1)}, bf16[384,768]{1,0:T(8,128)(2,1)S(1)}, u32[]{:S(2)}, u32[]{:S(2)}) collective-permute-start(bf16[384,768]{1,0:T(8,128)(2,1)S(1)} %fusion.10), channel_id=1, source_target_pairs={{0,4},{4,0},{8,12},{12,8},{16,20},{20,16},{24,28},{28,24},{1,5},{5... | collective-permute-start | bytes 1769480 | tf_op jit(solution)/shard_map/ppermute | solution.py:729
  276.8 22.0 %collective-permute-start.46 = (bf16[384,768]{1,0:T(8,128)(2,1)S(1)}, bf16[384,768]{1,0:T(8,128)(2,1)S(1)}, u32[]{:S(2)}, u32[]{:S(2)}) collective-permute-start(bf16[384,768]{1,0:T(8,128)(2,1)S(1)} %maximum_select_fusion.5), channel_id=1, source_target_pairs={{0,8},{4,12},{8,0},{12,4},{16,24},{20,28},{24,16},{28,20},{1,9},{5... | collective-permute-start | bytes 1769480 | tf_op jit(solution)/shard_map/ppermute | solution.py:729
  285.8 15.5 %collective-permute-start.47 = (bf16[96,768]{1,0:T(8,128)(2,1)S(1)}, bf16[96,768]{1,0:T(8,128)(2,1)S(1)}, u32[]{:S(2)}, u32[]{:S(2)}) collective-permute-start(bf16[96,768]{1,0:T(8,128)(2,1)S(1)} %get-tuple-element.446), channel_id=1, source_target_pairs={{0,8},{4,12},{8,0},{12,4},{16,24},{20,28},{24,16},{28,20},{1,9},{5... | collective-permute-start | bytes 442376 | tf_op jit(solution)/shard_map/ppermute | solution.py:729
  289.0 15.4 %collective-permute-start.49 = (bf16[96,768]{1,0:T(8,128)(2,1)S(1)}, bf16[96,768]{1,0:T(8,128)(2,1)S(1)}, u32[]{:S(2)}, u32[]{:S(2)}) collective-permute-start(bf16[96,768]{1,0:T(8,128)(2,1)S(1)} %get-tuple-element.444), channel_id=1, source_target_pairs={{0,24},{4,28},{8,16},{12,20},{16,8},{20,12},{24,0},{28,4},{1,25},{... | collective-permute-start | bytes 442376 | tf_op jit(solution)/shard_map/ppermute | solution.py:729
  304.9 33.8 %collective-permute-start.60 = (bf16[768,768]{1,0:T(8,128)(2,1)S(1)}, bf16[768,768]{1,0:T(8,128)(2,1)}, u32[]{:S(2)}, u32[]{:S(2)}) collective-permute-start(bf16[768,768]{1,0:T(8,128)(2,1)S(1)} %maximum_select_fusion), channel_id=1, source_target_pairs={{0,4},{4,0},{8,12},{12,8},{16,20},{20,16},{24,28},{28,24},{1,5},{5... | collective-permute-start | bytes 3538952 | tf_op jit(solution)/shard_map/ppermute | solution.py:729
  332.1 16.4 %collective-permute-start.59 = (bf16[384,768]{1,0:T(8,128)(2,1)S(1)}, bf16[384,768]{1,0:T(8,128)(2,1)}, u32[]{:S(2)}, u32[]{:S(2)}) collective-permute-start(bf16[384,768]{1,0:T(8,128)(2,1)S(1)} %maximum_select_fusion.7), channel_id=1, source_target_pairs={{0,4},{4,0},{8,12},{12,8},{16,20},{20,16},{24,28},{28,24},{1,5},{5... | collective-permute-start | bytes 1769480 | tf_op jit(solution)/shard_map/ppermute | solution.py:729
  335.1 21.4 %collective-permute-start.58 = (bf16[384,768]{1,0:T(8,128)(2,1)S(1)}, bf16[384,768]{1,0:T(8,128)(2,1)}, u32[]{:S(2)}, u32[]{:S(2)}) collective-permute-start(bf16[384,768]{1,0:T(8,128)(2,1)S(1)} %maximum_select_fusion.6), channel_id=1, source_target_pairs={{0,4},{4,0},{8,12},{12,8},{16,20},{20,16},{24,28},{28,24},{1,5},{5... | collective-permute-start | bytes 1769480 | tf_op jit(solution)/shard_map/ppermute | solution.py:729
  (111 other events, 1092.7 us)

commit v5 on v4

--- a/solution.py
+++ b/solution.py
@@ -909,7 +909,7 @@
     small_got = core(small)
     yc, small_got, s1, xs, f_got = fence(yc, small_got, s1, xs, f_got)
     ys = sent_y(gs0, s1, xs)
-    zc = stage_z(plus(*[jnp.where(y_is0, a_, b_) for a_, b_ in zip(qo_t, kv_t)], yc))
+    zc = stage_z_reversed(plus(*[jnp.where(y_is0, a_, b_) for a_, b_ in zip(qo_t, kv_t)], yc))
     small = small + small_got
     small_got = over_x(small)
     f_w = in_order(f_w, f_got, z_bits[1])
@@ -919,21 +919,24 @@
     small = small + small_got
     small_got = over_y(small)
     c_w = plus(*zc)
-    small_got, c_w, f_got, *zs = fence(small_got, c_w, f_got, *zs)
+    for bit in z_bits[:1:-1]:
+        c_w = in_order(c_w, swap(c_w, "dp", bit), bit)
+    c_got = swap(c_w, "dp", z_bits[1])
+    small_got, c_got, f_got, *zs = fence(small_got, c_got, f_got, *zs)
     f_v = in_order(f_w, f_got, 2)
     f_f = over_y(f_v)
-    bc = stage_z_back(c_w)
+    c_w = in_order(c_w, c_got, z_bits[1])
+    c_got = swap(c_w, "dp", 2)
     bit = 2
     small = small + small_got
     small_got = swap(small, "dp", bit)
     bs = stage_z_back(plus(*zs))
-    both = fence(small_got, *bs, *bc)
-    small_got, bs, bc = both[0], both[1 : 1 + rest_size], both[1 + rest_size :]
+    small_got, c_got, *bs = fence(small_got, c_got, *bs)
     small = small + small_got
     while 2 * bit < dp_size:
         bit *= 2
         small = small + swap(small, "dp", bit)
-    c_v = ordered_z(bc)
+    c_v = in_order(c_w, c_got, 2)
     c_f = over_y(c_v)
     s_v = ordered_z(bs)
     s_f = over_y(s_v)
@@ -944,8 +947,8 @@
     r_s = ordered(s_v, s_f)
     g_s = [r_s[i * w : (i + 1) * w].astype(f32) for i in range(4)]
     c_f, *g_s = fence(c_f, *g_s)
-    c_w = [jnp.where(y_is0, a_, b_) for a_, b_ in ((c_v, c_f), (c_f, c_v))]
-    g_c = [v[i * w : (i + 1) * w].astype(f32) for v in c_w for i in range(2)]
+    c_both = [jnp.where(y_is0, a_, b_) for a_, b_ in ((c_v, c_f), (c_f, c_v))]
+    g_c = [v[i * w : (i + 1) * w].astype(f32) for v in c_both for i in range(2)]
     grad_rel = lax.dynamic_slice(small[3], (t_index * heads * BUCKETS,), (heads * BUCKETS,)).reshape(heads, BUCKETS).T
 
     return (

time: 365 us -> 366 us (level)
  starting transfers between devices: 63.1 us -> 66.8 us
    ppermute x61 -> x60, starting transfers between devices: 63.1 us -> 66.8 us  [swap(): return lax.ppermute(v, axis, [(i, i ^ bit) for i in range(n)])]
    ppermute x61 -> x60, waiting for transfers between devices: 97 us -> 93.8 us  [swap(): return lax.ppermute(v, axis, [(i, i ^ bit) for i in range(n)])]
  transfers between devices with their start and end apart: 61 -> 60, of which waited for: 25 -> 25; matrix products, arithmetic and copies ran while one was open for 11% -> 10% of each run, Pallas kernels for 35% -> 35%
where the time goes in v5:
time: 366 us; the launch traced here: 360 us
  Pallas kernels  127 us (35%)
  waiting for transfers between devices  93.8 us (26%)
  starting transfers between devices  66.8 us (18%)
  other arithmetic  43 us (12%)
  local copies, waits for them, and re-layouts  25.7 us (7%)
    pallas_call x11, Pallas kernels, call(): pl.pallas_call(kernel, out_shape=out_shape, grid=grid, scratch_shapes=scr...  127 us
    ppermute x60, waiting for transfers between devices, swap(): return lax.ppermute(v, axis, [(i, i ^ bit) for i in range(n)])  93.8 us
    ppermute x60, starting transfers between devices, swap(): return lax.ppermute(v, axis, [(i, i ^ bit) for i in range(n)])  66.8 us
    convert_element_type x17, other arithmetic, plus(): return total.astype(bf16)  22.2 us
    unnamed x164, local copies, waits for them, and re-layouts  20.7 us
  transfers between devices with their start and end apart: 60, of which 25 were waited for; matrix products, arithmetic and copies ran while one was open for 10% of the time, Pallas kernels for 35%

profile of v5, /device:TPU:0, one launch (start us, length us, event | category | flops | bytes accessed | tf_op | source)
XLA Modules:
  0.0 360.5 jit_solution(9440272611506773967)
XLA Ops:
  2.9 2.9 collective-permute-start.3
  11.9 5.2 %self_fwd.2 = (bf16[512,384]{1,0:T(8,128)(2,1)S(1)}, bf16[512,384]{1,0:T(8,128)(2,1)S(1)}, bf16[384,512]{1,0:T(8,128)(2,1)S(1)}, bf16[2,6,256,256]{3,2,1,0:T(8,1...) custom-call(s32[2]{0:T(128)S(1)} %pad_add_fusion.r_0_.r__0_.y_ref, ...), custom_call_target="tpu_custom_call" | custom-call | flops 1 | bytes 1 | tf_op jit(solution)/shard_map/self_fwd/pallas_call | solution.py:83
  19.4 4.8 %enc_kv.2 = (bf16[2048,384]{1,0:T(8,128)(2,1)S(1)}, bf16[2048,384]{1,0:T(8,128)(2,1)S(1)}) custom-call(s32[2]{0:T(128)S(1)} %pad_add_fusion.r_0_.r__0_.y_ref, bf16[2048,768]{1,0:T(8,128)(2,1)S(1)} %copy-done.3, bf16[768,768]{1,0:T(8,128)(2,1)S(1)} %pad_maximum_fusion.r_2_.r_4_.r__4_.rest_0_, bf16[768,768]{1,0:T(8,128)(2,1)S(1)} %collective-permute-done.2.r_3_.r_5_.r__5_.rest_1_), custom_call_target="tpu_custom_call" | custom-call | flops 1 | bytes 1 | tf_op jit(solution)/shard_map/enc_kv/pallas_call | solution.py:83
  26.6 5.6 %collective-permute-done.4 = f32[3,256]{1,0:T(4,128)} collective-permute-done((f32[3,256]{1,0:T(4,128)}, f32[3,256]{1,0:T(4,128)}, u32[]{:S(2)}, u32[]{:S(2)}) %collective-permute-start.4) | collective-permute-done | bytes 3104 | tf_op jit(solution)/shard_map/ppermute | solution.py:729
  37.9 5.9 %self_fwd.3 = (bf16[512,384]{1,0:T(8,128)(2,1)S(1)}, bf16[512,384]{1,0:T(8,128)(2,1)S(1)}, bf16[384,512]{1,0:T(8,128)(2,1)S(1)}, bf16[2,6,256,256]{3,2,1,0:T(8,1...) custom-call(s32[2]{0:T(128)S(1)} %pad_add_fusion.r_0_.r__0_.y_ref, ...), custom_call_target="tpu_custom_call" | custom-call | flops 1 | bytes 1 | tf_op jit(solution)/shard_map/self_fwd/pallas_call | solution.py:83
  52.8 8.9 %cross_fwd.2 = (bf16[512,384]{1,0:T(8,128)(2,1)S(1)}, f32[6,4,256]{2,1,0:T(4,128)S(1)}, bf16[384,512]{1,0:T(8,128)(2,1)S(1)}, f32[512,768]{1,0:T(8,128)S(1)}) custom-call(s32[2]{0:T(128)S(1)} %pad_add_fusion.r_0_.r__0_.y_ref, s32[8]{0:T(128)S(1)} %copy-done.51, bf16[512,768]{1,0:T(8,128)(2,1)S(1)} %get-tuple-element.243.r_2_.r__3_, ...), custom_call_target="tpu_custom_call" | custom-call | flops 1 | bytes 1 | tf_op jit(solution)/shard_map/cross_fwd/pallas_call | solution.py:83
  66.5 4.6 %enc_kv.3 = (bf16[2048,384]{1,0:T(8,128)(2,1)S(1)}, bf16[2048,384]{1,0:T(8,128)(2,1)S(1)}) custom-call(s32[2]{0:T(128)S(1)} %pad_add_fusion.r_0_.r__0_.y_ref, bf16[2048,768]{1,0:T(8,128)(2,1)S(1)} %copy-done.4, bf16[384,768]{1,0:T(8,128)(2,1)S(1)} %collective-permute-done.7.r_2_.r_4_.r__6_.rest_2_, ...), custom_call_target="tpu_custom_call" | custom-call | flops 1 | bytes 1 | tf_op jit(solution)/shard_map/enc_kv/pallas_call | solution.py:83
  71.2 8.5 %collective-permute-done.11.r_3_.r_4_ = bf16[768,768]{1,0:T(8,128)(2,1)S(1)} collective-permute-done((bf16[768,768]{1,0:T(8,128)(2,1)S(1)}, bf16[768,768]{1,0:T(8,128)(2,1)S(1)}, u32[]{:S(2)}, u32[]{:S(2)}) %collective-permute-start.11) | collective-permute-done | bytes 1179680 | tf_op jit(solution)/shard_map/ppermute | solution.py:729
  79.9 9.1 %cross_fwd.3 = (bf16[512,384]{1,0:T(8,128)(2,1)S(1)}, f32[6,4,256]{2,1,0:T(4,128)S(1)}, bf16[384,512]{1,0:T(8,128)(2,1)S(1)}, f32[512,768]{1,0:T(8,128)S(1)}, bf16[512,768]{1,0:T(8,128)(2,1)S(1)}) custom-call(s32[2]{0:T(128)S(1)} %pad_add_fusion.r_0_.r__0_.y_ref, s32[8]{0:T(128)S(1)} %copy-done.51, bf16[512,768]{1,0:T(8,128)(2,1)S(1)} %get-tuple-element.243.r_2_.r__3_, ...), custom_call_target="tpu_custom_call" | custom-call | flops 1 | bytes 1 | tf_op jit(solution)/shard_map/cross_fwd/pallas_call | solution.py:83
  91.2 10.9 %ff.2 = (bf16[768,768]{1,0:T(8,128)(2,1)S(1)}, bf16[768,768]{1,0:T(8,128)(2,1)S(1)}, bf16[768,768]{1,0:T(8,128)(2,1)S(1)}, bf16[768,768]{1,0:T(8,128)(2,1)S(1)},...) custom-call(s32[2]{0:T(128)S(1)} %pad_add_fusion.r_0_.r__0_.y_ref, bf16[512,768]{1,0:T(8,128)(2,1)S(1)} %get-tuple-element.260.r_1_, ...), custom_call_target="tpu_custom_call" | custom-call | flops 1 | bytes 1 | tf_op jit(solution)/shard_map/ff/pallas_call | solution.py:83
  102.1 5.9 %collective-permute-done.15.r_5_.r_6_ = bf16[768,768]{1,0:T(8,128)(2,1)S(1)} collective-permute-done((bf16[768,768]{1,0:T(8,128)(2,1)S(1)}, bf16[768,768]{1,0:T(8,128)(2,1)S(1)}, u32[]{:S(2)}, u32[]{:S(2)}) %collective-permute-start.15) | collective-permute-done | bytes 1179680 | tf_op jit(solution)/shard_map/ppermute | solution.py:729
  110.9 12.4 %ff.3 = (bf16[768,768]{1,0:T(8,128)(2,1)S(1)}, bf16[768,768]{1,0:T(8,128)(2,1)S(1)}, bf16[768,768]{1,0:T(8,128)(2,1)}, bf16[768,768]{1,0:T(8,128)(2,1)}, bf16[51...) custom-call(s32[2]{0:T(128)S(1)} %pad_add_fusion.r_0_.r__0_.y_ref, ...), custom_call_target="tpu_custom_call" | custom-call | flops 1 | bytes 1 | tf_op jit(solution)/shard_map/ff/pallas_call | solution.py:83
  138.4 29.3 %cross_bwd.1 = (bf16[2048,384]{1,0:T(8,128)(2,1)}, bf16[2048,384]{1,0:T(8,128)(2,1)}, bf16[2048,384]{1,0:T(8,128)(2,1)}, bf16[2048,384]{1,0:T(8,128)(2,1)}, bf16...) custom-call(s32[2]{0:T(128)} %copy-done.46, ...), custom_call_target="tpu_custom_call" | custom-call | flops 1 | bytes 1 | tf_op jit(solution)/shard_map/cross_bwd/pallas_call | solution.py:83
  176.6 18.1 %enc_grad.1 = (f32[2048,768]{1,0:T(8,128)}, bf16[384,768]{1,0:T(8,128)(2,1)}, bf16[384,768]{1,0:T(8,128)(2,1)}, bf16[384,768]{1,0:T(8,128)(2,1)}, bf16[384,768]{1,0:T(8,128)(2,1)}) custom-call(s32[2]{0:T(128)} %copy-done.46, bf16[2048,768]{1,0:T(8,128)(2,1)} %enc_ref.1, bf16[2048,384]{1,0:T(8,128)(2,1)} %get-tuple-element.309.gk1_ref, ...), custom_call_target="tpu_custom_call" | custom-call | flops 1 | bytes 1 | tf_op jit(solution)/shard_map/enc_grad/pallas_call | solution.py:83
  204.4 2.6 collective-permute-start.32
  207.2 18.2 %self_bwd.1 = (bf16[768,768]{1,0:T(8,128)(2,1)}, bf16[768,768]{1,0:T(8,128)(2,1)}, bf16[768,768]{1,0:T(8,128)(2,1)}, bf16[768,768]{1,0:T(8,128)(2,1)}, f32[12,25...) custom-call(bf16[512,768]{1,0:T(8,128)(2,1)} %x_ref.1, f32[512,768]{1,0:T(8,128)} %copy-done.14, ...), custom_call_target="tpu_custom_call" | custom-call | flops 1 | bytes 1 | tf_op jit(solution)/shard_map/self_bwd/pallas_call | solution.py:83
  225.4 2.4 collective-permute-done.32
  235.8 6.5 %collective-permute-start.39 = (bf16[192,768]{1,0:T(8,128)(2,1)}, bf16[192,768]{1,0:T(8,128)(2,1)}, u32[]{:S(2)}, u32[]{:S(2)}) collective-permute-start(bf16[192,768]{1,0:T(8,128)(2,1)} %add_convert_fusion.10), channel_id=1, source_target_pairs={{0,16},{4,20},{8,24},{12,28},{16,0},{20,4},{24,8},{28,12},{1,17},{... | collective-permute-start | bytes 884744 | tf_op jit(solution)/shard_map/ppermute | solution.py:729
  246.6 9.3 %collective-permute-done.39 = bf16[192,768]{1,0:T(8,128)(2,1)} collective-permute-done((bf16[192,768]{1,0:T(8,128)(2,1)}, bf16[192,768]{1,0:T(8,128)(2,1)}, u32[]{:S(2)}, u32[]{:S(2)}) %collective-permute-start.39) | collective-permute-done | bytes 294944 | tf_op jit(solution)/shard_map/ppermute | solution.py:729
  256.0 5.0 %collective-permute-done.38 = bf16[768,768]{1,0:T(8,128)(2,1)} collective-permute-done((bf16[768,768]{1,0:T(8,128)(2,1)}, bf16[768,768]{1,0:T(8,128)(2,1)}, u32[]{:S(2)}, u32[]{:S(2)}) %collective-permute-start.38) | collective-permute-done | bytes 1179680 | tf_op jit(solution)/shard_map/ppermute | solution.py:729
  264.9 5.6 %collective-permute-start.42 = (bf16[96,768]{1,0:T(8,128)(2,1)S(1)}, bf16[96,768]{1,0:T(8,128)(2,1)S(1)}, u32[]{:S(2)}, u32[]{:S(2)}) collective-permute-start(bf16[96,768]{1,0:T(8,128)(2,1)S(1)} %get-tuple-element.444), channel_id=1, source_target_pairs={{0,8},{4,12},{8,0},{12,4},{16,24},{20,28},{24,16},{28,20},{1,9},{5... | collective-permute-start | bytes 442376 | tf_op jit(solution)/shard_map/ppermute | solution.py:729
  277.8 6.3 %collective-permute-done.43 = bf16[96,768]{1,0:T(8,128)(2,1)S(1)} collective-permute-done((bf16[96,768]{1,0:T(8,128)(2,1)S(1)}, bf16[96,768]{1,0:T(8,128)(2,1)S(1)}, u32[]{:S(2)}, u32[]{:S(2)}) %collective-permute-start.43) | collective-permute-done | bytes 147488 | tf_op jit(solution)/shard_map/ppermute | solution.py:729
  292.5 9.5 %collective-permute-done.47 = bf16[384,768]{1,0:T(8,128)(2,1)S(1)} collective-permute-done((bf16[384,768]{1,0:T(8,128)(2,1)S(1)}, bf16[384,768]{1,0:T(8,128)(2,1)S(1)}, u32[]{:S(2)}, u32[]{:S(2)}) %collective-permute-start.47) | collective-permute-done | bytes 589856 | tf_op jit(solution)/shard_map/ppermute | solution.py:729
  306.1 2.7 collective-permute-done.46
  313.3 3.2 collective-permute-start.54
  316.5 2.8 collective-permute-done.51
  319.4 6.7 %collective-permute-start.55 = (bf16[96,768]{1,0:T(8,128)(2,1)S(1)}, bf16[96,768]{1,0:T(8,128)(2,1)S(1)}, u32[]{:S(2)}, u32[]{:S(2)}) collective-permute-start(bf16[96,768]{1,0:T(8,128)(2,1)S(1)} %add_convert_fusion.11), channel_id=1, source_target_pairs={{0,24},{4,28},{8,16},{12,20},{16,8},{20,12},{24,0},{28,4},{1,25},{... | collective-permute-start | bytes 442376 | tf_op jit(solution)/shard_map/ppermute | solution.py:729
  326.1 3.3 collective-permute-done.55
  332.1 2.6 collective-permute-done.56
  337.4 2.7 fusion
  340.1 8.1 %collective-permute-done.58 = bf16[384,768]{1,0:T(8,128)(2,1)} collective-permute-done((bf16[384,768]{1,0:T(8,128)(2,1)S(1)}, bf16[384,768]{1,0:T(8,128)(2,1)}, u32[]{:S(2)}, u32[]{:S(2)}) %collective-permute-start.58) | collective-permute-done | bytes 589856 | tf_op jit(solution)/shard_map/ppermute | solution.py:729
  351.3 5.6 %collective-permute-done.57 = bf16[384,768]{1,0:T(8,128)(2,1)} collective-permute-done((bf16[384,768]{1,0:T(8,128)(2,1)S(1)}, bf16[384,768]{1,0:T(8,128)(2,1)}, u32[]{:S(2)}, u32[]{:S(2)}) %collective-permute-start.57) | collective-permute-done | bytes 589856 | tf_op jit(solution)/shard_map/ppermute | solution.py:729
  (325 shorter events, 123.2 us)
Async XLA Ops:
  2.9 29.3 %collective-permute-start.3 = (bf16[768,768]{1,0:T(8,128)(2,1)S(1)}, bf16[768,768]{1,0:T(8,128)(2,1)}, u32[]{:S(2)}, u32[]{:S(2)}) collective-permute-start(bf16[768,768]{1,0:T(8,128)(2,1)S(1)} %pad_maximum_fusion.1.r_4_.rest_0_), channel_id=1, source_target_pairs={{0,2},{1,3},{2,0},{3,1},{4,6},{5,7},{6,4},{7,5},{8,10},{9,11},{10,... | collective-permute-start | bytes 3538952 | tf_op jit(solution)/shard_map/ppermute | solution.py:729
  6.6 25.7 %collective-permute-start.4 = (f32[3,256]{1,0:T(4,128)}, f32[3,256]{1,0:T(4,128)}, u32[]{:S(2)}, u32[]{:S(2)}) collective-permute-start(f32[3,256]{1,0:T(4,128)} %convolution_bitcast_fusion), channel_id=1, source_target_pairs={{0,2},{1,3},{2,0},{3,1},{4,6},{5,7},{6,4},{7,5},{8,10},{9,11},{10,... | collective-permute-start | bytes 9224 | tf_op jit(solution)/shard_map/ppermute | solution.py:729
  51.3 28.4 %collective-permute-start.11 = (bf16[768,768]{1,0:T(8,128)(2,1)S(1)}, bf16[768,768]{1,0:T(8,128)(2,1)S(1)}, u32[]{:S(2)}, u32[]{:S(2)}) collective-permute-start(bf16[768,768]{1,0:T(8,128)(2,1)S(1)} %broadcast_select_fusion), channel_id=1, source_target_pairs={{0,2},{1,3},{2,0},{3,1},{4,6},{5,7},{6,4},{7,5},{8,10},{9,11},{10,... | collective-permute-start | bytes 3538952 | tf_op jit(solution)/shard_map/ppermute | solution.py:729
  64.6 26.6 %collective-permute-start.12 = (bf16[768,768]{1,0:T(8,128)(2,1)S(1)}, bf16[768,768]{1,0:T(8,128)(2,1)S(1)}, u32[]{:S(2)}, u32[]{:S(2)}) collective-permute-start(bf16[768,768]{1,0:T(8,128)(2,1)S(1)} %copy-done.21), channel_id=1, source_target_pairs={{0,1},{1,0},{2,3},{3,2},{4,5},{5,4},{6,7},{7,6},{8,9},{9,8},{10,11... | collective-permute-start | bytes 3538952 | tf_op jit(solution)/shard_map/ppermute | solution.py:729
  65.1 26.1 %collective-permute-start.13 = (bf16[768,768]{1,0:T(8,128)(2,1)S(1)}, bf16[768,768]{1,0:T(8,128)(2,1)S(1)}, u32[]{:S(2)}, u32[]{:S(2)}) collective-permute-start(bf16[768,768]{1,0:T(8,128)(2,1)S(1)} %copy-done.22), channel_id=1, source_target_pairs={{0,1},{1,0},{2,3},{3,2},{4,5},{5,4},{6,7},{7,6},{8,9},{9,8},{10,11... | collective-permute-start | bytes 3538952 | tf_op jit(solution)/shard_map/ppermute | solution.py:729
  79.6 28.4 %collective-permute-start.15 = (bf16[768,768]{1,0:T(8,128)(2,1)S(1)}, bf16[768,768]{1,0:T(8,128)(2,1)S(1)}, u32[]{:S(2)}, u32[]{:S(2)}) collective-permute-start(bf16[768,768]{1,0:T(8,128)(2,1)S(1)} %collective-permute-done.11.r_3_.r_4_), channel_id=1, source_target_pairs={{0,4},{4,0},{8,12},{12,8},{16,20},{20,16},{24,28},{28,24},{1,5},{5... | collective-permute-start | bytes 3538952 | tf_op jit(solution)/shard_map/ppermute | solution.py:729
  108.0 17.4 %collective-permute-start.17 = (bf16[768,768]{1,0:T(8,128)(2,1)S(1)}, bf16[768,768]{1,0:T(8,128)(2,1)S(1)}, u32[]{:S(2)}, u32[]{:S(2)}) collective-permute-start(bf16[768,768]{1,0:T(8,128)(2,1)S(1)} %get-tuple-element.277), channel_id=1, source_target_pairs={{0,1},{1,0},{2,3},{3,2},{4,5},{5,4},{6,7},{7,6},{8,9},{9,8},{10,11... | collective-permute-start | bytes 3538952 | tf_op jit(solution)/shard_map/ppermute | solution.py:729
  108.5 16.9 %collective-permute-start.18 = (bf16[768,768]{1,0:T(8,128)(2,1)S(1)}, bf16[768,768]{1,0:T(8,128)(2,1)S(1)}, u32[]{:S(2)}, u32[]{:S(2)}) collective-permute-start(bf16[768,768]{1,0:T(8,128)(2,1)S(1)} %get-tuple-element.278), channel_id=1, source_target_pairs={{0,1},{1,0},{2,3},{3,2},{4,5},{5,4},{6,7},{7,6},{8,9},{9,8},{10,11... | collective-permute-start | bytes 3538952 | tf_op jit(solution)/shard_map/ppermute | solution.py:729
  136.3 31.4 %collective-permute-start.21 = (bf16[768,768]{1,0:T(8,128)(2,1)S(1)}, bf16[768,768]{1,0:T(8,128)(2,1)S(1)}, u32[]{:S(2)}, u32[]{:S(2)}) collective-permute-start(bf16[768,768]{1,0:T(8,128)(2,1)S(1)} %add_convert_fusion.1), channel_id=1, source_target_pairs={{0,2},{1,3},{2,0},{3,1},{4,6},{5,7},{6,4},{7,5},{8,10},{9,11},{10,... | collective-permute-start | bytes 3538952 | tf_op jit(solution)/shard_map/ppermute | solution.py:729
  137.9 30.9 %collective-permute-start.22 = (bf16[768,768]{1,0:T(8,128)(2,1)}, bf16[768,768]{1,0:T(8,128)(2,1)}, u32[]{:S(2)}, u32[]{:S(2)}) collective-permute-start(bf16[768,768]{1,0:T(8,128)(2,1)} %pad_maximum_fusion.2), channel_id=1, source_target_pairs={{0,4},{4,0},{8,12},{12,8},{16,20},{20,16},{24,28},{28,24},{1,5},{5... | collective-permute-start | bytes 3538952 | tf_op jit(solution)/shard_map/ppermute | solution.py:729
  172.4 24.3 %collective-permute-start.24 = (bf16[384,768]{1,0:T(8,128)(2,1)S(1)}, bf16[384,768]{1,0:T(8,128)(2,1)}, u32[]{:S(2)}, u32[]{:S(2)}) collective-permute-start(bf16[384,768]{1,0:T(8,128)(2,1)S(1)} %fusion.6), channel_id=1, source_target_pairs={{0,2},{1,3},{2,0},{3,1},{4,6},{5,7},{6,4},{7,5},{8,10},{9,11},{10,... | collective-permute-start | bytes 1769480 | tf_op jit(solution)/shard_map/ppermute | solution.py:729
  172.8 24.0 %collective-permute-start.25 = (bf16[384,768]{1,0:T(8,128)(2,1)}, bf16[384,768]{1,0:T(8,128)(2,1)}, u32[]{:S(2)}, u32[]{:S(2)}) collective-permute-start(bf16[384,768]{1,0:T(8,128)(2,1)} %fusion.9), channel_id=1, source_target_pairs={{0,4},{4,0},{8,12},{12,8},{16,20},{20,16},{24,28},{28,24},{1,5},{5... | collective-permute-start | bytes 1769480 | tf_op jit(solution)/shard_map/ppermute | solution.py:729
  174.5 32.4 %collective-permute-start.30 = (bf16[384,768]{1,0:T(8,128)(2,1)}, bf16[384,768]{1,0:T(8,128)(2,1)S(1)}, u32[]{:S(2)}, u32[]{:S(2)}) collective-permute-start(bf16[384,768]{1,0:T(8,128)(2,1)} %get-tuple-element.357), channel_id=1, source_target_pairs={{0,1},{1,0},{2,3},{3,2},{4,5},{5,4},{6,7},{7,6},{8,9},{9,8},{10,11... | collective-permute-start | bytes 1769480 | tf_op jit(solution)/shard_map/ppermute | solution.py:729
  195.3 30.1 %collective-permute-start.28 = (bf16[384,768]{1,0:T(8,128)(2,1)}, bf16[384,768]{1,0:T(8,128)(2,1)S(1)}, u32[]{:S(2)}, u32[]{:S(2)}) collective-permute-start(bf16[384,768]{1,0:T(8,128)(2,1)} %add_convert_fusion.6), channel_id=1, source_target_pairs={{0,2},{1,3},{2,0},{3,1},{4,6},{5,7},{6,4},{7,5},{8,10},{9,11},{10,... | collective-permute-start | bytes 1769480 | tf_op jit(solution)/shard_map/ppermute | solution.py:729
  202.1 25.7 %collective-permute-start.29 = (bf16[384,768]{1,0:T(8,128)(2,1)}, bf16[384,768]{1,0:T(8,128)(2,1)S(1)}, u32[]{:S(2)}, u32[]{:S(2)}) collective-permute-start(bf16[384,768]{1,0:T(8,128)(2,1)} %add_convert_fusion.5), channel_id=1, source_target_pairs={{0,2},{1,3},{2,0},{3,1},{4,6},{5,7},{6,4},{7,5},{8,10},{9,11},{10,... | collective-permute-start | bytes 1769480 | tf_op jit(solution)/shard_map/ppermute | solution.py:729
  202.7 22.7 %collective-permute-start.31 = (bf16[192,768]{1,0:T(8,128)(2,1)S(1)}, bf16[192,768]{1,0:T(8,128)(2,1)S(1)}, u32[]{:S(2)}, u32[]{:S(2)}) collective-permute-start(bf16[192,768]{1,0:T(8,128)(2,1)S(1)} %get-tuple-element.432), channel_id=1, source_target_pairs={{0,8},{4,12},{8,0},{12,4},{16,24},{20,28},{24,16},{28,20},{1,9},{5... | collective-permute-start | bytes 884744 | tf_op jit(solution)/shard_map/ppermute | solution.py:729
  204.4 23.5 %collective-permute-start.32 = (bf16[192,768]{1,0:T(8,128)(2,1)S(1)}, bf16[192,768]{1,0:T(8,128)(2,1)S(1)}, u32[]{:S(2)}, u32[]{:S(2)}) collective-permute-start(bf16[192,768]{1,0:T(8,128)(2,1)S(1)} %get-tuple-element.431), channel_id=1, source_target_pairs={{0,16},{4,20},{8,24},{12,28},{16,0},{20,4},{24,8},{28,12},{1,17},{... | collective-permute-start | bytes 884744 | tf_op jit(solution)/shard_map/ppermute | solution.py:729
  207.0 20.9 %collective-permute-start.33 = (bf16[192,768]{1,0:T(8,128)(2,1)S(1)}, bf16[192,768]{1,0:T(8,128)(2,1)S(1)}, u32[]{:S(2)}, u32[]{:S(2)}) collective-permute-start(bf16[192,768]{1,0:T(8,128)(2,1)S(1)} %get-tuple-element.430), channel_id=1, source_target_pairs={{0,24},{4,28},{8,16},{12,20},{16,8},{20,12},{24,0},{28,4},{1,25},{... | collective-permute-start | bytes 884744 | tf_op jit(solution)/shard_map/ppermute | solution.py:729
  232.3 23.7 %collective-permute-start.37 = (bf16[768,768]{1,0:T(8,128)(2,1)}, bf16[768,768]{1,0:T(8,128)(2,1)}, u32[]{:S(2)}, u32[]{:S(2)}) collective-permute-start(bf16[768,768]{1,0:T(8,128)(2,1)} %get-tuple-element.381), channel_id=1, source_target_pairs={{0,1},{1,0},{2,3},{3,2},{4,5},{5,4},{6,7},{7,6},{8,9},{9,8},{10,11... | collective-permute-start | bytes 3538952 | tf_op jit(solution)/shard_map/ppermute | solution.py:729
  232.4 28.6 %collective-permute-start.38 = (bf16[768,768]{1,0:T(8,128)(2,1)}, bf16[768,768]{1,0:T(8,128)(2,1)}, u32[]{:S(2)}, u32[]{:S(2)}) collective-permute-start(bf16[768,768]{1,0:T(8,128)(2,1)} %add_convert_fusion), channel_id=1, source_target_pairs={{0,2},{1,3},{2,0},{3,1},{4,6},{5,7},{6,4},{7,5},{8,10},{9,11},{10,... | collective-permute-start | bytes 3538952 | tf_op jit(solution)/shard_map/ppermute | solution.py:729
  233.9 22.0 %collective-permute-start.35 = (bf16[384,768]{1,0:T(8,128)(2,1)}, bf16[384,768]{1,0:T(8,128)(2,1)}, u32[]{:S(2)}, u32[]{:S(2)}) collective-permute-start(bf16[384,768]{1,0:T(8,128)(2,1)} %add_convert_fusion.4), channel_id=1, source_target_pairs={{0,4},{4,0},{8,12},{12,8},{16,20},{20,16},{24,28},{28,24},{1,5},{5... | collective-permute-start | bytes 1769480 | tf_op jit(solution)/shard_map/ppermute | solution.py:729
  235.8 20.1 %collective-permute-start.39 = (bf16[192,768]{1,0:T(8,128)(2,1)}, bf16[192,768]{1,0:T(8,128)(2,1)}, u32[]{:S(2)}, u32[]{:S(2)}) collective-permute-start(bf16[192,768]{1,0:T(8,128)(2,1)} %add_convert_fusion.10), channel_id=1, source_target_pairs={{0,16},{4,20},{8,24},{12,28},{16,0},{20,4},{24,8},{28,12},{1,17},{... | collective-permute-start | bytes 884744 | tf_op jit(solution)/shard_map/ppermute | solution.py:729
  262.6 21.5 %collective-permute-start.40 = (bf16[384,768]{1,0:T(8,128)(2,1)S(1)}, bf16[384,768]{1,0:T(8,128)(2,1)S(1)}, u32[]{:S(2)}, u32[]{:S(2)}) collective-permute-start(bf16[384,768]{1,0:T(8,128)(2,1)S(1)} %fusion.10), channel_id=1, source_target_pairs={{0,4},{4,0},{8,12},{12,8},{16,20},{20,16},{24,28},{28,24},{1,5},{5... | collective-permute-start | bytes 1769480 | tf_op jit(solution)/shard_map/ppermute | solution.py:729
  276.7 25.3 %collective-permute-start.47 = (bf16[384,768]{1,0:T(8,128)(2,1)S(1)}, bf16[384,768]{1,0:T(8,128)(2,1)S(1)}, u32[]{:S(2)}, u32[]{:S(2)}) collective-permute-start(bf16[384,768]{1,0:T(8,128)(2,1)S(1)} %maximum_select_fusion.5), channel_id=1, source_target_pairs={{0,8},{4,12},{8,0},{12,4},{16,24},{20,28},{24,16},{28,20},{1,9},{5... | collective-permute-start | bytes 1769480 | tf_op jit(solution)/shard_map/ppermute | solution.py:729
  285.7 20.0 %collective-permute-start.48 = (bf16[96,768]{1,0:T(8,128)(2,1)S(1)}, bf16[96,768]{1,0:T(8,128)(2,1)S(1)}, u32[]{:S(2)}, u32[]{:S(2)}) collective-permute-start(bf16[96,768]{1,0:T(8,128)(2,1)S(1)} %get-tuple-element.440), channel_id=1, source_target_pairs={{0,8},{4,12},{8,0},{12,4},{16,24},{20,28},{24,16},{28,20},{1,9},{5... | collective-permute-start | bytes 442376 | tf_op jit(solution)/shard_map/ppermute | solution.py:729
  287.9 17.8 %collective-permute-start.49 = (bf16[96,768]{1,0:T(8,128)(2,1)S(1)}, bf16[96,768]{1,0:T(8,128)(2,1)S(1)}, u32[]{:S(2)}, u32[]{:S(2)}) collective-permute-start(bf16[96,768]{1,0:T(8,128)(2,1)S(1)} %get-tuple-element.439), channel_id=1, source_target_pairs={{0,16},{4,20},{8,24},{12,28},{16,0},{20,4},{24,8},{28,12},{1,17},{... | collective-permute-start | bytes 442376 | tf_op jit(solution)/shard_map/ppermute | solution.py:729
  289.0 17.1 %collective-permute-start.50 = (bf16[96,768]{1,0:T(8,128)(2,1)S(1)}, bf16[96,768]{1,0:T(8,128)(2,1)S(1)}, u32[]{:S(2)}, u32[]{:S(2)}) collective-permute-start(bf16[96,768]{1,0:T(8,128)(2,1)S(1)} %get-tuple-element.438), channel_id=1, source_target_pairs={{0,24},{4,28},{8,16},{12,20},{16,8},{20,12},{24,0},{28,4},{1,25},{... | collective-permute-start | bytes 442376 | tf_op jit(solution)/shard_map/ppermute | solution.py:729
  290.5 18.3 %collective-permute-start.46 = (bf16[96,768]{1,0:T(8,128)(2,1)S(1)}, bf16[96,768]{1,0:T(8,128)(2,1)S(1)}, u32[]{:S(2)}, u32[]{:S(2)}) collective-permute-start(bf16[96,768]{1,0:T(8,128)(2,1)S(1)} %add_convert_fusion.12), channel_id=1, source_target_pairs={{0,16},{4,20},{8,24},{12,28},{16,0},{20,4},{24,8},{28,12},{1,17},{... | collective-permute-start | bytes 442376 | tf_op jit(solution)/shard_map/ppermute | solution.py:729
  309.3 26.9 %collective-permute-start.59 = (bf16[768,768]{1,0:T(8,128)(2,1)S(1)}, bf16[768,768]{1,0:T(8,128)(2,1)}, u32[]{:S(2)}, u32[]{:S(2)}) collective-permute-start(bf16[768,768]{1,0:T(8,128)(2,1)S(1)} %maximum_select_fusion), channel_id=1, source_target_pairs={{0,4},{4,0},{8,12},{12,8},{16,20},{20,16},{24,28},{28,24},{1,5},{5... | collective-permute-start | bytes 3538952 | tf_op jit(solution)/shard_map/ppermute | solution.py:729
  311.0 18.4 %collective-permute-start.52 = (bf16[192,768]{1,0:T(8,128)(2,1)S(1)}, bf16[192,768]{1,0:T(8,128)(2,1)S(1)}, u32[]{:S(2)}, u32[]{:S(2)}) collective-permute-start(bf16[192,768]{1,0:T(8,128)(2,1)S(1)} %maximum_select_fusion.8), channel_id=1, source_target_pairs={{0,8},{4,12},{8,0},{12,4},{16,24},{20,28},{24,16},{28,20},{1,9},{5... | collective-permute-start | bytes 884744 | tf_op jit(solution)/shard_map/ppermute | solution.py:729
  329.8 18.5 %collective-permute-start.58 = (bf16[384,768]{1,0:T(8,128)(2,1)S(1)}, bf16[384,768]{1,0:T(8,128)(2,1)}, u32[]{:S(2)}, u32[]{:S(2)}) collective-permute-start(bf16[384,768]{1,0:T(8,128)(2,1)S(1)} %maximum_select_fusion.7), channel_id=1, source_target_pairs={{0,4},{4,0},{8,12},{12,8},{16,20},{20,16},{24,28},{28,24},{1,5},{5... | collective-permute-start | bytes 1769480 | tf_op jit(solution)/shard_map/ppermute | solution.py:729
  330.3 26.5 %collective-permute-start.57 = (bf16[384,768]{1,0:T(8,128)(2,1)S(1)}, bf16[384,768]{1,0:T(8,128)(2,1)}, u32[]{:S(2)}, u32[]{:S(2)}) collective-permute-start(bf16[384,768]{1,0:T(8,128)(2,1)S(1)} %maximum_select_fusion.6), channel_id=1, source_target_pairs={{0,4},{4,0},{8,12},{12,8},{16,20},{20,16},{24,28},{28,24},{1,5},{5... | collective-permute-start | bytes 1769480 | tf_op jit(solution)/shard_map/ppermute | solution.py:729
  (110 other events, 1088.2 us)

commit v6 on v4

--- a/solution.py
+++ b/solution.py
@@ -13,7 +13,7 @@
 LEN = 256
 ENC = 1024
 DH = 64
-KEYS = 256
+KEYS = 128
 
 norm_eps = 1e-06
 masked_score = -1000000000.0

time: 365 us -> 365 us (level)
  no operation moved by 1% of the time
where the time goes in v6:
time: 365 us; the launch traced here: 360 us
  Pallas kernels  127 us (35%)
  waiting for transfers between devices  96.9 us (27%)
  starting transfers between devices  63.1 us (17%)
  other arithmetic  43.2 us (12%)
  local copies, waits for them, and re-layouts  25.7 us (7%)
    pallas_call x11, Pallas kernels, call(): pl.pallas_call(kernel, out_shape=out_shape, grid=grid, scratch_shapes=scr...  127 us
    ppermute x61, waiting for transfers between devices, swap(): return lax.ppermute(v, axis, [(i, i ^ bit) for i in range(n)])  96.9 us
    ppermute x61, starting transfers between devices, swap(): return lax.ppermute(v, axis, [(i, i ^ bit) for i in range(n)])  63.1 us
    convert_element_type x17, other arithmetic, plus(): return total.astype(bf16)  22.2 us
    unnamed x164, local copies, waits for them, and re-layouts  20.7 us
  transfers between devices with their start and end apart: 61, of which 25 were waited for; matrix products, arithmetic and copies ran while one was open for 11% of the time, Pallas kernels for 35%

profile of v6, /device:TPU:0, one launch (start us, length us, event | category | flops | bytes accessed | tf_op | source)
XLA Modules:
  0.0 359.9 jit_solution(12414024154739818062)
XLA Ops:
  2.9 2.9 collective-permute-start.3
  11.9 5.2 %self_fwd.2 = (bf16[512,384]{1,0:T(8,128)(2,1)S(1)}, bf16[512,384]{1,0:T(8,128)(2,1)S(1)}, bf16[384,512]{1,0:T(8,128)(2,1)S(1)}, bf16[2,6,256,256]{3,2,1,0:T(8,1...) custom-call(s32[2]{0:T(128)S(1)} %pad_add_fusion.r_0_.r__0_.y_ref, ...), custom_call_target="tpu_custom_call" | custom-call | flops 1 | bytes 1 | tf_op jit(solution)/shard_map/self_fwd/pallas_call | solution.py:83
  19.4 4.8 %enc_kv.2 = (bf16[2048,384]{1,0:T(8,128)(2,1)S(1)}, bf16[2048,384]{1,0:T(8,128)(2,1)S(1)}) custom-call(s32[2]{0:T(128)S(1)} %pad_add_fusion.r_0_.r__0_.y_ref, bf16[2048,768]{1,0:T(8,128)(2,1)S(1)} %copy-done.3, bf16[768,768]{1,0:T(8,128)(2,1)S(1)} %pad_maximum_fusion.r_2_.r_4_.r__4_.rest_0_, bf16[768,768]{1,0:T(8,128)(2,1)S(1)} %collective-permute-done.2.r_3_.r_5_.r__5_.rest_1_), custom_call_target="tpu_custom_call" | custom-call | flops 1 | bytes 1 | tf_op jit(solution)/shard_map/enc_kv/pallas_call | solution.py:83
  26.6 5.7 %collective-permute-done.4 = f32[3,256]{1,0:T(4,128)} collective-permute-done((f32[3,256]{1,0:T(4,128)}, f32[3,256]{1,0:T(4,128)}, u32[]{:S(2)}, u32[]{:S(2)}) %collective-permute-start.4) | collective-permute-done | bytes 3104 | tf_op jit(solution)/shard_map/ppermute | solution.py:729
  37.9 5.9 %self_fwd.3 = (bf16[512,384]{1,0:T(8,128)(2,1)S(1)}, bf16[512,384]{1,0:T(8,128)(2,1)S(1)}, bf16[384,512]{1,0:T(8,128)(2,1)S(1)}, bf16[2,6,256,256]{3,2,1,0:T(8,1...) custom-call(s32[2]{0:T(128)S(1)} %pad_add_fusion.r_0_.r__0_.y_ref, ...), custom_call_target="tpu_custom_call" | custom-call | flops 1 | bytes 1 | tf_op jit(solution)/shard_map/self_fwd/pallas_call | solution.py:83
  52.8 8.9 %cross_fwd.2 = (bf16[512,384]{1,0:T(8,128)(2,1)S(1)}, f32[6,4,256]{2,1,0:T(4,128)S(1)}, bf16[384,512]{1,0:T(8,128)(2,1)S(1)}, f32[512,768]{1,0:T(8,128)S(1)}) custom-call(s32[2]{0:T(128)S(1)} %pad_add_fusion.r_0_.r__0_.y_ref, s32[8]{0:T(128)S(1)} %copy-done.51, bf16[512,768]{1,0:T(8,128)(2,1)S(1)} %get-tuple-element.246.r_2_.r__3_, ...), custom_call_target="tpu_custom_call" | custom-call | flops 1 | bytes 1 | tf_op jit(solution)/shard_map/cross_fwd/pallas_call | solution.py:83
  66.5 4.6 %enc_kv.3 = (bf16[2048,384]{1,0:T(8,128)(2,1)S(1)}, bf16[2048,384]{1,0:T(8,128)(2,1)S(1)}) custom-call(s32[2]{0:T(128)S(1)} %pad_add_fusion.r_0_.r__0_.y_ref, bf16[2048,768]{1,0:T(8,128)(2,1)S(1)} %copy-done.4, bf16[384,768]{1,0:T(8,128)(2,1)S(1)} %collective-permute-done.7.r_2_.r_4_.r__6_.rest_2_, ...), custom_call_target="tpu_custom_call" | custom-call | flops 1 | bytes 1 | tf_op jit(solution)/shard_map/enc_kv/pallas_call | solution.py:83
  71.2 8.5 %collective-permute-done.11.r_3_.r_4_ = bf16[768,768]{1,0:T(8,128)(2,1)S(1)} collective-permute-done((bf16[768,768]{1,0:T(8,128)(2,1)S(1)}, bf16[768,768]{1,0:T(8,128)(2,1)S(1)}, u32[]{:S(2)}, u32[]{:S(2)}) %collective-permute-start.11) | collective-permute-done | bytes 1179680 | tf_op jit(solution)/shard_map/ppermute | solution.py:729
  79.9 9.1 %cross_fwd.3 = (bf16[512,384]{1,0:T(8,128)(2,1)S(1)}, f32[6,4,256]{2,1,0:T(4,128)S(1)}, bf16[384,512]{1,0:T(8,128)(2,1)S(1)}, f32[512,768]{1,0:T(8,128)S(1)}, bf16[512,768]{1,0:T(8,128)(2,1)S(1)}) custom-call(s32[2]{0:T(128)S(1)} %pad_add_fusion.r_0_.r__0_.y_ref, s32[8]{0:T(128)S(1)} %copy-done.51, bf16[512,768]{1,0:T(8,128)(2,1)S(1)} %get-tuple-element.246.r_2_.r__3_, ...), custom_call_target="tpu_custom_call" | custom-call | flops 1 | bytes 1 | tf_op jit(solution)/shard_map/cross_fwd/pallas_call | solution.py:83
  91.2 10.9 %ff.2 = (bf16[768,768]{1,0:T(8,128)(2,1)S(1)}, bf16[768,768]{1,0:T(8,128)(2,1)S(1)}, bf16[768,768]{1,0:T(8,128)(2,1)S(1)}, bf16[768,768]{1,0:T(8,128)(2,1)S(1)},...) custom-call(s32[2]{0:T(128)S(1)} %pad_add_fusion.r_0_.r__0_.y_ref, bf16[512,768]{1,0:T(8,128)(2,1)S(1)} %get-tuple-element.263.r_1_, ...), custom_call_target="tpu_custom_call" | custom-call | flops 1 | bytes 1 | tf_op jit(solution)/shard_map/ff/pallas_call | solution.py:83
  102.1 5.9 %collective-permute-done.15.r_5_.r_6_ = bf16[768,768]{1,0:T(8,128)(2,1)S(1)} collective-permute-done((bf16[768,768]{1,0:T(8,128)(2,1)S(1)}, bf16[768,768]{1,0:T(8,128)(2,1)S(1)}, u32[]{:S(2)}, u32[]{:S(2)}) %collective-permute-start.15) | collective-permute-done | bytes 1179680 | tf_op jit(solution)/shard_map/ppermute | solution.py:729
  110.9 12.4 %ff.3 = (bf16[768,768]{1,0:T(8,128)(2,1)S(1)}, bf16[768,768]{1,0:T(8,128)(2,1)S(1)}, bf16[768,768]{1,0:T(8,128)(2,1)}, bf16[768,768]{1,0:T(8,128)(2,1)}, bf16[51...) custom-call(s32[2]{0:T(128)S(1)} %pad_add_fusion.r_0_.r__0_.y_ref, ...), custom_call_target="tpu_custom_call" | custom-call | flops 1 | bytes 1 | tf_op jit(solution)/shard_map/ff/pallas_call | solution.py:83
  138.5 29.1 %cross_bwd.1 = (bf16[2048,384]{1,0:T(8,128)(2,1)}, bf16[2048,384]{1,0:T(8,128)(2,1)}, bf16[2048,384]{1,0:T(8,128)(2,1)}, bf16[2048,384]{1,0:T(8,128)(2,1)}, bf16...) custom-call(s32[2]{0:T(128)} %copy-done.46, ...), custom_call_target="tpu_custom_call" | custom-call | flops 1 | bytes 1 | tf_op jit(solution)/shard_map/cross_bwd/pallas_call | solution.py:83
  176.4 18.1 %enc_grad.1 = (f32[2048,768]{1,0:T(8,128)}, bf16[384,768]{1,0:T(8,128)(2,1)}, bf16[384,768]{1,0:T(8,128)(2,1)}, bf16[384,768]{1,0:T(8,128)(2,1)}, bf16[384,768]{1,0:T(8,128)(2,1)}) custom-call(s32[2]{0:T(128)} %copy-done.46, bf16[2048,768]{1,0:T(8,128)(2,1)} %enc_ref.1, bf16[2048,384]{1,0:T(8,128)(2,1)} %get-tuple-element.312.gk1_ref, ...), custom_call_target="tpu_custom_call" | custom-call | flops 1 | bytes 1 | tf_op jit(solution)/shard_map/enc_grad/pallas_call | solution.py:83
  204.2 2.6 collective-permute-start.32
  207.0 18.2 %self_bwd.1 = (bf16[768,768]{1,0:T(8,128)(2,1)}, bf16[768,768]{1,0:T(8,128)(2,1)}, bf16[768,768]{1,0:T(8,128)(2,1)}, bf16[768,768]{1,0:T(8,128)(2,1)}, f32[12,25...) custom-call(bf16[512,768]{1,0:T(8,128)(2,1)} %x_ref.1, f32[512,768]{1,0:T(8,128)} %copy-done.14, ...), custom_call_target="tpu_custom_call" | custom-call | flops 1 | bytes 1 | tf_op jit(solution)/shard_map/self_bwd/pallas_call | solution.py:83
  235.6 6.5 %collective-permute-start.39 = (bf16[192,768]{1,0:T(8,128)(2,1)}, bf16[192,768]{1,0:T(8,128)(2,1)}, u32[]{:S(2)}, u32[]{:S(2)}) collective-permute-start(bf16[192,768]{1,0:T(8,128)(2,1)} %add_convert_fusion.10), channel_id=1, source_target_pairs={{0,16},{4,20},{8,24},{12,28},{16,0},{20,4},{24,8},{28,12},{1,17},{... | collective-permute-start | bytes 884744 | tf_op jit(solution)/shard_map/ppermute | solution.py:729
  246.5 9.3 %collective-permute-done.39 = bf16[192,768]{1,0:T(8,128)(2,1)} collective-permute-done((bf16[192,768]{1,0:T(8,128)(2,1)}, bf16[192,768]{1,0:T(8,128)(2,1)}, u32[]{:S(2)}, u32[]{:S(2)}) %collective-permute-start.39) | collective-permute-done | bytes 294944 | tf_op jit(solution)/shard_map/ppermute | solution.py:729
  255.8 5.0 %collective-permute-done.38 = bf16[768,768]{1,0:T(8,128)(2,1)} collective-permute-done((bf16[768,768]{1,0:T(8,128)(2,1)}, bf16[768,768]{1,0:T(8,128)(2,1)}, u32[]{:S(2)}, u32[]{:S(2)}) %collective-permute-start.38) | collective-permute-done | bytes 1179680 | tf_op jit(solution)/shard_map/ppermute | solution.py:729
  264.8 5.6 %collective-permute-start.42 = (bf16[96,768]{1,0:T(8,128)(2,1)S(1)}, bf16[96,768]{1,0:T(8,128)(2,1)S(1)}, u32[]{:S(2)}, u32[]{:S(2)}) collective-permute-start(bf16[96,768]{1,0:T(8,128)(2,1)S(1)} %get-tuple-element.450), channel_id=1, source_target_pairs={{0,8},{4,12},{8,0},{12,4},{16,24},{20,28},{24,16},{28,20},{1,9},{5... | collective-permute-start | bytes 442376 | tf_op jit(solution)/shard_map/ppermute | solution.py:729
  277.6 6.3 %collective-permute-done.43 = bf16[96,768]{1,0:T(8,128)(2,1)S(1)} collective-permute-done((bf16[96,768]{1,0:T(8,128)(2,1)S(1)}, bf16[96,768]{1,0:T(8,128)(2,1)S(1)}, u32[]{:S(2)}, u32[]{:S(2)}) %collective-permute-start.43) | collective-permute-done | bytes 147488 | tf_op jit(solution)/shard_map/ppermute | solution.py:729
  291.9 6.7 %collective-permute-done.46 = bf16[384,768]{1,0:T(8,128)(2,1)S(1)} collective-permute-done((bf16[384,768]{1,0:T(8,128)(2,1)S(1)}, bf16[384,768]{1,0:T(8,128)(2,1)S(1)}, u32[]{:S(2)}, u32[]{:S(2)}) %collective-permute-start.46) | collective-permute-done | bytes 589856 | tf_op jit(solution)/shard_map/ppermute | solution.py:729
  298.6 2.5 collective-permute-done.47
  301.1 3.1 collective-permute-done.49
  308.6 2.4 collective-permute-start.53
  311.0 3.2 collective-permute-done.50
  314.2 2.5 collective-permute-start.54
  316.7 4.1 %collective-permute-done.52 = bf16[96,768]{1,0:T(8,128)(2,1)S(1)} collective-permute-done((bf16[96,768]{1,0:T(8,128)(2,1)S(1)}, bf16[96,768]{1,0:T(8,128)(2,1)S(1)}, u32[]{:S(2)}, u32[]{:S(2)}) %collective-permute-start.52) | collective-permute-done | bytes 147488 | tf_op jit(solution)/shard_map/ppermute | solution.py:729
  322.4 9.2 %collective-permute-done.55 = bf16[96,768]{1,0:T(8,128)(2,1)S(1)} collective-permute-done((bf16[96,768]{1,0:T(8,128)(2,1)S(1)}, bf16[96,768]{1,0:T(8,128)(2,1)S(1)}, u32[]{:S(2)}, u32[]{:S(2)}) %collective-permute-start.55) | collective-permute-done | bytes 147488 | tf_op jit(solution)/shard_map/ppermute | solution.py:729
  339.8 2.7 fusion
  342.4 5.9 %collective-permute-done.59 = bf16[384,768]{1,0:T(8,128)(2,1)} collective-permute-done((bf16[384,768]{1,0:T(8,128)(2,1)S(1)}, bf16[384,768]{1,0:T(8,128)(2,1)}, u32[]{:S(2)}, u32[]{:S(2)}) %collective-permute-start.59) | collective-permute-done | bytes 589856 | tf_op jit(solution)/shard_map/ppermute | solution.py:729
  351.4 4.9 %collective-permute-done.58 = bf16[384,768]{1,0:T(8,128)(2,1)} collective-permute-done((bf16[384,768]{1,0:T(8,128)(2,1)S(1)}, bf16[384,768]{1,0:T(8,128)(2,1)}, u32[]{:S(2)}, u32[]{:S(2)}) %collective-permute-start.58) | collective-permute-done | bytes 589856 | tf_op jit(solution)/shard_map/ppermute | solution.py:729
  (327 shorter events, 125.1 us)
Async XLA Ops:
  2.8 16.6 %collective-permute-start.2 = (bf16[768,768]{1,0:T(8,128)(2,1)S(1)}, bf16[768,768]{1,0:T(8,128)(2,1)S(1)}, u32[]{:S(2)}, u32[]{:S(2)}) collective-permute-start(bf16[768,768]{1,0:T(8,128)(2,1)S(1)} %pad_maximum_fusion.r_2_.r_4_.r__4_.rest_0_), channel_id=1, source_target_pairs={{0,1},{1,0},{2,3},{3,2},{4,5},{5,4},{6,7},{7,6},{8,9},{9,8},{10,11... | collective-permute-start | bytes 3538952 | tf_op jit(solution)/shard_map/ppermute | solution.py:729
  2.9 29.3 %collective-permute-start.3 = (bf16[768,768]{1,0:T(8,128)(2,1)S(1)}, bf16[768,768]{1,0:T(8,128)(2,1)}, u32[]{:S(2)}, u32[]{:S(2)}) collective-permute-start(bf16[768,768]{1,0:T(8,128)(2,1)S(1)} %pad_maximum_fusion.1.r_4_.rest_0_), channel_id=1, source_target_pairs={{0,2},{1,3},{2,0},{3,1},{4,6},{5,7},{6,4},{7,5},{8,10},{9,11},{10,... | collective-permute-start | bytes 3538952 | tf_op jit(solution)/shard_map/ppermute | solution.py:729
  6.6 25.7 %collective-permute-start.4 = (f32[3,256]{1,0:T(4,128)}, f32[3,256]{1,0:T(4,128)}, u32[]{:S(2)}, u32[]{:S(2)}) collective-permute-start(f32[3,256]{1,0:T(4,128)} %convolution_bitcast_fusion), channel_id=1, source_target_pairs={{0,2},{1,3},{2,0},{3,1},{4,6},{5,7},{6,4},{7,5},{8,10},{9,11},{10,... | collective-permute-start | bytes 9224 | tf_op jit(solution)/shard_map/ppermute | solution.py:729
  33.7 15.8 %collective-permute-start.7 = (bf16[384,768]{1,0:T(8,128)(2,1)S(1)}, bf16[384,768]{1,0:T(8,128)(2,1)S(1)}, u32[]{:S(2)}, u32[]{:S(2)}) collective-permute-start(bf16[384,768]{1,0:T(8,128)(2,1)S(1)} %maximum_select_fusion.4), channel_id=1, source_target_pairs={{0,2},{1,3},{2,0},{3,1},{4,6},{5,7},{6,4},{7,5},{8,10},{9,11},{10,... | collective-permute-start | bytes 1769480 | tf_op jit(solution)/shard_map/ppermute | solution.py:729
  49.5 15.0 %collective-permute-start.8 = (bf16[384,768]{1,0:T(8,128)(2,1)S(1)}, bf16[384,768]{1,0:T(8,128)(2,1)S(1)}, u32[]{:S(2)}, u32[]{:S(2)}) collective-permute-start(bf16[384,768]{1,0:T(8,128)(2,1)S(1)} %collective-permute-done.7.r_2_.r_4_.r__6_.rest_2_), channel_id=1, source_target_pairs={{0,4},{4,0},{8,12},{12,8},{16,20},{20,16},{24,28},{28,24},{1,5},{5... | collective-permute-start | bytes 1769480 | tf_op jit(solution)/shard_map/ppermute | solution.py:729
  51.3 28.4 %collective-permute-start.11 = (bf16[768,768]{1,0:T(8,128)(2,1)S(1)}, bf16[768,768]{1,0:T(8,128)(2,1)S(1)}, u32[]{:S(2)}, u32[]{:S(2)}) collective-permute-start(bf16[768,768]{1,0:T(8,128)(2,1)S(1)} %broadcast_select_fusion), channel_id=1, source_target_pairs={{0,2},{1,3},{2,0},{3,1},{4,6},{5,7},{6,4},{7,5},{8,10},{9,11},{10,... | collective-permute-start | bytes 3538952 | tf_op jit(solution)/shard_map/ppermute | solution.py:729
  64.6 26.6 %collective-permute-start.12 = (bf16[768,768]{1,0:T(8,128)(2,1)S(1)}, bf16[768,768]{1,0:T(8,128)(2,1)S(1)}, u32[]{:S(2)}, u32[]{:S(2)}) collective-permute-start(bf16[768,768]{1,0:T(8,128)(2,1)S(1)} %copy-done.21), channel_id=1, source_target_pairs={{0,1},{1,0},{2,3},{3,2},{4,5},{5,4},{6,7},{7,6},{8,9},{9,8},{10,11... | collective-permute-start | bytes 3538952 | tf_op jit(solution)/shard_map/ppermute | solution.py:729
  65.1 26.1 %collective-permute-start.13 = (bf16[768,768]{1,0:T(8,128)(2,1)S(1)}, bf16[768,768]{1,0:T(8,128)(2,1)S(1)}, u32[]{:S(2)}, u32[]{:S(2)}) collective-permute-start(bf16[768,768]{1,0:T(8,128)(2,1)S(1)} %copy-done.22), channel_id=1, source_target_pairs={{0,1},{1,0},{2,3},{3,2},{4,5},{5,4},{6,7},{7,6},{8,9},{9,8},{10,11... | collective-permute-start | bytes 3538952 | tf_op jit(solution)/shard_map/ppermute | solution.py:729
  79.6 28.4 %collective-permute-start.15 = (bf16[768,768]{1,0:T(8,128)(2,1)S(1)}, bf16[768,768]{1,0:T(8,128)(2,1)S(1)}, u32[]{:S(2)}, u32[]{:S(2)}) collective-permute-start(bf16[768,768]{1,0:T(8,128)(2,1)S(1)} %collective-permute-done.11.r_3_.r_4_), channel_id=1, source_target_pairs={{0,4},{4,0},{8,12},{12,8},{16,20},{20,16},{24,28},{28,24},{1,5},{5... | collective-permute-start | bytes 3538952 | tf_op jit(solution)/shard_map/ppermute | solution.py:729
  108.0 17.4 %collective-permute-start.17 = (bf16[768,768]{1,0:T(8,128)(2,1)S(1)}, bf16[768,768]{1,0:T(8,128)(2,1)S(1)}, u32[]{:S(2)}, u32[]{:S(2)}) collective-permute-start(bf16[768,768]{1,0:T(8,128)(2,1)S(1)} %get-tuple-element.280), channel_id=1, source_target_pairs={{0,1},{1,0},{2,3},{3,2},{4,5},{5,4},{6,7},{7,6},{8,9},{9,8},{10,11... | collective-permute-start | bytes 3538952 | tf_op jit(solution)/shard_map/ppermute | solution.py:729
  108.5 16.9 %collective-permute-start.18 = (bf16[768,768]{1,0:T(8,128)(2,1)S(1)}, bf16[768,768]{1,0:T(8,128)(2,1)S(1)}, u32[]{:S(2)}, u32[]{:S(2)}) collective-permute-start(bf16[768,768]{1,0:T(8,128)(2,1)S(1)} %get-tuple-element.281), channel_id=1, source_target_pairs={{0,1},{1,0},{2,3},{3,2},{4,5},{5,4},{6,7},{7,6},{8,9},{9,8},{10,11... | collective-permute-start | bytes 3538952 | tf_op jit(solution)/shard_map/ppermute | solution.py:729
  136.4 31.2 %collective-permute-start.21 = (bf16[768,768]{1,0:T(8,128)(2,1)S(1)}, bf16[768,768]{1,0:T(8,128)(2,1)S(1)}, u32[]{:S(2)}, u32[]{:S(2)}) collective-permute-start(bf16[768,768]{1,0:T(8,128)(2,1)S(1)} %add_convert_fusion.1), channel_id=1, source_target_pairs={{0,2},{1,3},{2,0},{3,1},{4,6},{5,7},{6,4},{7,5},{8,10},{9,11},{10,... | collective-permute-start | bytes 3538952 | tf_op jit(solution)/shard_map/ppermute | solution.py:729
  137.9 30.7 %collective-permute-start.22 = (bf16[768,768]{1,0:T(8,128)(2,1)}, bf16[768,768]{1,0:T(8,128)(2,1)}, u32[]{:S(2)}, u32[]{:S(2)}) collective-permute-start(bf16[768,768]{1,0:T(8,128)(2,1)} %pad_maximum_fusion.2), channel_id=1, source_target_pairs={{0,4},{4,0},{8,12},{12,8},{16,20},{20,16},{24,28},{28,24},{1,5},{5... | collective-permute-start | bytes 3538952 | tf_op jit(solution)/shard_map/ppermute | solution.py:729
  172.3 24.3 %collective-permute-start.24 = (bf16[384,768]{1,0:T(8,128)(2,1)S(1)}, bf16[384,768]{1,0:T(8,128)(2,1)}, u32[]{:S(2)}, u32[]{:S(2)}) collective-permute-start(bf16[384,768]{1,0:T(8,128)(2,1)S(1)} %fusion.6), channel_id=1, source_target_pairs={{0,2},{1,3},{2,0},{3,1},{4,6},{5,7},{6,4},{7,5},{8,10},{9,11},{10,... | collective-permute-start | bytes 1769480 | tf_op jit(solution)/shard_map/ppermute | solution.py:729
  172.6 24.0 %collective-permute-start.25 = (bf16[384,768]{1,0:T(8,128)(2,1)}, bf16[384,768]{1,0:T(8,128)(2,1)}, u32[]{:S(2)}, u32[]{:S(2)}) collective-permute-start(bf16[384,768]{1,0:T(8,128)(2,1)} %fusion.9), channel_id=1, source_target_pairs={{0,4},{4,0},{8,12},{12,8},{16,20},{20,16},{24,28},{28,24},{1,5},{5... | collective-permute-start | bytes 1769480 | tf_op jit(solution)/shard_map/ppermute | solution.py:729
  174.4 32.4 %collective-permute-start.30 = (bf16[384,768]{1,0:T(8,128)(2,1)}, bf16[384,768]{1,0:T(8,128)(2,1)S(1)}, u32[]{:S(2)}, u32[]{:S(2)}) collective-permute-start(bf16[384,768]{1,0:T(8,128)(2,1)} %get-tuple-element.360), channel_id=1, source_target_pairs={{0,1},{1,0},{2,3},{3,2},{4,5},{5,4},{6,7},{7,6},{8,9},{9,8},{10,11... | collective-permute-start | bytes 1769480 | tf_op jit(solution)/shard_map/ppermute | solution.py:729
  195.1 30.2 %collective-permute-start.28 = (bf16[384,768]{1,0:T(8,128)(2,1)}, bf16[384,768]{1,0:T(8,128)(2,1)S(1)}, u32[]{:S(2)}, u32[]{:S(2)}) collective-permute-start(bf16[384,768]{1,0:T(8,128)(2,1)} %add_convert_fusion.6), channel_id=1, source_target_pairs={{0,2},{1,3},{2,0},{3,1},{4,6},{5,7},{6,4},{7,5},{8,10},{9,11},{10,... | collective-permute-start | bytes 1769480 | tf_op jit(solution)/shard_map/ppermute | solution.py:729
  202.0 25.7 %collective-permute-start.29 = (bf16[384,768]{1,0:T(8,128)(2,1)}, bf16[384,768]{1,0:T(8,128)(2,1)S(1)}, u32[]{:S(2)}, u32[]{:S(2)}) collective-permute-start(bf16[384,768]{1,0:T(8,128)(2,1)} %add_convert_fusion.5), channel_id=1, source_target_pairs={{0,2},{1,3},{2,0},{3,1},{4,6},{5,7},{6,4},{7,5},{8,10},{9,11},{10,... | collective-permute-start | bytes 1769480 | tf_op jit(solution)/shard_map/ppermute | solution.py:729
  202.6 22.7 %collective-permute-start.31 = (bf16[192,768]{1,0:T(8,128)(2,1)S(1)}, bf16[192,768]{1,0:T(8,128)(2,1)S(1)}, u32[]{:S(2)}, u32[]{:S(2)}) collective-permute-start(bf16[192,768]{1,0:T(8,128)(2,1)S(1)} %get-tuple-element.438), channel_id=1, source_target_pairs={{0,8},{4,12},{8,0},{12,4},{16,24},{20,28},{24,16},{28,20},{1,9},{5... | collective-permute-start | bytes 884744 | tf_op jit(solution)/shard_map/ppermute | solution.py:729
  204.2 23.5 %collective-permute-start.32 = (bf16[192,768]{1,0:T(8,128)(2,1)S(1)}, bf16[192,768]{1,0:T(8,128)(2,1)S(1)}, u32[]{:S(2)}, u32[]{:S(2)}) collective-permute-start(bf16[192,768]{1,0:T(8,128)(2,1)S(1)} %get-tuple-element.437), channel_id=1, source_target_pairs={{0,16},{4,20},{8,24},{12,28},{16,0},{20,4},{24,8},{28,12},{1,17},{... | collective-permute-start | bytes 884744 | tf_op jit(solution)/shard_map/ppermute | solution.py:729
  206.8 20.9 %collective-permute-start.33 = (bf16[192,768]{1,0:T(8,128)(2,1)S(1)}, bf16[192,768]{1,0:T(8,128)(2,1)S(1)}, u32[]{:S(2)}, u32[]{:S(2)}) collective-permute-start(bf16[192,768]{1,0:T(8,128)(2,1)S(1)} %get-tuple-element.436), channel_id=1, source_target_pairs={{0,24},{4,28},{8,16},{12,20},{16,8},{20,12},{24,0},{28,4},{1,25},{... | collective-permute-start | bytes 884744 | tf_op jit(solution)/shard_map/ppermute | solution.py:729
  232.1 23.7 %collective-permute-start.37 = (bf16[768,768]{1,0:T(8,128)(2,1)}, bf16[768,768]{1,0:T(8,128)(2,1)}, u32[]{:S(2)}, u32[]{:S(2)}) collective-permute-start(bf16[768,768]{1,0:T(8,128)(2,1)} %get-tuple-element.384), channel_id=1, source_target_pairs={{0,1},{1,0},{2,3},{3,2},{4,5},{5,4},{6,7},{7,6},{8,9},{9,8},{10,11... | collective-permute-start | bytes 3538952 | tf_op jit(solution)/shard_map/ppermute | solution.py:729
  232.3 28.6 %collective-permute-start.38 = (bf16[768,768]{1,0:T(8,128)(2,1)}, bf16[768,768]{1,0:T(8,128)(2,1)}, u32[]{:S(2)}, u32[]{:S(2)}) collective-permute-start(bf16[768,768]{1,0:T(8,128)(2,1)} %add_convert_fusion), channel_id=1, source_target_pairs={{0,2},{1,3},{2,0},{3,1},{4,6},{5,7},{6,4},{7,5},{8,10},{9,11},{10,... | collective-permute-start | bytes 3538952 | tf_op jit(solution)/shard_map/ppermute | solution.py:729
  233.8 22.0 %collective-permute-start.35 = (bf16[384,768]{1,0:T(8,128)(2,1)}, bf16[384,768]{1,0:T(8,128)(2,1)}, u32[]{:S(2)}, u32[]{:S(2)}) collective-permute-start(bf16[384,768]{1,0:T(8,128)(2,1)} %add_convert_fusion.4), channel_id=1, source_target_pairs={{0,4},{4,0},{8,12},{12,8},{16,20},{20,16},{24,28},{28,24},{1,5},{5... | collective-permute-start | bytes 1769480 | tf_op jit(solution)/shard_map/ppermute | solution.py:729
  235.6 20.1 %collective-permute-start.39 = (bf16[192,768]{1,0:T(8,128)(2,1)}, bf16[192,768]{1,0:T(8,128)(2,1)}, u32[]{:S(2)}, u32[]{:S(2)}) collective-permute-start(bf16[192,768]{1,0:T(8,128)(2,1)} %add_convert_fusion.10), channel_id=1, source_target_pairs={{0,16},{4,20},{8,24},{12,28},{16,0},{20,4},{24,8},{28,12},{1,17},{... | collective-permute-start | bytes 884744 | tf_op jit(solution)/shard_map/ppermute | solution.py:729
  262.5 21.5 %collective-permute-start.40 = (bf16[384,768]{1,0:T(8,128)(2,1)S(1)}, bf16[384,768]{1,0:T(8,128)(2,1)S(1)}, u32[]{:S(2)}, u32[]{:S(2)}) collective-permute-start(bf16[384,768]{1,0:T(8,128)(2,1)S(1)} %fusion.10), channel_id=1, source_target_pairs={{0,4},{4,0},{8,12},{12,8},{16,20},{20,16},{24,28},{28,24},{1,5},{5... | collective-permute-start | bytes 1769480 | tf_op jit(solution)/shard_map/ppermute | solution.py:729
  276.6 22.0 %collective-permute-start.46 = (bf16[384,768]{1,0:T(8,128)(2,1)S(1)}, bf16[384,768]{1,0:T(8,128)(2,1)S(1)}, u32[]{:S(2)}, u32[]{:S(2)}) collective-permute-start(bf16[384,768]{1,0:T(8,128)(2,1)S(1)} %maximum_select_fusion.5), channel_id=1, source_target_pairs={{0,8},{4,12},{8,0},{12,4},{16,24},{20,28},{24,16},{28,20},{1,9},{5... | collective-permute-start | bytes 1769480 | tf_op jit(solution)/shard_map/ppermute | solution.py:729
  285.6 15.5 %collective-permute-start.47 = (bf16[96,768]{1,0:T(8,128)(2,1)S(1)}, bf16[96,768]{1,0:T(8,128)(2,1)S(1)}, u32[]{:S(2)}, u32[]{:S(2)}) collective-permute-start(bf16[96,768]{1,0:T(8,128)(2,1)S(1)} %get-tuple-element.446), channel_id=1, source_target_pairs={{0,8},{4,12},{8,0},{12,4},{16,24},{20,28},{24,16},{28,20},{1,9},{5... | collective-permute-start | bytes 442376 | tf_op jit(solution)/shard_map/ppermute | solution.py:729
  288.8 15.4 %collective-permute-start.49 = (bf16[96,768]{1,0:T(8,128)(2,1)S(1)}, bf16[96,768]{1,0:T(8,128)(2,1)S(1)}, u32[]{:S(2)}, u32[]{:S(2)}) collective-permute-start(bf16[96,768]{1,0:T(8,128)(2,1)S(1)} %get-tuple-element.444), channel_id=1, source_target_pairs={{0,24},{4,28},{8,16},{12,20},{16,8},{20,12},{24,0},{28,4},{1,25},{... | collective-permute-start | bytes 442376 | tf_op jit(solution)/shard_map/ppermute | solution.py:729
  304.7 33.8 %collective-permute-start.60 = (bf16[768,768]{1,0:T(8,128)(2,1)S(1)}, bf16[768,768]{1,0:T(8,128)(2,1)}, u32[]{:S(2)}, u32[]{:S(2)}) collective-permute-start(bf16[768,768]{1,0:T(8,128)(2,1)S(1)} %maximum_select_fusion), channel_id=1, source_target_pairs={{0,4},{4,0},{8,12},{12,8},{16,20},{20,16},{24,28},{28,24},{1,5},{5... | collective-permute-start | bytes 3538952 | tf_op jit(solution)/shard_map/ppermute | solution.py:729
  331.9 16.4 %collective-permute-start.59 = (bf16[384,768]{1,0:T(8,128)(2,1)S(1)}, bf16[384,768]{1,0:T(8,128)(2,1)}, u32[]{:S(2)}, u32[]{:S(2)}) collective-permute-start(bf16[384,768]{1,0:T(8,128)(2,1)S(1)} %maximum_select_fusion.7), channel_id=1, source_target_pairs={{0,4},{4,0},{8,12},{12,8},{16,20},{20,16},{24,28},{28,24},{1,5},{5... | collective-permute-start | bytes 1769480 | tf_op jit(solution)/shard_map/ppermute | solution.py:729
  334.9 21.4 %collective-permute-start.58 = (bf16[384,768]{1,0:T(8,128)(2,1)S(1)}, bf16[384,768]{1,0:T(8,128)(2,1)}, u32[]{:S(2)}, u32[]{:S(2)}) collective-permute-start(bf16[384,768]{1,0:T(8,128)(2,1)S(1)} %maximum_select_fusion.6), channel_id=1, source_target_pairs={{0,4},{4,0},{8,12},{12,8},{16,20},{20,16},{24,28},{28,24},{1,5},{5... | collective-permute-start | bytes 1769480 | tf_op jit(solution)/shard_map/ppermute | solution.py:729
  (111 other events, 1092.5 us)
